TPU v7x, 128 devices: a whole 4x4x4 slice. The times are simulated.
128 devices in a mesh: dom: 128 (over z, y, x, core).
Axes of the slice: x: 4, y: 4, z: 4, core: 2. Of those that a mesh axis runs over, the one named last changes fastest.
Arguments:
- right_side: float32 [64, 16384], P(None, 'dom'), may hold values from -8 to 8
- sigma: float32 [64, 16384], P(None, 'dom'), may hold values from 0.5 to 2
- reluctivity: float32 [64, 16384], P(None, 'dom'), may hold values from 0.2 to 5
- curl_blocks: float32 [6, 64, 64, 16384], P(None, None, None, 'dom'), may hold values from -0.3125 to 0.3125
- pattern: int32 [6, 16384], P(None, 'dom'), may hold values from 0 to 191
- cond_weight: float32 [64, 65536], P(None, 'dom'), may hold values from -0.125 to 0.125
- cond_block: int32 [65536], P('dom'), may hold values from 0 to 127
- cond_coil: int32 [65536, 1], P('dom'), may hold values from 0 to 83; in each aligned block of 512 rows (0 to 511, 512 to 1023, ...) at most 16 rows name the same one
- coil_phase: int32 [84], replicated, may hold values from 0 to 3
- coil_resistance: float32 [84], replicated, may hold values from 0.5 to 2
- switch_state: int32 [3], replicated, may hold values from 0 to 1
Outputs:
- solution_field: float32 [64, 16384], P(None, 'dom')
- residual: float32 [64, 16384], P(None, 'dom')
Inputs may be any that keep to these rules, and one draw needn't show every extreme that they name: `cond_coil`: no coil is named by more than 16 of one partition's 512 conductor rows, a bound that some block reaches.
All inputs are finite; a program needn't handle non-finite values.
Results may differ from a plain program's by a relative error of at most 0.00055.
Values sent between devices are 32-bit elements; how exact they have to be, the bound alone decides.
No kernel may reach another device: no remote copies, remote signals or barrier semaphores. Data moves between devices by JAX's collectives and lax.ppermute only.
A program may use at most 64 MiB of HBM per device.

v0:
```python
import functools

import jax
import jax.numpy as jnp
from jax import lax
from jax.experimental import pallas as pl
from jax.experimental.pallas import tpu as pltpu
from jax.sharding import PartitionSpec as P

ITERS = 3
LINK_SCALE = 16.0
LANES = 128
F32 = jnp.float32
BF16 = jnp.bfloat16
VMEM = pltpu.VMEM


def gather_lanes(x, idx):
    dims = lax.GatherDimensionNumbers(
        offset_dims=(),
        collapsed_slice_dims=(1,),
        start_index_map=(1,),
        operand_batching_dims=(0,),
        start_indices_batching_dims=(0,),
    )
    return lax.gather(
        x,
        idx[..., None],
        dims,
        slice_sizes=(1, 1),
        mode=lax.GatherScatterMode.PROMISE_IN_BOUNDS,
    )


def lane_iota(rows=1, lanes=LANES):
    return lax.broadcasted_iota(jnp.int32, (rows, lanes), 1)


def nt_dot(a, b):
    return lax.dot_general(a, b, (((1,), (1,)), ((), ())), preferred_element_type=F32)


def split_rows(x):
    high = x.astype(BF16)
    low = (x - high.astype(F32)).astype(BF16)
    return jnp.concatenate([high, low], axis=0)


def add_halves(x):
    half = x.shape[0] // 2
    return x[:half] + x[half:]


def rows_of(ids):
    return jnp.concatenate([ids[i : i + 1] for i in range(ids.shape[0])], axis=1)


def onehot(ids, count):
    slots = lax.broadcasted_iota(jnp.int32, (count, ids.shape[1]), 0)
    return jnp.where(slots == ids, 1.0, 0.0).astype(BF16)


def weighted(weight, table, coils):
    parts = []
    wide = jnp.broadcast_to(table, (8, LANES))
    for i in range(coils.shape[1] // LANES):
        tile = coils[:, i * LANES : (i + 1) * LANES]
        got = gather_lanes(wide, jnp.broadcast_to(tile, (8, LANES)))
        cut = weight[:, i * LANES : (i + 1) * LANES]
        parts.append(cut * jnp.broadcast_to(got[0:1], cut.shape))
    return jnp.concatenate(parts, axis=1)


def pad_lanes(row, scratch):
    scratch[...] = jnp.zeros_like(scratch)
    scratch[0:1, 0 : row.shape[1]] = row
    return scratch[0:1, :]


def rhs_kernel(
    side_ref, weight_ref, block_ref, coil_ref, phase_ref, ohm_ref, state_ref, rhs_ref, pad_ref
):
    s0, s1, s2 = (state_ref[i].astype(F32) for i in range(3))
    mean = (s0 + s1 + s2) / 3.0
    phase = phase_ref[...]
    volts = jnp.where(
        phase == 0,
        s0 - mean,
        jnp.where(phase == 1, s1 - mean, jnp.where(phase == 2, s2 - mean, 0.0)),
    )
    source = pad_lanes(LINK_SCALE * volts / ohm_ref[...], pad_ref)
    coils, blocks = rows_of(coil_ref[...]), rows_of(block_ref[...])
    spread = split_rows(weighted(weight_ref[...], source, coils))
    rhs_ref[...] = side_ref[...] + add_halves(nt_dot(spread, onehot(blocks, LANES)))


def table_kernel(pattern_ref, block_ref, coil_ref, ohm_ref, pat_ref, blk_ref, coil_hot_ref, inv_ref):
    for k in range(pattern_ref.shape[0]):
        q = pattern_ref[k : k + 1, :]
        slot = jnp.where(q < 32, q + 128, jnp.where(q < 160, q - 32, q))
        pat_ref[:, k * LANES : (k + 1) * LANES] = onehot(slot, 2 * LANES)
    blk_ref[...] = onehot(rows_of(block_ref[...]), LANES)
    coil_hot_ref[...] = onehot(rows_of(coil_ref[...]), LANES)
    inv_ref[...] = jnp.zeros_like(inv_ref)
    inv_ref[0:1, 0 : ohm_ref.shape[1]] = 1.0 / ohm_ref[...]


def sides(a, b):
    even = lax.rem(lax.axis_index("dom"), 2) == 0
    return jnp.where(even, b, a), jnp.where(even, a, b)


def halo_mask(count):
    me = lax.axis_index("dom")
    lane = lane_iota()
    left = jnp.where(me > 0, 1.0, 0.0)
    right = jnp.where(me < count - 1, 1.0, 0.0)
    return jnp.where(lane < 32, left, jnp.where(lane < 64, right, 0.0))


def halo_of(left, right, count):
    lane = lane_iota(*left.shape)
    moved = jnp.where(lane < 32, pltpu.roll(left, 32, 1), pltpu.roll(right, 32, 1))
    return moved * halo_mask(count)


def apply_local(refs, own, halo, previous, row_out, msg_out, centre_out, rim_out, scratch):
    (sigma_ref, reluct_ref, curl_ref, pattern_ref, weight_ref, block_ref, coil_ref,
     pat_ref, coil_hot_ref) = refs
    picked_ref, face_ref, back_ref = scratch
    width = own.shape[0]
    rows = curl_ref.shape[1]
    kinds = pattern_ref.shape[0]

    for k in range(kinds):
        q = pattern_ref[k : k + 1, :]
        inside = jnp.logical_and(q >= 32, q < 160)
        idx = jnp.where(q < 32, q, jnp.where(inside, q - 32, q - 128))
        idx = jnp.broadcast_to(idx, (width, LANES))
        inside = jnp.broadcast_to(inside, (width, LANES))
        picked_ref[k] = jnp.where(inside, gather_lanes(own, idx), gather_lanes(halo, idx))

    @pl.loop(0, rows // 8)
    def _(step):
        first = pl.multiple_of(step * 8, 8)
        total = None
        for k in range(kinds):
            for t in range(0, width, 8):
                term = curl_ref[k, pl.ds(first, 8), t : t + 8, :] * picked_ref[k, t : t + 8, :][None]
                total = term if total is None else total + term
        face_ref[pl.ds(first, 8), :] = jnp.sum(total, axis=1)

    face = face_ref[...]
    bent = reluct_ref[...] * face
    energy = jnp.sum(bent * face + sigma_ref[...] * own * own, axis=0, keepdims=True)
    face_ref[...] = bent

    @pl.loop(0, kinds)
    def _(k):
        total = curl_ref[k, 0] * face_ref[0:1, :]
        for a in range(1, rows):
            total = total + curl_ref[k, a] * face_ref[a : a + 1, :]
        back_ref[:, pl.ds(pl.multiple_of(k * LANES, LANES), LANES)] = split_rows(total)

    spread = add_halves(nt_dot(back_ref[...], pat_ref[...]))
    rim = spread[:, LANES:]
    centre = sigma_ref[...] * own + spread[:, :LANES]
    centre_out[...] = centre
    rim_out[...] = rim
    lane = lane_iota(width)
    edges = jnp.logical_or(lane < 32, lane >= 96)
    msg_out[0:width, 0:LANES] = jnp.where(
        edges, centre, jnp.where(lane < 64, rim, pltpu.roll(rim, 64, 1))
    )

    links = []
    for i in range(block_ref.shape[0]):
        idx = jnp.broadcast_to(block_ref[i : i + 1, :], (width, LANES))
        got = gather_lanes(own, idx) * weight_ref[:, i * LANES : (i + 1) * LANES]
        links.append(jnp.sum(got, axis=0, keepdims=True))
    link = jnp.concatenate(links, axis=1)
    high = link.astype(BF16).astype(F32)
    mid = (link - high).astype(BF16).astype(F32)
    low = link - high - mid
    sub = lax.broadcasted_iota(jnp.int32, (8, link.shape[1]), 0)
    terms = jnp.where(sub == 0, high, jnp.where(sub == 1, mid, jnp.where(sub == 2, low, 0.0)))
    linkage = jnp.sum(nt_dot(terms.astype(BF16), coil_hot_ref[...]), axis=0, keepdims=True)

    coils = 84
    lane = lane_iota()
    norm = jnp.sum(jnp.sum(own * own, axis=0, keepdims=True), axis=1, keepdims=True)
    energy = jnp.sum(energy, axis=1, keepdims=True)
    line = linkage + jnp.where(lane == coils, norm, 0.0) + jnp.where(lane == coils + 1, energy, 0.0)
    if previous is not None:
        cross = jnp.sum(jnp.sum(own * previous, axis=0, keepdims=True), axis=1, keepdims=True)
        line = line + jnp.where(lane == coils + 2, cross, 0.0)
    row_out[...] = jnp.broadcast_to(line, row_out.shape)


def pick(line, at):
    return jnp.sum(jnp.where(lane_iota() == at, line, 0.0), axis=1, keepdims=True)


def first_kernel(count, rhs_ref, even_ref, odd_ref, sigma_ref, reluct_ref, curl_ref, pattern_ref,
                 weight_ref, block_ref, coil_ref, pat_ref, coil_hot_ref,
                 row_ref, msg_ref, centre_ref, rim_ref, halo_ref, *scratch):
    left, right = sides(even_ref[...], odd_ref[...])
    halo = halo_of(left, right, count)
    halo_ref[...] = halo
    width = rhs_ref.shape[0]
    msg_ref[0:width, LANES:] = weight_ref[...]
    msg_ref[width:, :] = jnp.zeros_like(msg_ref[width:, :])
    msg_ref[width : width + 1, LANES:] = rows_of(block_ref[...]).astype(F32)
    msg_ref[width + 1 : width + 2, LANES:] = rows_of(coil_ref[...]).astype(F32)
    refs = (sigma_ref, reluct_ref, curl_ref, pattern_ref, weight_ref, block_ref, coil_ref,
            pat_ref, coil_hot_ref)
    apply_local(refs, rhs_ref[...], halo, None, row_ref, msg_ref, centre_ref, rim_ref, scratch)


def scalars(rows_ref, inv_ref, scal_ref):
    coils = 84
    total = jnp.sum(rows_ref[...], axis=0, keepdims=True)
    current = total * inv_ref[0:1, :]
    norm, energy = pick(total, coils), pick(total, coils + 1)
    energy = energy + jnp.sum(current * total, axis=1, keepdims=True)
    if scal_ref is None:
        beta = None
        curve = energy
    else:
        beta = norm / pick(scal_ref[0:1, :], 0)
        cross = pick(total, coils + 2)
        curve = energy + 2.0 * beta * cross + beta * beta * pick(scal_ref[0:1, :], 1)
    lane = lane_iota()
    state = jnp.where(lane == 0, norm, jnp.where(lane == 1, curve, 0.0))
    return current, norm / curve, beta, state


def own_image(left, right, centre, weight, current, coils, blk):
    lane = lane_iota(*centre.shape)
    image = centre + jnp.where(lane < 32, pltpu.roll(left, 96, 1), 0.0)
    image = image + jnp.where(lane >= 96, pltpu.roll(right, 32, 1), 0.0)
    return image + add_halves(nt_dot(split_rows(weighted(weight, current, coils)), blk))


def step_kernel(count, first, *refs):
    names = ["rows", "even", "odd"] + ([] if first else ["evenc", "oddc"])
    names += ["centre", "rim", "res", "halo"] + ([] if first else ["dir", "img", "imgh", "sol", "scal"])
    names += ["inv", "blk", "sigma", "reluct", "curl", "pattern", "weight", "block", "coil", "pat",
              "coilhot"]
    names += ["row_o", "msg_o", "centre_o", "rim_o", "res_o", "halo_o", "dir_o", "img_o", "imgh_o",
              "sol_o", "scal_o"]
    r = dict(zip(names, refs))
    scratch = refs[len(names):]
    width = r["res"].shape[0]
    current, alpha, beta, state = scalars(r["rows"], r["inv"], r.get("scal"))
    r["scal_o"][...] = jnp.broadcast_to(state, r["scal_o"].shape)

    left, right = sides(r["even"][0:width, 0:LANES], r["odd"][0:width, 0:LANES])
    image = own_image(left, right, r["centre"][...], r["weight"][...], current,
                      rows_of(r["coil"][...]), r["blk"][...])

    ce, co = (r["even"], r["odd"]) if first else (r["evenc"], r["oddc"])
    cl, cr = sides(ce[:, LANES:], co[:, LANES:])
    spot = jnp.concatenate(
        [cl[width : width + 1].astype(jnp.int32) - 96, cr[width : width + 1].astype(jnp.int32) + 32],
        axis=1,
    )
    amount = jnp.concatenate(
        [
            weighted(c[0:width], current, c[width + 1 : width + 2].astype(jnp.int32))
            for c in (cl, cr)
        ],
        axis=1,
    )
    beyond = add_halves(nt_dot(split_rows(amount), onehot(spot, LANES)))
    lane = lane_iota(width)
    moved = jnp.where(lane < 32, pltpu.roll(left, 32, 1), pltpu.roll(right, 32, 1))
    image_halo = (moved + r["rim"][...] + beyond) * halo_mask(count)

    old = r["res"][...]
    if first:
        direction = old
        r["sol_o"][...] = alpha * direction
    else:
        direction = old + beta * r["dir"][...]
        image = image + beta * r["img"][...]
        image_halo = image_halo + beta * r["imgh"][...]
        r["sol_o"][...] = r["sol"][...] + alpha * direction
    r["dir_o"][...] = direction
    r["img_o"][...] = image
    r["imgh_o"][...] = image_halo
    own = old - alpha * image
    halo = r["halo"][...] - alpha * image_halo
    r["res_o"][...] = own
    r["halo_o"][...] = halo
    refs = tuple(r[k] for k in ("sigma", "reluct", "curl", "pattern", "weight", "block", "coil", "pat",
                                "coilhot"))
    apply_local(refs, own, halo, image, r["row_o"], r["msg_o"], r["centre_o"], r["rim_o"], scratch)


def last_kernel(rows_ref, even_ref, odd_ref, centre_ref, res_ref, dir_ref, img_ref, sol_ref, scal_ref,
                inv_ref, blk_ref, weight_ref, coil_ref, sol_out, res_out):
    current, alpha, beta, _ = scalars(rows_ref, inv_ref, scal_ref)
    left, right = sides(even_ref[...], odd_ref[...])
    image = own_image(left, right, centre_ref[...], weight_ref[...], current,
                      rows_of(coil_ref[...]), blk_ref[...])
    image = image + beta * img_ref[...]
    sol_out[...] = sol_ref[...] + alpha * (res_ref[...] + beta * dir_ref[...])
    res_out[...] = res_ref[...] - alpha * image


def call(kernel, args, outs, name, smem=(), scratch=()):
    return pl.pallas_call(
        kernel,
        name=name,
        in_specs=[
            pl.BlockSpec(memory_space=pltpu.SMEM if i in smem else VMEM) for i in range(len(args))
        ],
        out_specs=[pl.BlockSpec(memory_space=VMEM)] * len(outs),
        out_shape=[jax.ShapeDtypeStruct(s, d) for s, d in outs],
        scratch_shapes=list(scratch),
        compiler_params=pltpu.CompilerParams(vmem_limit_bytes=24 << 20),
    )(*args)


def body(count, right_side, sigma, reluctivity, curl_blocks, pattern, cond_weight, cond_block,
         cond_coil, coil_phase, coil_resistance, switch_state):
    width, blocks = right_side.shape
    kinds = pattern.shape[0]
    conductors = cond_weight.shape[1]
    block = cond_block.reshape(-1, LANES)
    coil = cond_coil.reshape(-1, LANES)
    phase = coil_phase.reshape(1, -1)
    ohm = coil_resistance.reshape(1, -1)
    tile = ((width, LANES), F32)

    inner = [(i, i ^ 1) for i in range(count)]
    outer = [(i, i + 1) for i in range(1, count - 1, 2)]
    outer = outer + [(b, a) for a, b in outer]

    def exchange(message):
        return lax.ppermute(message, "dom", outer), lax.ppermute(message, "dom", inner)

    def gather_rows(rows):
        return lax.all_to_all(rows, "dom", 0, 0, tiled=True)

    (rhs,) = call(
        rhs_kernel,
        (right_side, cond_weight, block, coil, phase, ohm, switch_state),
        [tile],
        "rhs",
        smem=(6,),
        scratch=[VMEM((8, LANES), F32)],
    )
    odd, even = exchange(rhs)
    pat, blk, coil_hot, inv = call(
        table_kernel,
        (pattern, block, coil, ohm),
        [((2 * LANES, kinds * LANES), BF16), ((LANES, conductors), BF16),
         ((LANES, conductors), BF16), ((8, LANES), F32)],
        "tables",
    )
    scratch = [VMEM((kinds, width, LANES), F32), VMEM((width, LANES), F32),
               VMEM((2 * width, kinds * LANES), BF16)]
    shared = (sigma, reluctivity, curl_blocks, pattern, cond_weight, block, coil, pat, coil_hot)
    line = ((count, LANES), F32)
    wide = ((width + 8, LANES + conductors), F32)
    row, message, centre, rim, halo = call(
        functools.partial(first_kernel, count),
        (rhs, even, odd) + shared,
        [line, wide, tile, tile, tile],
        "apply0",
        scratch=scratch,
    )
    odd_c, even_c = odd, even = exchange(message)
    rows = gather_rows(row)
    state = [line, tile, tile, tile, tile, tile, tile, tile, tile, tile, ((8, LANES), F32)]
    row, message, centre, rim, res, halo, direction, image, image_halo, sol, scal = call(
        functools.partial(step_kernel, count, True),
        (rows, even, odd, centre, rim, rhs, halo, inv, blk) + shared,
        state,
        "apply1",
        scratch=scratch,
    )
    for turn in range(2, ITERS):
        odd, even = exchange(message)
        rows = gather_rows(row)
        row, message, centre, rim, res, halo, direction, image, image_halo, sol, scal = call(
            functools.partial(step_kernel, count, False),
            (rows, even, odd, even_c, odd_c, centre, rim, res, halo, direction, image, image_halo,
             sol, scal, inv, blk) + shared,
            state,
            "apply%d" % turn,
            scratch=scratch,
        )
    odd, even = exchange(message)
    rows = gather_rows(row)
    sol, res = call(
        last_kernel,
        (rows, even, odd, centre, res, direction, image, sol, scal, inv, blk, cond_weight, coil),
        [tile, tile],
        "finish",
    )
    return sol, res


def solution(mesh):
    return jax.shard_map(
        functools.partial(body, mesh.shape["dom"]),
        mesh=mesh,
        in_specs=(
            P(None, "dom"),
            P(None, "dom"),
            P(None, "dom"),
            P(None, None, None, "dom"),
            P(None, "dom"),
            P(None, "dom"),
            P("dom"),
            P("dom", None),
            P(),
            P(),
            P(),
        ),
        out_specs=(P(None, "dom"), P(None, "dom")),
        check_vma=False,
    )
```

profile of v0, /device:TPU:1, one launch (start us, length us, event | category | flops | bytes accessed | tf_op | source)
XLA Modules:
  0.0 96.6 jit_solution(6964284019698723117)
XLA Ops:
  0.6 0.0 copy-start.3
  0.6 0.9 copy-done.3
  1.5 0.7 copy-done.10
  2.2 0.7 copy-done.15
  2.9 0.8 copy-done.17
  3.7 0.7 copy-done.18
  4.3 0.7 copy-done.19
  5.0 0.7 copy-done.20
  5.6 0.8 rhs.1.rhs_ref.refs_5_
  6.4 4.5 %collective-permute-start.1 = (f32[64,128]{1,0:T(8,128)S(1)}, f32[64,128]{1,0:T(8,128)S(1)}, u32[]{:S(2)}, u32[]{:S(2)}) collective-permute-start(f32[64,128]{1,0:T(8,128)S(1)} %rhs.1.rhs_ref.refs_5_), channel_id=1, source_target_pairs={{1,2},{3,4},{5,6},{7,8},{9,10},{11,12},{13,14},{15,16},{17,18},{19... | collective-permute-start | bytes 98312 | tf_op jit(solution)/shard_map/ppermute | solution.py:342
  10.9 0.1 collective-permute-start
  11.0 0.0 copy-start.12
  11.0 0.7 copy-done.12
  11.7 0.1 tables.1
  11.9 0.7 collective-permute-done.1.odd_ref
  12.5 0.0 collective-permute-done.even_ref
  12.5 4.6 %copy-done = f32[6,64,64,128]{3,2,1,0:T(8,128)S(1)} copy-done((f32[6,64,64,128]{3,2,1,0:T(8,128)S(1)}, f32[6,64,64,128]{3,2,1,0:T(8,128)}, u32[]{:S(2)}) %copy-start) | copy-done | bytes 12582936
  17.1 0.9 copy-done.4
  18.0 0.8 copy-done.6
  18.8 0.8 copy-done.8
  19.5 0.7 copy-done.13
  20.2 0.0 copy-start.11
  20.2 0.0 copy-start.16
  20.3 3.3 %apply0.1 = (f32[128,128]{1,0:T(8,128)S(1)}, f32[72,640]{1,0:T(8,128)S(1)}, f32[64,128]{1,0:T(8,128)S(1)}, f32[64,128]{1,0:T(8,128)S(1)}, f32[64,128]{1,0:T(8,128)S(1)}) custom-call(f32[64,128]{1,0:T(8,128)S(1)} %rhs.1.rhs_ref.refs_5_, f32[64,128]{1,0:T(8,128)S(1)} %collective-permute-done.even_ref, f32[64,128]{1,0:T(8,128)S(1)} %collective-permute-done.1.odd_ref, ...), custom_call_target="tpu_custom_call" | custom-call | tf_op jit(solution)/shard_map/apply0/pallas_call | solution.py:313
  23.6 3.8 %collective-permute-start.3 = (f32[72,640]{1,0:T(8,128)S(1)}, f32[72,640]{1,0:T(8,128)S(1)}, u32[]{:S(2)}, u32[]{:S(2)}) collective-permute-start(f32[72,640]{1,0:T(8,128)S(1)} %get-tuple-element.33), channel_id=1, source_target_pairs={{1,2},{3,4},{5,6},{7,8},{9,10},{11,12},{13,14},{15,16},{17,18},{19... | collective-permute-start | bytes 552968 | tf_op jit(solution)/shard_map/ppermute | solution.py:342
  27.3 0.1 collective-permute-start.2
  27.4 23.2 %all_to_all.33 = f32[128,1,128]{2,1,0:T(1,128)S(1)} all-to-all(f32[128,1,128]{2,1,0:T(1,128)S(1)} %bitcast.25), channel_id=1, replica_groups=mesh['dom'=128] {'dom'}, dimensions={0} | all-to-all | bytes 131072 | tf_op jit(solution)/shard_map/all_to_all | solution.py:345
  50.6 0.0 collective-permute-done.3.refs_2_.refs_4_
  50.6 0.0 collective-permute-done.2.refs_1_.refs_3_
  50.7 4.2 %apply1.1 = (f32[128,128]{1,0:T(8,128)}, f32[64,128]{1,0:T(8,128)S(1)}, f32[64,128]{1,0:T(8,128)S(1)}, f32[64,128]{1,0:T(8,128)S(1)}, f32[64,128]{1,0:T(8,128)S(...) custom-call(f32[128,128]{1,0:T(8,128)S(1)} %bitcast.17, ...), custom_call_target="tpu_custom_call" | custom-call | tf_op jit(solution)/shard_map/apply1/pallas_call | solution.py:313
  54.8 4.5 %all-to-all-start.1 = ((f32[128,1,128]{2,1,0:T(1,128)}), f32[128,1,128]{2,1,0:T(1,128)S(1)}, u32[]{:S(2)}, u32[]{:S(2)}) async-start(f32[128,1,128]{2,1,0:T(1,128)} %bitcast.8), calls=%async_computation.1 | async-start | bytes 131072 | tf_op jit(solution)/shard_map/all_to_all | solution.py:345
  59.3 3.5 %collective-permute-start.5 = (f32[64,128]{1,0:T(8,128)S(1)}, f32[64,128]{1,0:T(8,128)S(1)}, u32[]{:S(2)}, u32[]{:S(2)}) collective-permute-start(f32[64,128]{1,0:T(8,128)S(1)} %get-tuple-element.40), channel_id=1, source_target_pairs={{1,2},{3,4},{5,6},{7,8},{9,10},{11,12},{13,14},{15,16},{17,18},{19... | collective-permute-start | bytes 98312 | tf_op jit(solution)/shard_map/ppermute | solution.py:342
  62.9 0.1 collective-permute-start.4
  63.0 1.9 %collective-permute-done.5.refs_2_ = f32[64,128]{1,0:T(8,128)S(1)} collective-permute-done((f32[64,128]{1,0:T(8,128)S(1)}, f32[64,128]{1,0:T(8,128)S(1)}, u32[]{:S(2)}, u32[]{:S(2)}) %collective-permute-start.5) | collective-permute-done | bytes 32800 | tf_op jit(solution)/shard_map/ppermute | solution.py:342
  64.9 0.0 collective-permute-done.4.refs_1_
  64.9 4.1 %all-to-all-done.1 = f32[128,1,128]{2,1,0:T(1,128)S(1)} async-done(((f32[128,1,128]{2,1,0:T(1,128)}), f32[128,1,128]{2,1,0:T(1,128)S(1)}, u32[]{:S(2)}, u32[]{:S(2)}) %all-to-all-start.1) | async-done | bytes 65568 | tf_op jit(solution)/shard_map/all_to_all | solution.py:345
  69.0 0.0 copy-done.5
  69.0 0.0 copy-done.9
  69.0 0.0 copy-start.2
  69.0 4.6 %copy-done.2 = f32[6,64,64,128]{3,2,1,0:T(8,128)S(1)} copy-done((f32[6,64,64,128]{3,2,1,0:T(8,128)S(1)}, f32[6,64,64,128]{3,2,1,0:T(8,128)}, u32[]{:S(2)}) %copy-start.2) | copy-done | bytes 12582936
  73.6 3.7 %apply2.1 = (f32[128,128]{1,0:T(8,128)}, f32[64,128]{1,0:T(8,128)S(1)}, f32[64,128]{1,0:T(8,128)S(1)}, f32[64,128]{1,0:T(8,128)}, f32[64,128]{1,0:T(8,128)S(1)},...) custom-call(f32[128,128]{1,0:T(8,128)S(1)} %bitcast.16, ...), custom_call_target="tpu_custom_call" | custom-call | tf_op jit(solution)/shard_map/apply2/pallas_call | solution.py:313
  77.3 8.9 %all-to-all-start.2 = ((f32[128,1,128]{2,1,0:T(1,128)}), f32[128,1,128]{2,1,0:T(1,128)S(1)}, u32[]{:S(2)}, u32[]{:S(2)}) async-start(f32[128,1,128]{2,1,0:T(1,128)} %bitcast.11), calls=%async_computation.2 | async-start | bytes 131072 | tf_op jit(solution)/shard_map/all_to_all | solution.py:345
  86.2 3.5 %collective-permute-start.7 = (f32[64,128]{1,0:T(8,128)S(1)}, f32[64,128]{1,0:T(8,128)S(1)}, u32[]{:S(2)}, u32[]{:S(2)}) collective-permute-start(f32[64,128]{1,0:T(8,128)S(1)} %get-tuple-element.51), channel_id=1, source_target_pairs={{1,2},{3,4},{5,6},{7,8},{9,10},{11,12},{13,14},{15,16},{17,18},{19... | collective-permute-start | bytes 98312 | tf_op jit(solution)/shard_map/ppermute | solution.py:342
  89.7 0.1 collective-permute-start.6
  89.8 1.9 %collective-permute-done.7.odd_ref = f32[64,128]{1,0:T(8,128)S(1)} collective-permute-done((f32[64,128]{1,0:T(8,128)S(1)}, f32[64,128]{1,0:T(8,128)S(1)}, u32[]{:S(2)}, u32[]{:S(2)}) %collective-permute-start.7) | collective-permute-done | bytes 32800 | tf_op jit(solution)/shard_map/ppermute | solution.py:342
  91.7 0.0 collective-permute-done.6.even_ref
  91.7 4.1 %all-to-all-done.2 = f32[128,1,128]{2,1,0:T(1,128)S(1)} async-done(((f32[128,1,128]{2,1,0:T(1,128)}), f32[128,1,128]{2,1,0:T(1,128)S(1)}, u32[]{:S(2)}, u32[]{:S(2)}) %all-to-all-start.2) | async-done | bytes 65568 | tf_op jit(solution)/shard_map/all_to_all | solution.py:345
  95.8 0.9 finish.1
  (21 shorter events, 0.0 us)
Async XLA Ops:
  0.6 0.9 copy-start.3
  1.5 0.7 copy-start.10
  2.2 0.7 copy-start.15
  2.9 0.8 copy-start.17
  3.7 0.7 copy-start.18
  4.3 0.7 copy-start.19
  5.0 0.7 copy-start.20
  6.4 6.1 %collective-permute-start.1 = (f32[64,128]{1,0:T(8,128)S(1)}, f32[64,128]{1,0:T(8,128)S(1)}, u32[]{:S(2)}, u32[]{:S(2)}) collective-permute-start(f32[64,128]{1,0:T(8,128)S(1)} %rhs.1.rhs_ref.refs_5_), channel_id=1, source_target_pairs={{1,2},{3,4},{5,6},{7,8},{9,10},{11,12},{13,14},{15,16},{17,18},{19... | collective-permute-start | bytes 98312 | tf_op jit(solution)/shard_map/ppermute | solution.py:342
  10.9 1.6 %collective-permute-start = (f32[64,128]{1,0:T(8,128)S(1)}, f32[64,128]{1,0:T(8,128)S(1)}, u32[]{:S(2)}, u32[]{:S(2)}) collective-permute-start(f32[64,128]{1,0:T(8,128)S(1)} %rhs.1.rhs_ref.refs_5_), channel_id=1, source_target_pairs={{0,1},{1,0},{2,3},{3,2},{4,5},{5,4},{6,7},{7,6},{8,9},{9,8},{10,11... | collective-permute-start | bytes 98312 | tf_op jit(solution)/shard_map/ppermute | solution.py:342
  11.0 0.7 copy-start.12
  12.5 4.6 %copy-start = (f32[6,64,64,128]{3,2,1,0:T(8,128)S(1)}, f32[6,64,64,128]{3,2,1,0:T(8,128)}, u32[]{:S(2)}) copy-start(f32[6,64,64,128]{3,2,1,0:T(8,128)} %refs_18_.1) | copy-start | bytes 37748740
  17.1 0.9 copy-start.4
  18.0 0.8 copy-start.6
  18.8 0.8 copy-start.8
  19.5 0.7 copy-start.13
  20.2 30.4 %copy-start.1 = (f32[6,64,64,128]{3,2,1,0:T(8,128)S(1)}, f32[6,64,64,128]{3,2,1,0:T(8,128)}, u32[]{:S(2)}) copy-start(f32[6,64,64,128]{3,2,1,0:T(8,128)} %refs_18_.1) | copy-start | bytes 37748740
  20.2 48.7 %copy-start.5 = (f32[64,512]{1,0:T(8,128)S(1)}, f32[64,512]{1,0:T(8,128)}, u32[]{:S(2)}) copy-start(f32[64,512]{1,0:T(8,128)} %weight_ref.5) | copy-start | bytes 393220
  20.2 48.7 %copy-start.7 = (f32[64,128]{1,0:T(8,128)S(1)}, f32[64,128]{1,0:T(8,128)}, u32[]{:S(2)}) copy-start(f32[64,128]{1,0:T(8,128)} %refs_16_.1) | copy-start | bytes 98308
  20.2 48.7 %copy-start.9 = (f32[64,128]{1,0:T(8,128)S(1)}, f32[64,128]{1,0:T(8,128)}, u32[]{:S(2)}) copy-start(f32[64,128]{1,0:T(8,128)} %refs_17_.1) | copy-start | bytes 98308
  20.2 48.7 %copy-start.11 = (s32[512,1]{0,1:T(1,128)S(1)}, s32[512,1]{0,1:T(1,128)}, u32[]{:S(2)}) copy-start(s32[512,1]{0,1:T(1,128)} %param.18) | copy-start | bytes 6148
  20.2 48.7 %copy-start.14 = (s32[6,128]{1,0:T(8,128)S(1)}, s32[6,128]{1,0:T(8,128)}, u32[]{:S(2)}) copy-start(s32[6,128]{1,0:T(8,128)} %refs_19_.1) | copy-start | bytes 9220
  20.2 48.7 %copy-start.16 = (s32[512]{0:T(512)S(1)}, s32[512]{0:T(512)}, u32[]{:S(2)}) copy-start(s32[512]{0:T(512)} %param.17) | copy-start | bytes 6148
  23.6 27.1 %collective-permute-start.3 = (f32[72,640]{1,0:T(8,128)S(1)}, f32[72,640]{1,0:T(8,128)S(1)}, u32[]{:S(2)}, u32[]{:S(2)}) collective-permute-start(f32[72,640]{1,0:T(8,128)S(1)} %get-tuple-element.33), channel_id=1, source_target_pairs={{1,2},{3,4},{5,6},{7,8},{9,10},{11,12},{13,14},{15,16},{17,18},{19... | collective-permute-start | bytes 552968 | tf_op jit(solution)/shard_map/ppermute | solution.py:342
  27.3 23.3 %collective-permute-start.2 = (f32[72,640]{1,0:T(8,128)S(1)}, f32[72,640]{1,0:T(8,128)S(1)}, u32[]{:S(2)}, u32[]{:S(2)}) collective-permute-start(f32[72,640]{1,0:T(8,128)S(1)} %get-tuple-element.33), channel_id=1, source_target_pairs={{0,1},{1,0},{2,3},{3,2},{4,5},{5,4},{6,7},{7,6},{8,9},{9,8},{10,11... | collective-permute-start | bytes 552968 | tf_op jit(solution)/shard_map/ppermute | solution.py:342
  54.8 14.1 %all-to-all-start.1 = ((f32[128,1,128]{2,1,0:T(1,128)}), f32[128,1,128]{2,1,0:T(1,128)S(1)}, u32[]{:S(2)}, u32[]{:S(2)}) async-start(f32[128,1,128]{2,1,0:T(1,128)} %bitcast.8), calls=%async_computation.1 | async-start | bytes 131072 | tf_op jit(solution)/shard_map/all_to_all | solution.py:345
  59.3 5.5 %collective-permute-start.5 = (f32[64,128]{1,0:T(8,128)S(1)}, f32[64,128]{1,0:T(8,128)S(1)}, u32[]{:S(2)}, u32[]{:S(2)}) collective-permute-start(f32[64,128]{1,0:T(8,128)S(1)} %get-tuple-element.40), channel_id=1, source_target_pairs={{1,2},{3,4},{5,6},{7,8},{9,10},{11,12},{13,14},{15,16},{17,18},{19... | collective-permute-start | bytes 98312 | tf_op jit(solution)/shard_map/ppermute | solution.py:342
  62.9 2.0 %collective-permute-start.4 = (f32[64,128]{1,0:T(8,128)S(1)}, f32[64,128]{1,0:T(8,128)S(1)}, u32[]{:S(2)}, u32[]{:S(2)}) collective-permute-start(f32[64,128]{1,0:T(8,128)S(1)} %get-tuple-element.40), channel_id=1, source_target_pairs={{0,1},{1,0},{2,3},{3,2},{4,5},{5,4},{6,7},{7,6},{8,9},{9,8},{10,11... | collective-permute-start | bytes 98312 | tf_op jit(solution)/shard_map/ppermute | solution.py:342
  69.0 4.6 %copy-start.2 = (f32[6,64,64,128]{3,2,1,0:T(8,128)S(1)}, f32[6,64,64,128]{3,2,1,0:T(8,128)}, u32[]{:S(2)}) copy-start(f32[6,64,64,128]{3,2,1,0:T(8,128)} %refs_18_.1) | copy-start | bytes 37748740
  77.3 18.5 %all-to-all-start.2 = ((f32[128,1,128]{2,1,0:T(1,128)}), f32[128,1,128]{2,1,0:T(1,128)S(1)}, u32[]{:S(2)}, u32[]{:S(2)}) async-start(f32[128,1,128]{2,1,0:T(1,128)} %bitcast.11), calls=%async_computation.2 | async-start | bytes 131072 | tf_op jit(solution)/shard_map/all_to_all | solution.py:345
  86.2 5.5 %collective-permute-start.7 = (f32[64,128]{1,0:T(8,128)S(1)}, f32[64,128]{1,0:T(8,128)S(1)}, u32[]{:S(2)}, u32[]{:S(2)}) collective-permute-start(f32[64,128]{1,0:T(8,128)S(1)} %get-tuple-element.51), channel_id=1, source_target_pairs={{1,2},{3,4},{5,6},{7,8},{9,10},{11,12},{13,14},{15,16},{17,18},{19... | collective-permute-start | bytes 98312 | tf_op jit(solution)/shard_map/ppermute | solution.py:342
  89.7 2.0 %collective-permute-start.6 = (f32[64,128]{1,0:T(8,128)S(1)}, f32[64,128]{1,0:T(8,128)S(1)}, u32[]{:S(2)}, u32[]{:S(2)}) collective-permute-start(f32[64,128]{1,0:T(8,128)S(1)} %get-tuple-element.51), channel_id=1, source_target_pairs={{0,1},{1,0},{2,3},{3,2},{4,5},{5,4},{6,7},{7,6},{8,9},{9,8},{10,11... | collective-permute-start | bytes 98312 | tf_op jit(solution)/shard_map/ppermute | solution.py:342
where the time goes:
time: 97.3 us; the launch traced here: 96.6 us
  starting transfers between devices  29.1 us (30%)
  blocking collectives  23.2 us (24%)
  local copies, waits for them, and re-layouts  17.9 us (18%)
  Pallas kernels  13 us (13%)
  waiting for transfers between devices  12.6 us (13%)
    all_to_all x1, blocking collectives, gather_rows(): return lax.all_to_all(rows, 'dom', 0, 0, tiled=True)  23.2 us
    unnamed x42, local copies, waits for them, and re-layouts  17.9 us
    ppermute x4, starting transfers between devices, exchange(): lax.ppermute(message, 'dom', outer)  15.4 us
    all_to_all x2, starting transfers between devices, gather_rows(): return lax.all_to_all(rows, 'dom', 0, 0, tiled=True)  13.4 us
    pallas_call x6, Pallas kernels, call(): pl.pallas_call(kernel, name=name, in_specs=[pl.BlockSpec(memory_space=plt...  13 us
    all_to_all x2, waiting for transfers between devices, gather_rows(): return lax.all_to_all(rows, 'dom', 0, 0, tiled=True)  8.15 us
    ppermute x4, waiting for transfers between devices, exchange(): lax.ppermute(message, 'dom', outer)  4.44 us
  transfers between devices with their start and end apart: 10, of which 5 were waited for; matrix products, arithmetic and copies ran while one was open for 0% of the time, Pallas kernels for 0%

commit v1 on v0

--- a/solution.py
+++ b/solution.py
@@ -77,9 +77,33 @@
     return scratch[0:1, :]
 
 
+def move(pairs, sems):
+    copies = [pltpu.make_async_copy(src, dst, sems.at[i]) for i, (src, dst) in enumerate(pairs)]
+    for copy in copies:
+        copy.start()
+    return copies
+
+
 def rhs_kernel(
-    side_ref, weight_ref, block_ref, coil_ref, phase_ref, ohm_ref, state_ref, rhs_ref, pad_ref
+    side_hbm, weight_hbm, block_hbm, coil_hbm, phase_hbm, ohm_hbm, state_hbm, curl_hbm,
+    rhs_ref, weight_ref, block_ref, coil_ref, curl_ref,
+    side_ref, phase_ref, ohm_ref, state_ref, pad_ref, sems,
 ):
+    copies = move(
+        [
+            (coil_hbm, coil_ref),
+            (phase_hbm, phase_ref),
+            (ohm_hbm, ohm_ref),
+            (state_hbm, state_ref),
+            (weight_hbm, weight_ref),
+            (block_hbm, block_ref),
+            (side_hbm, side_ref),
+            (curl_hbm.at[0 : curl_ref.shape[0]], curl_ref),
+        ],
+        sems,
+    )
+    for copy in copies[:-1]:
+        copy.wait()
     s0, s1, s2 = (state_ref[i].astype(F32) for i in range(3))
     mean = (s0 + s1 + s2) / 3.0
     phase = phase_ref[...]
@@ -92,17 +116,35 @@
     coils, blocks = rows_of(coil_ref[...]), rows_of(block_ref[...])
     spread = split_rows(weighted(weight_ref[...], source, coils))
     rhs_ref[...] = side_ref[...] + add_halves(nt_dot(spread, onehot(blocks, LANES)))
-
-
-def table_kernel(pattern_ref, block_ref, coil_ref, ohm_ref, pat_ref, blk_ref, coil_hot_ref, inv_ref):
+    copies[-1].wait()
+
+
+def table_kernel(
+    pattern_hbm, ohm_hbm, sigma_hbm, reluct_hbm, curl_hbm, block_ref, coil_ref,
+    pat_ref, blk_ref, coil_hot_ref, inv_ref, pattern_ref, sigma_ref, reluct_ref, curl_ref,
+    ohm_ref, sems,
+):
+    copies = move(
+        [
+            (pattern_hbm, pattern_ref),
+            (ohm_hbm, ohm_ref),
+            (sigma_hbm, sigma_ref),
+            (reluct_hbm, reluct_ref),
+            (curl_hbm.at[2 : 2 + curl_ref.shape[0]], curl_ref),
+        ],
+        sems,
+    )
+    blk_ref[...] = onehot(rows_of(block_ref[...]), LANES)
+    coil_hot_ref[...] = onehot(rows_of(coil_ref[...]), LANES)
+    for copy in copies[:-1]:
+        copy.wait()
     for k in range(pattern_ref.shape[0]):
         q = pattern_ref[k : k + 1, :]
         slot = jnp.where(q < 32, q + 128, jnp.where(q < 160, q - 32, q))
         pat_ref[:, k * LANES : (k + 1) * LANES] = onehot(slot, 2 * LANES)
-    blk_ref[...] = onehot(rows_of(block_ref[...]), LANES)
-    coil_hot_ref[...] = onehot(rows_of(coil_ref[...]), LANES)
     inv_ref[...] = jnp.zeros_like(inv_ref)
     inv_ref[0:1, 0 : ohm_ref.shape[1]] = 1.0 / ohm_ref[...]
+    copies[-1].wait()
 
 
 def sides(a, b):
@@ -124,12 +166,23 @@
     return moved * halo_mask(count)
 
 
-def apply_local(refs, own, halo, previous, row_out, msg_out, centre_out, rim_out, scratch):
-    (sigma_ref, reluct_ref, curl_ref, pattern_ref, weight_ref, block_ref, coil_ref,
+def face_part(curl_refs, first_kind, picked_ref, first, total):
+    kind = first_kind
+    for curl_ref in curl_refs:
+        for k in range(curl_ref.shape[0]):
+            for t in range(0, picked_ref.shape[1], 8):
+                term = curl_ref[k, pl.ds(first, 8), t : t + 8, :] * picked_ref[kind, t : t + 8, :][None]
+                total = term if total is None else total + term
+            kind += 1
+    return total
+
+
+def apply_local(refs, own, halo, previous, row_out, msg_out, centre_out, rim_out, scratch, late=None):
+    (sigma_ref, reluct_ref, curl_refs, pattern_ref, weight_ref, block_ref, coil_ref,
      pat_ref, coil_hot_ref) = refs
-    picked_ref, face_ref, back_ref = scratch
+    picked_ref, face_ref, back_ref, partial_ref = scratch
     width = own.shape[0]
-    rows = curl_ref.shape[1]
+    rows = curl_refs[0].shape[1]
     kinds = pattern_ref.shape[0]
 
     for k in range(kinds):
@@ -140,14 +193,22 @@
         inside = jnp.broadcast_to(inside, (width, LANES))
         picked_ref[k] = jnp.where(inside, gather_lanes(own, idx), gather_lanes(halo, idx))
 
+    if late is not None:
+
+        @pl.loop(0, rows // 8)
+        def _(step):
+            first = pl.multiple_of(step * 8, 8)
+            partial_ref[pl.ds(first, 8)] = face_part(curl_refs[:2], 0, picked_ref, first, None)
+
+        late.wait()
+
     @pl.loop(0, rows // 8)
     def _(step):
         first = pl.multiple_of(step * 8, 8)
-        total = None
-        for k in range(kinds):
-            for t in range(0, width, 8):
-                term = curl_ref[k, pl.ds(first, 8), t : t + 8, :] * picked_ref[k, t : t + 8, :][None]
-                total = term if total is None else total + term
+        if late is None:
+            total = face_part(curl_refs, 0, picked_ref, first, None)
+        else:
+            total = face_part(curl_refs[2:], 4, picked_ref, first, partial_ref[pl.ds(first, 8)])
         face_ref[pl.ds(first, 8), :] = jnp.sum(total, axis=1)
 
     face = face_ref[...]
@@ -155,12 +216,15 @@
     energy = jnp.sum(bent * face + sigma_ref[...] * own * own, axis=0, keepdims=True)
     face_ref[...] = bent
 
-    @pl.loop(0, kinds)
-    def _(k):
-        total = curl_ref[k, 0] * face_ref[0:1, :]
-        for a in range(1, rows):
-            total = total + curl_ref[k, a] * face_ref[a : a + 1, :]
-        back_ref[:, pl.ds(pl.multiple_of(k * LANES, LANES), LANES)] = split_rows(total)
+    for at, curl_ref in enumerate(curl_refs):
+
+        @pl.loop(0, curl_ref.shape[0])
+        def _(k):
+            total = curl_ref[k, 0] * face_ref[0:1, :]
+            for a in range(1, rows):
+                total = total + curl_ref[k, a] * face_ref[a : a + 1, :]
+            where = pl.multiple_of((k + 2 * at) * LANES, LANES)
+            back_ref[:, pl.ds(where, LANES)] = split_rows(total)
 
     spread = add_halves(nt_dot(back_ref[...], pat_ref[...]))
     rim = spread[:, LANES:]
@@ -192,6 +256,7 @@
     energy = jnp.sum(energy, axis=1, keepdims=True)
     line = linkage + jnp.where(lane == coils, norm, 0.0) + jnp.where(lane == coils + 1, energy, 0.0)
     if previous is not None:
+        msg_out[:, LANES:] = jnp.zeros_like(msg_out[:, LANES:])
         cross = jnp.sum(jnp.sum(own * previous, axis=0, keepdims=True), axis=1, keepdims=True)
         line = line + jnp.where(lane == coils + 2, cross, 0.0)
     row_out[...] = jnp.broadcast_to(line, row_out.shape)
@@ -201,9 +266,11 @@
     return jnp.sum(jnp.where(lane_iota() == at, line, 0.0), axis=1, keepdims=True)
 
 
-def first_kernel(count, rhs_ref, even_ref, odd_ref, sigma_ref, reluct_ref, curl_ref, pattern_ref,
-                 weight_ref, block_ref, coil_ref, pat_ref, coil_hot_ref,
-                 row_ref, msg_ref, centre_ref, rim_ref, halo_ref, *scratch):
+def first_kernel(count, rhs_ref, even_ref, odd_ref, curl_hbm, sigma_ref, reluct_ref, curl0_ref,
+                 curl1_ref, pattern_ref, weight_ref, block_ref, coil_ref, pat_ref, coil_hot_ref,
+                 row_ref, msg_ref, centre_ref, rim_ref, halo_ref, curl2_ref, *scratch):
+    late = pltpu.make_async_copy(curl_hbm.at[4:], curl2_ref, scratch[-1])
+    late.start()
     left, right = sides(even_ref[...], odd_ref[...])
     halo = halo_of(left, right, count)
     halo_ref[...] = halo
@@ -212,9 +279,10 @@
     msg_ref[width:, :] = jnp.zeros_like(msg_ref[width:, :])
     msg_ref[width : width + 1, LANES:] = rows_of(block_ref[...]).astype(F32)
     msg_ref[width + 1 : width + 2, LANES:] = rows_of(coil_ref[...]).astype(F32)
-    refs = (sigma_ref, reluct_ref, curl_ref, pattern_ref, weight_ref, block_ref, coil_ref,
-            pat_ref, coil_hot_ref)
-    apply_local(refs, rhs_ref[...], halo, None, row_ref, msg_ref, centre_ref, rim_ref, scratch)
+    refs = (sigma_ref, reluct_ref, (curl0_ref, curl1_ref, curl2_ref), pattern_ref, weight_ref,
+            block_ref, coil_ref, pat_ref, coil_hot_ref)
+    apply_local(refs, rhs_ref[...], halo, None, row_ref, msg_ref, centre_ref, rim_ref, scratch[:-1],
+                late)
 
 
 def scalars(rows_ref, inv_ref, scal_ref):
@@ -245,8 +313,8 @@
 def step_kernel(count, first, *refs):
     names = ["rows", "even", "odd"] + ([] if first else ["evenc", "oddc"])
     names += ["centre", "rim", "res", "halo"] + ([] if first else ["dir", "img", "imgh", "sol", "scal"])
-    names += ["inv", "blk", "sigma", "reluct", "curl", "pattern", "weight", "block", "coil", "pat",
-              "coilhot"]
+    names += ["inv", "blk", "sigma", "reluct", "curl0", "curl1", "curl2", "pattern", "weight",
+              "block", "coil", "pat", "coilhot"]
     names += ["row_o", "msg_o", "centre_o", "rim_o", "res_o", "halo_o", "dir_o", "img_o", "imgh_o",
               "sol_o", "scal_o"]
     r = dict(zip(names, refs))
@@ -293,15 +361,15 @@
     halo = r["halo"][...] - alpha * image_halo
     r["res_o"][...] = own
     r["halo_o"][...] = halo
-    refs = tuple(r[k] for k in ("sigma", "reluct", "curl", "pattern", "weight", "block", "coil", "pat",
-                                "coilhot"))
+    refs = (r["sigma"], r["reluct"], (r["curl0"], r["curl1"], r["curl2"]))
+    refs += tuple(r[k] for k in ("pattern", "weight", "block", "coil", "pat", "coilhot"))
     apply_local(refs, own, halo, image, r["row_o"], r["msg_o"], r["centre_o"], r["rim_o"], scratch)
 
 
 def last_kernel(rows_ref, even_ref, odd_ref, centre_ref, res_ref, dir_ref, img_ref, sol_ref, scal_ref,
                 inv_ref, blk_ref, weight_ref, coil_ref, sol_out, res_out):
     current, alpha, beta, _ = scalars(rows_ref, inv_ref, scal_ref)
-    left, right = sides(even_ref[...], odd_ref[...])
+    left, right = sides(even_ref[:, 0:LANES], odd_ref[:, 0:LANES])
     image = own_image(left, right, centre_ref[...], weight_ref[...], current,
                       rows_of(coil_ref[...]), blk_ref[...])
     image = image + beta * img_ref[...]
@@ -309,17 +377,21 @@
     res_out[...] = res_ref[...] - alpha * image
 
 
-def call(kernel, args, outs, name, smem=(), scratch=()):
+def call(kernel, args, outs, name, hbm=(), scratch=()):
+    args = [
+        pltpu.with_memory_space_constraint(x, pltpu.HBM) if i in hbm else x
+        for i, x in enumerate(args)
+    ]
     return pl.pallas_call(
         kernel,
         name=name,
         in_specs=[
-            pl.BlockSpec(memory_space=pltpu.SMEM if i in smem else VMEM) for i in range(len(args))
+            pl.BlockSpec(memory_space=pltpu.HBM if i in hbm else VMEM) for i in range(len(args))
         ],
         out_specs=[pl.BlockSpec(memory_space=VMEM)] * len(outs),
         out_shape=[jax.ShapeDtypeStruct(s, d) for s, d in outs],
         scratch_shapes=list(scratch),
-        compiler_params=pltpu.CompilerParams(vmem_limit_bytes=24 << 20),
+        compiler_params=pltpu.CompilerParams(vmem_limit_bytes=8 << 20),
     )(*args)
 
 
@@ -344,37 +416,47 @@
     def gather_rows(rows):
         return lax.all_to_all(rows, "dom", 0, 0, tiled=True)
 
-    (rhs,) = call(
+    def like(x, count=None):
+        return ((x.shape if count is None else (count,) + x.shape[1:]), x.dtype)
+
+    rhs, weight_v, block_v, coil_v, curl0 = call(
         rhs_kernel,
-        (right_side, cond_weight, block, coil, phase, ohm, switch_state),
-        [tile],
+        (right_side, cond_weight, block, coil, phase, ohm, switch_state, curl_blocks),
+        [tile, like(cond_weight), like(block), like(coil), like(curl_blocks, 2)],
         "rhs",
-        smem=(6,),
-        scratch=[VMEM((8, LANES), F32)],
+        hbm=range(8),
+        scratch=[VMEM((width, LANES), F32), VMEM(phase.shape, phase.dtype), VMEM(ohm.shape, F32),
+                 pltpu.SMEM(switch_state.shape, switch_state.dtype), VMEM((8, LANES), F32),
+                 pltpu.SemaphoreType.DMA((8,))],
     )
     odd, even = exchange(rhs)
-    pat, blk, coil_hot, inv = call(
+    pat, blk, coil_hot, inv, pattern_v, sigma_v, reluct_v, curl1 = call(
         table_kernel,
-        (pattern, block, coil, ohm),
+        (pattern, ohm, sigma, reluctivity, curl_blocks, block_v, coil_v),
         [((2 * LANES, kinds * LANES), BF16), ((LANES, conductors), BF16),
-         ((LANES, conductors), BF16), ((8, LANES), F32)],
+         ((LANES, conductors), BF16), ((8, LANES), F32), like(pattern), tile, tile,
+         like(curl_blocks, 2)],
         "tables",
+        hbm=range(5),
+        scratch=[VMEM(ohm.shape, F32), pltpu.SemaphoreType.DMA((5,))],
     )
     scratch = [VMEM((kinds, width, LANES), F32), VMEM((width, LANES), F32),
-               VMEM((2 * width, kinds * LANES), BF16)]
-    shared = (sigma, reluctivity, curl_blocks, pattern, cond_weight, block, coil, pat, coil_hot)
+               VMEM((2 * width, kinds * LANES), BF16), VMEM((width, 8, LANES), F32)]
+    plane = (pattern_v, weight_v, block_v, coil_v, pat, coil_hot)
     line = ((count, LANES), F32)
     wide = ((width + 8, LANES + conductors), F32)
-    row, message, centre, rim, halo = call(
+    row, message, centre, rim, halo, curl2 = call(
         functools.partial(first_kernel, count),
-        (rhs, even, odd) + shared,
-        [line, wide, tile, tile, tile],
+        (rhs, even, odd, curl_blocks, sigma_v, reluct_v, curl0, curl1) + plane,
+        [line, wide, tile, tile, tile, like(curl_blocks, 2)],
         "apply0",
-        scratch=scratch,
-    )
+        hbm=(3,),
+        scratch=scratch + [pltpu.SemaphoreType.DMA(())],
+    )
+    shared = (sigma_v, reluct_v, curl0, curl1, curl2) + plane
     odd_c, even_c = odd, even = exchange(message)
     rows = gather_rows(row)
-    state = [line, tile, tile, tile, tile, tile, tile, tile, tile, tile, ((8, LANES), F32)]
+    state = [line, ((width, 3 * LANES), F32), tile, tile, tile, tile, tile, tile, tile, tile, ((8, LANES), F32)]
     row, message, centre, rim, res, halo, direction, image, image_halo, sol, scal = call(
         functools.partial(step_kernel, count, True),
         (rows, even, odd, centre, rim, rhs, halo, inv, blk) + shared,
@@ -397,7 +479,7 @@
     rows = gather_rows(row)
     sol, res = call(
         last_kernel,
-        (rows, even, odd, centre, res, direction, image, sol, scal, inv, blk, cond_weight, coil),
+        (rows, even, odd, centre, res, direction, image, sol, scal, inv, blk, weight_v, coil_v),
         [tile, tile],
         "finish",
     )

time: 97.3 us -> 87.7 us (0.901)
  blocking collectives: 23.2 us -> 56 us
  local copies, waits for them, and re-layouts: 17.9 us -> 0 us
  starting transfers between devices: 29.1 us -> 14 us
  waiting for transfers between devices: 12.6 us -> 0.02 us
  Pallas kernels: 13 us -> 16.7 us
    all_to_all x1 -> x3, blocking collectives: 23.2 us -> 56 us  [gather_rows(): return lax.all_to_all(rows, 'dom', 0, 0, tiled=True)]
    unnamed x42 -> x0, local copies, waits for them, and re-layouts: 17.9 us -> none
    all_to_all x2 -> x0, starting transfers between devices: 13.4 us -> none  [gather_rows(): return lax.all_to_all(rows, 'dom', 0, 0, tiled=True)]
    all_to_all x2 -> x0, waiting for transfers between devices: 8.15 us -> none  [gather_rows(): return lax.all_to_all(rows, 'dom', 0, 0, tiled=True)]
    ppermute x4, waiting for transfers between devices: 4.44 us -> 0.01 us  [exchange(): lax.ppermute(message, 'dom', outer)]
    pallas_call x6, Pallas kernels: 13 us -> 16.7 us  [call(): pl.pallas_call(kernel, name=name, in_specs=[pl.BlockSpec(memory_space=plt...]
    ppermute x4, starting transfers between devices: 15.4 us -> 13.7 us  [exchange(): lax.ppermute(message, 'dom', outer)]
  transfers between devices with their start and end apart: 10 -> 8, of which waited for: 5 -> 0; matrix products, arithmetic and copies ran while one was open for 0% -> 0% of each run, Pallas kernels for 0% -> 3%
where the time goes in v1:
time: 87.7 us; the launch traced here: 87.4 us
  blocking collectives  56 us (64%)
  Pallas kernels  16.7 us (19%)
  starting transfers between devices  14 us (16%)
    all_to_all x3, blocking collectives, gather_rows(): return lax.all_to_all(rows, 'dom', 0, 0, tiled=True)  56 us
    pallas_call x6, Pallas kernels, call(): pl.pallas_call(kernel, name=name, in_specs=[pl.BlockSpec(memory_space=plt...  16.7 us
    ppermute x4, starting transfers between devices, exchange(): lax.ppermute(message, 'dom', outer)  13.7 us
  transfers between devices with their start and end apart: 8, of which 0 were waited for; matrix products, arithmetic and copies ran while one was open for 0% of the time, Pallas kernels for 3%

profile of v1, /device:TPU:1, one launch (start us, length us, event | category | flops | bytes accessed | tf_op | source)
XLA Modules:
  0.0 87.4 jit_solution(4987549651741651945)
XLA Ops:
  0.6 2.4 %rhs.1 = (f32[64,128]{1,0:T(8,128)S(1)}, f32[64,512]{1,0:T(8,128)S(1)}, s32[4,128]{1,0:T(4,128)S(1)}, s32[4,128]{1,0:T(4,128)S(1)}, f32[2,64,64,128]{3,2,1,0:T(8,128)S(1)}) custom-call(f32[64,128]{1,0:T(8,128)} %side_hbm.1, f32[64,512]{1,0:T(8,128)} %weight_hbm.1, s32[4,128]{1,0:T(4,128)} %bitcast.22, s32[4,128]{1,0:T(4,128)} %bitcast.23, s32[1,84]{1,0:T(1,128)} %bitcast.26, ...), custom_call_target="tpu_custom_call" | custom-call | tf_op jit(solution)/shard_map/rhs/pallas_call | solution.py:385
  3.1 4.5 %collective-permute-start.1 = (f32[64,128]{1,0:T(8,128)S(1)}, f32[64,128]{1,0:T(8,128)S(1)}, u32[]{:S(2)}, u32[]{:S(2)}) collective-permute-start(f32[64,128]{1,0:T(8,128)S(1)} %get-tuple-element.40.rhs_ref.refs_5_), channel_id=1, source_target_pairs={{1,2},{3,4},{5,6},{7,8},{9,10},{11,12},{13,14},{15,16},{17,18},{19... | collective-permute-start | bytes 98312 | tf_op jit(solution)/shard_map/ppermute | solution.py:414
  7.6 0.1 collective-permute-start
  7.7 2.3 %tables.1 = (bf16[256,768]{1,0:T(8,128)(2,1)S(1)}, bf16[128,512]{1,0:T(8,128)(2,1)S(1)}, bf16[128,512]{1,0:T(8,128)(2,1)S(1)}, f32[8,128]{1,0:T(8,128)S(1)}, s32...) custom-call(s32[6,128]{1,0:T(8,128)} %pattern_hbm.1, ...), custom_call_target="tpu_custom_call" | custom-call | tf_op jit(solution)/shard_map/tables/pallas_call | solution.py:385
  10.0 0.0 collective-permute-done.1.odd_ref
  10.0 0.0 collective-permute-done.even_ref
  10.0 4.3 %apply0.1 = (f32[128,128]{1,0:T(8,128)S(1)}, f32[72,640]{1,0:T(8,128)S(1)}, f32[64,128]{1,0:T(8,128)S(1)}, f32[64,128]{1,0:T(8,128)S(1)}, f32[64,128]{1,0:T(8,128)S(1)}, /*index=5*/f32[2,64,64,128]{3,2,1,0:T(8,128)S(1)}) custom-call(f32[64,128]{1,0:T(8,128)S(1)} %get-tuple-element.40.rhs_ref.refs_5_, f32[64,128]{1,0:T(8,128)S(1)} %collective-permute-done.even_ref, ...), custom_call_target="tpu_custom_call" | custom-call | tf_op jit(solution)/shard_map/apply0/pallas_call | solution.py:385
  14.3 3.5 %collective-permute-start.3 = (f32[72,640]{1,0:T(8,128)S(1)}, f32[72,640]{1,0:T(8,128)S(1)}, u32[]{:S(2)}, u32[]{:S(2)}) collective-permute-start(f32[72,640]{1,0:T(8,128)S(1)} %get-tuple-element.52), channel_id=1, source_target_pairs={{1,2},{3,4},{5,6},{7,8},{9,10},{11,12},{13,14},{15,16},{17,18},{19... | collective-permute-start | bytes 552968 | tf_op jit(solution)/shard_map/ppermute | solution.py:414
  17.8 0.1 collective-permute-start.2
  17.9 22.5 %all_to_all.33 = f32[128,1,128]{2,1,0:T(1,128)S(1)} all-to-all(f32[128,1,128]{2,1,0:T(1,128)S(1)} %bitcast.21), channel_id=1, replica_groups=mesh['dom'=128] {'dom'}, dimensions={0} | all-to-all | bytes 131072 | tf_op jit(solution)/shard_map/all_to_all | solution.py:417
  40.4 0.0 collective-permute-done.3.refs_2_.refs_4_
  40.4 0.0 collective-permute-done.2.refs_1_.refs_3_
  40.4 3.1 %apply1.1 = (f32[128,128]{1,0:T(8,128)S(1)}, f32[64,384]{1,0:T(8,128)S(1)}, f32[64,128]{1,0:T(8,128)S(1)}, f32[64,128]{1,0:T(8,128)S(1)}, f32[64,128]{1,0:T(8,12...) custom-call(f32[128,128]{1,0:T(8,128)S(1)} %bitcast.17, ...), custom_call_target="tpu_custom_call" | custom-call | tf_op jit(solution)/shard_map/apply1/pallas_call | solution.py:385
  43.5 2.8 %collective-permute-start.5 = (f32[64,384]{1,0:T(8,128)S(1)}, f32[64,384]{1,0:T(8,128)S(1)}, u32[]{:S(2)}, u32[]{:S(2)}) collective-permute-start(f32[64,384]{1,0:T(8,128)S(1)} %get-tuple-element.60), channel_id=1, source_target_pairs={{1,2},{3,4},{5,6},{7,8},{9,10},{11,12},{13,14},{15,16},{17,18},{19... | collective-permute-start | bytes 294920 | tf_op jit(solution)/shard_map/ppermute | solution.py:414
  46.3 0.1 collective-permute-start.4
  46.4 16.7 %all_to_all.34 = f32[128,1,128]{2,1,0:T(1,128)S(1)} all-to-all(f32[128,1,128]{2,1,0:T(1,128)S(1)} %bitcast.20), channel_id=1, replica_groups=mesh['dom'=128] {'dom'}, dimensions={0} | all-to-all | bytes 131072 | tf_op jit(solution)/shard_map/all_to_all | solution.py:417
  63.2 0.0 collective-permute-done.5.refs_2_
  63.2 0.0 collective-permute-done.4.refs_1_
  63.2 3.7 %apply2.1 = (f32[128,128]{1,0:T(8,128)S(1)}, f32[64,384]{1,0:T(8,128)S(1)}, f32[64,128]{1,0:T(8,128)S(1)}, f32[64,128]{1,0:T(8,128)}, f32[64,128]{1,0:T(8,128)S(...) custom-call(f32[128,128]{1,0:T(8,128)S(1)} %bitcast.16, ...), custom_call_target="tpu_custom_call" | custom-call | tf_op jit(solution)/shard_map/apply2/pallas_call | solution.py:385
  66.9 2.8 %collective-permute-start.7 = (f32[64,384]{1,0:T(8,128)S(1)}, f32[64,384]{1,0:T(8,128)S(1)}, u32[]{:S(2)}, u32[]{:S(2)}) collective-permute-start(f32[64,384]{1,0:T(8,128)S(1)} %get-tuple-element.71), channel_id=1, source_target_pairs={{1,2},{3,4},{5,6},{7,8},{9,10},{11,12},{13,14},{15,16},{17,18},{19... | collective-permute-start | bytes 294920 | tf_op jit(solution)/shard_map/ppermute | solution.py:414
  69.7 0.1 collective-permute-start.6
  69.8 16.7 %all_to_all.35 = f32[128,1,128]{2,1,0:T(1,128)S(1)} all-to-all(f32[128,1,128]{2,1,0:T(1,128)S(1)} %bitcast.19), channel_id=1, replica_groups=mesh['dom'=128] {'dom'}, dimensions={0} | all-to-all | bytes 131072 | tf_op jit(solution)/shard_map/all_to_all | solution.py:417
  86.5 0.0 collective-permute-done.7.odd_ref
  86.5 0.0 collective-permute-done.6.even_ref
  86.5 0.9 %finish.1 = (f32[64,128]{1,0:T(8,128)}, f32[64,128]{1,0:T(8,128)}) custom-call(f32[128,128]{1,0:T(8,128)S(1)} %bitcast.18, f32[64,384]{1,0:T(8,128)S(1)} %collective-permute-done.6.even_ref, f32[64,384]{1,0:T(8,128)S(1)} %collective-permute-done.7.odd_ref, f32[64,128]{1,0:T(8,128)S(1)} %get-tuple-element.72.centre_ref, ...), custom_call_target="tpu_custom_call" | custom-call | tf_op jit(solution)/shard_map/finish/pallas_call | solution.py:385
Async XLA Ops:
  3.1 6.9 %collective-permute-start.1 = (f32[64,128]{1,0:T(8,128)S(1)}, f32[64,128]{1,0:T(8,128)S(1)}, u32[]{:S(2)}, u32[]{:S(2)}) collective-permute-start(f32[64,128]{1,0:T(8,128)S(1)} %get-tuple-element.40.rhs_ref.refs_5_), channel_id=1, source_target_pairs={{1,2},{3,4},{5,6},{7,8},{9,10},{11,12},{13,14},{15,16},{17,18},{19... | collective-permute-start | bytes 98312 | tf_op jit(solution)/shard_map/ppermute | solution.py:414
  7.6 2.4 %collective-permute-start = (f32[64,128]{1,0:T(8,128)S(1)}, f32[64,128]{1,0:T(8,128)S(1)}, u32[]{:S(2)}, u32[]{:S(2)}) collective-permute-start(f32[64,128]{1,0:T(8,128)S(1)} %get-tuple-element.40.rhs_ref.refs_5_), channel_id=1, source_target_pairs={{0,1},{1,0},{2,3},{3,2},{4,5},{5,4},{6,7},{7,6},{8,9},{9,8},{10,11... | collective-permute-start | bytes 98312 | tf_op jit(solution)/shard_map/ppermute | solution.py:414
  14.3 26.1 %collective-permute-start.3 = (f32[72,640]{1,0:T(8,128)S(1)}, f32[72,640]{1,0:T(8,128)S(1)}, u32[]{:S(2)}, u32[]{:S(2)}) collective-permute-start(f32[72,640]{1,0:T(8,128)S(1)} %get-tuple-element.52), channel_id=1, source_target_pairs={{1,2},{3,4},{5,6},{7,8},{9,10},{11,12},{13,14},{15,16},{17,18},{19... | collective-permute-start | bytes 552968 | tf_op jit(solution)/shard_map/ppermute | solution.py:414
  17.8 22.6 %collective-permute-start.2 = (f32[72,640]{1,0:T(8,128)S(1)}, f32[72,640]{1,0:T(8,128)S(1)}, u32[]{:S(2)}, u32[]{:S(2)}) collective-permute-start(f32[72,640]{1,0:T(8,128)S(1)} %get-tuple-element.52), channel_id=1, source_target_pairs={{0,1},{1,0},{2,3},{3,2},{4,5},{5,4},{6,7},{7,6},{8,9},{9,8},{10,11... | collective-permute-start | bytes 552968 | tf_op jit(solution)/shard_map/ppermute | solution.py:414
  43.5 19.7 %collective-permute-start.5 = (f32[64,384]{1,0:T(8,128)S(1)}, f32[64,384]{1,0:T(8,128)S(1)}, u32[]{:S(2)}, u32[]{:S(2)}) collective-permute-start(f32[64,384]{1,0:T(8,128)S(1)} %get-tuple-element.60), channel_id=1, source_target_pairs={{1,2},{3,4},{5,6},{7,8},{9,10},{11,12},{13,14},{15,16},{17,18},{19... | collective-permute-start | bytes 294920 | tf_op jit(solution)/shard_map/ppermute | solution.py:414
  46.3 16.8 %collective-permute-start.4 = (f32[64,384]{1,0:T(8,128)S(1)}, f32[64,384]{1,0:T(8,128)S(1)}, u32[]{:S(2)}, u32[]{:S(2)}) collective-permute-start(f32[64,384]{1,0:T(8,128)S(1)} %get-tuple-element.60), channel_id=1, source_target_pairs={{0,1},{1,0},{2,3},{3,2},{4,5},{5,4},{6,7},{7,6},{8,9},{9,8},{10,11... | collective-permute-start | bytes 294920 | tf_op jit(solution)/shard_map/ppermute | solution.py:414
  66.9 19.7 %collective-permute-start.7 = (f32[64,384]{1,0:T(8,128)S(1)}, f32[64,384]{1,0:T(8,128)S(1)}, u32[]{:S(2)}, u32[]{:S(2)}) collective-permute-start(f32[64,384]{1,0:T(8,128)S(1)} %get-tuple-element.71), channel_id=1, source_target_pairs={{1,2},{3,4},{5,6},{7,8},{9,10},{11,12},{13,14},{15,16},{17,18},{19... | collective-permute-start | bytes 294920 | tf_op jit(solution)/shard_map/ppermute | solution.py:414
  69.7 16.8 %collective-permute-start.6 = (f32[64,384]{1,0:T(8,128)S(1)}, f32[64,384]{1,0:T(8,128)S(1)}, u32[]{:S(2)}, u32[]{:S(2)}) collective-permute-start(f32[64,384]{1,0:T(8,128)S(1)} %get-tuple-element.71), channel_id=1, source_target_pairs={{0,1},{1,0},{2,3},{3,2},{4,5},{5,4},{6,7},{7,6},{8,9},{9,8},{10,11... | collective-permute-start | bytes 294920 | tf_op jit(solution)/shard_map/ppermute | solution.py:414

commit v2 on v0

--- a/solution.py
+++ b/solution.py
@@ -10,6 +10,8 @@
 ITERS = 3
 LINK_SCALE = 16.0
 LANES = 128
+COILS = 84
+COST = 1 << 34
 F32 = jnp.float32
 BF16 = jnp.bfloat16
 VMEM = pltpu.VMEM
@@ -77,9 +79,32 @@
     return scratch[0:1, :]
 
 
+def move(pairs, sems):
+    copies = [pltpu.make_async_copy(src, dst, sems.at[i]) for i, (src, dst) in enumerate(pairs)]
+    for copy in copies:
+        copy.start()
+    return copies
+
+
 def rhs_kernel(
-    side_ref, weight_ref, block_ref, coil_ref, phase_ref, ohm_ref, state_ref, rhs_ref, pad_ref
+    side_hbm, weight_hbm, block_hbm, coil_hbm, phase_hbm, ohm_hbm, state_hbm,
+    rhs_ref, weight_ref, block_ref, coil_ref,
+    side_ref, phase_ref, ohm_ref, state_ref, pad_ref, sems,
 ):
+    copies = move(
+        [
+            (coil_hbm, coil_ref),
+            (phase_hbm, phase_ref),
+            (ohm_hbm, ohm_ref),
+            (state_hbm, state_ref),
+            (weight_hbm, weight_ref),
+            (block_hbm, block_ref),
+            (side_hbm, side_ref),
+        ],
+        sems,
+    )
+    for copy in copies:
+        copy.wait()
     s0, s1, s2 = (state_ref[i].astype(F32) for i in range(3))
     mean = (s0 + s1 + s2) / 3.0
     phase = phase_ref[...]
@@ -94,13 +119,28 @@
     rhs_ref[...] = side_ref[...] + add_halves(nt_dot(spread, onehot(blocks, LANES)))
 
 
-def table_kernel(pattern_ref, block_ref, coil_ref, ohm_ref, pat_ref, blk_ref, coil_hot_ref, inv_ref):
+def table_kernel(
+    pattern_hbm, ohm_hbm, sigma_hbm, reluct_hbm, block_ref, coil_ref,
+    pat_ref, blk_ref, coil_hot_ref, inv_ref, pattern_ref, sigma_ref, reluct_ref,
+    ohm_ref, sems,
+):
+    copies = move(
+        [
+            (pattern_hbm, pattern_ref),
+            (ohm_hbm, ohm_ref),
+            (sigma_hbm, sigma_ref),
+            (reluct_hbm, reluct_ref),
+        ],
+        sems,
+    )
+    blk_ref[...] = onehot(rows_of(block_ref[...]), LANES)
+    coil_hot_ref[...] = onehot(rows_of(coil_ref[...]), LANES)
+    for copy in copies:
+        copy.wait()
     for k in range(pattern_ref.shape[0]):
         q = pattern_ref[k : k + 1, :]
         slot = jnp.where(q < 32, q + 128, jnp.where(q < 160, q - 32, q))
         pat_ref[:, k * LANES : (k + 1) * LANES] = onehot(slot, 2 * LANES)
-    blk_ref[...] = onehot(rows_of(block_ref[...]), LANES)
-    coil_hot_ref[...] = onehot(rows_of(coil_ref[...]), LANES)
     inv_ref[...] = jnp.zeros_like(inv_ref)
     inv_ref[0:1, 0 : ohm_ref.shape[1]] = 1.0 / ohm_ref[...]
 
@@ -124,21 +164,19 @@
     return moved * halo_mask(count)
 
 
-def apply_local(refs, own, halo, previous, row_out, msg_out, centre_out, rim_out, scratch):
-    (sigma_ref, reluct_ref, curl_ref, pattern_ref, weight_ref, block_ref, coil_ref,
-     pat_ref, coil_hot_ref) = refs
-    picked_ref, face_ref, back_ref = scratch
+def pick_edges(pattern_ref, own, halo, picked_ref):
     width = own.shape[0]
-    rows = curl_ref.shape[1]
-    kinds = pattern_ref.shape[0]
-
-    for k in range(kinds):
+    for k in range(pattern_ref.shape[0]):
         q = pattern_ref[k : k + 1, :]
         inside = jnp.logical_and(q >= 32, q < 160)
         idx = jnp.where(q < 32, q, jnp.where(inside, q - 32, q - 128))
         idx = jnp.broadcast_to(idx, (width, LANES))
         inside = jnp.broadcast_to(inside, (width, LANES))
         picked_ref[k] = jnp.where(inside, gather_lanes(own, idx), gather_lanes(halo, idx))
+
+
+def forward(curl_ref, picked_ref, face_ref):
+    kinds, rows, width, _ = curl_ref.shape
 
     @pl.loop(0, rows // 8)
     def _(step):
@@ -150,29 +188,32 @@
                 total = term if total is None else total + term
         face_ref[pl.ds(first, 8), :] = jnp.sum(total, axis=1)
 
-    face = face_ref[...]
-    bent = reluct_ref[...] * face
-    energy = jnp.sum(bent * face + sigma_ref[...] * own * own, axis=0, keepdims=True)
-    face_ref[...] = bent
+
+def backward(curl_ref, bent_ref, back_ref, pat_ref, sigma_ref, own, centre_out, rim_out, msg_out):
+    kinds, rows, width, _ = curl_ref.shape
 
     @pl.loop(0, kinds)
     def _(k):
-        total = curl_ref[k, 0] * face_ref[0:1, :]
+        total = curl_ref[k, 0] * bent_ref[0:1, :]
         for a in range(1, rows):
-            total = total + curl_ref[k, a] * face_ref[a : a + 1, :]
+            total = total + curl_ref[k, a] * bent_ref[a : a + 1, :]
         back_ref[:, pl.ds(pl.multiple_of(k * LANES, LANES), LANES)] = split_rows(total)
 
     spread = add_halves(nt_dot(back_ref[...], pat_ref[...]))
     rim = spread[:, LANES:]
     centre = sigma_ref[...] * own + spread[:, :LANES]
     centre_out[...] = centre
-    rim_out[...] = rim
+    if rim_out is not None:
+        rim_out[...] = rim
     lane = lane_iota(width)
     edges = jnp.logical_or(lane < 32, lane >= 96)
     msg_out[0:width, 0:LANES] = jnp.where(
         edges, centre, jnp.where(lane < 64, rim, pltpu.roll(rim, 64, 1))
     )
 
+
+def summed_row(own, previous, energy, weight_ref, block_ref, coil_hot_ref, row_out):
+    width = own.shape[0]
     links = []
     for i in range(block_ref.shape[0]):
         idx = jnp.broadcast_to(block_ref[i : i + 1, :], (width, LANES))
@@ -186,15 +227,25 @@
     terms = jnp.where(sub == 0, high, jnp.where(sub == 1, mid, jnp.where(sub == 2, low, 0.0)))
     linkage = jnp.sum(nt_dot(terms.astype(BF16), coil_hot_ref[...]), axis=0, keepdims=True)
 
-    coils = 84
     lane = lane_iota()
     norm = jnp.sum(jnp.sum(own * own, axis=0, keepdims=True), axis=1, keepdims=True)
     energy = jnp.sum(energy, axis=1, keepdims=True)
-    line = linkage + jnp.where(lane == coils, norm, 0.0) + jnp.where(lane == coils + 1, energy, 0.0)
+    line = linkage + jnp.where(lane == COILS, norm, 0.0) + jnp.where(lane == COILS + 1, energy, 0.0)
     if previous is not None:
         cross = jnp.sum(jnp.sum(own * previous, axis=0, keepdims=True), axis=1, keepdims=True)
-        line = line + jnp.where(lane == coils + 2, cross, 0.0)
+        line = line + jnp.where(lane == COILS + 2, cross, 0.0)
     row_out[...] = jnp.broadcast_to(line, row_out.shape)
+
+
+def face_side(refs, own, halo, previous, row_out, picked_ref, face_ref):
+    sigma_ref, reluct_ref, curl_ref, pattern_ref, weight_ref, block_ref, coil_hot_ref = refs
+    pick_edges(pattern_ref, own, halo, picked_ref)
+    forward(curl_ref, picked_ref, face_ref)
+    face = face_ref[...]
+    bent = reluct_ref[...] * face
+    face_ref[...] = bent
+    energy = jnp.sum(bent * face + sigma_ref[...] * own * own, axis=0, keepdims=True)
+    summed_row(own, previous, energy, weight_ref, block_ref, coil_hot_ref, row_out)
 
 
 def pick(line, at):
@@ -202,8 +253,9 @@
 
 
 def first_kernel(count, rhs_ref, even_ref, odd_ref, sigma_ref, reluct_ref, curl_ref, pattern_ref,
-                 weight_ref, block_ref, coil_ref, pat_ref, coil_hot_ref,
-                 row_ref, msg_ref, centre_ref, rim_ref, halo_ref, *scratch):
+                 weight_ref, block_ref, coil_hot_ref, pat_ref, coil_ref,
+                 row_ref, msg_ref, centre_ref, rim_ref, halo_ref,
+                 picked_ref, face_ref, back_ref):
     left, right = sides(even_ref[...], odd_ref[...])
     halo = halo_of(left, right, count)
     halo_ref[...] = halo
@@ -212,23 +264,23 @@
     msg_ref[width:, :] = jnp.zeros_like(msg_ref[width:, :])
     msg_ref[width : width + 1, LANES:] = rows_of(block_ref[...]).astype(F32)
     msg_ref[width + 1 : width + 2, LANES:] = rows_of(coil_ref[...]).astype(F32)
-    refs = (sigma_ref, reluct_ref, curl_ref, pattern_ref, weight_ref, block_ref, coil_ref,
-            pat_ref, coil_hot_ref)
-    apply_local(refs, rhs_ref[...], halo, None, row_ref, msg_ref, centre_ref, rim_ref, scratch)
+    own = rhs_ref[...]
+    refs = (sigma_ref, reluct_ref, curl_ref, pattern_ref, weight_ref, block_ref, coil_hot_ref)
+    face_side(refs, own, halo, None, row_ref, picked_ref, face_ref)
+    backward(curl_ref, face_ref, back_ref, pat_ref, sigma_ref, own, centre_ref, rim_ref, msg_ref)
 
 
 def scalars(rows_ref, inv_ref, scal_ref):
-    coils = 84
     total = jnp.sum(rows_ref[...], axis=0, keepdims=True)
     current = total * inv_ref[0:1, :]
-    norm, energy = pick(total, coils), pick(total, coils + 1)
+    norm, energy = pick(total, COILS), pick(total, COILS + 1)
     energy = energy + jnp.sum(current * total, axis=1, keepdims=True)
     if scal_ref is None:
         beta = None
         curve = energy
     else:
         beta = norm / pick(scal_ref[0:1, :], 0)
-        cross = pick(total, coils + 2)
+        cross = pick(total, COILS + 2)
         curve = energy + 2.0 * beta * cross + beta * beta * pick(scal_ref[0:1, :], 1)
     lane = lane_iota()
     state = jnp.where(lane == 0, norm, jnp.where(lane == 1, curve, 0.0))
@@ -242,13 +294,13 @@
     return image + add_halves(nt_dot(split_rows(weighted(weight, current, coils)), blk))
 
 
-def step_kernel(count, first, *refs):
+def step_kernel(count, first, last, *refs):
     names = ["rows", "even", "odd"] + ([] if first else ["evenc", "oddc"])
     names += ["centre", "rim", "res", "halo"] + ([] if first else ["dir", "img", "imgh", "sol", "scal"])
-    names += ["inv", "blk", "sigma", "reluct", "curl", "pattern", "weight", "block", "coil", "pat",
-              "coilhot"]
-    names += ["row_o", "msg_o", "centre_o", "rim_o", "res_o", "halo_o", "dir_o", "img_o", "imgh_o",
-              "sol_o", "scal_o"]
+    names += ["inv", "blk", "sigma", "reluct", "curl", "pattern", "weight", "block", "coilhot", "pat",
+              "coil"]
+    names += ["row_o", "res_o", "dir_o", "img_o", "sol_o", "scal_o"]
+    names += ["msg_o", "centre_o"] + ([] if last else ["rim_o", "halo_o", "imgh_o"])
     r = dict(zip(names, refs))
     scratch = refs[len(names):]
     width = r["res"].shape[0]
@@ -288,20 +340,24 @@
         r["sol_o"][...] = r["sol"][...] + alpha * direction
     r["dir_o"][...] = direction
     r["img_o"][...] = image
-    r["imgh_o"][...] = image_halo
     own = old - alpha * image
     halo = r["halo"][...] - alpha * image_halo
     r["res_o"][...] = own
-    r["halo_o"][...] = halo
-    refs = tuple(r[k] for k in ("sigma", "reluct", "curl", "pattern", "weight", "block", "coil", "pat",
-                                "coilhot"))
-    apply_local(refs, own, halo, image, r["row_o"], r["msg_o"], r["centre_o"], r["rim_o"], scratch)
+    refs = tuple(r[k] for k in ("sigma", "reluct", "curl", "pattern", "weight", "block", "coilhot"))
+    picked_ref, face_ref, back_ref = scratch
+    face_side(refs, own, halo, image, r["row_o"], picked_ref, face_ref)
+    if not last:
+        r["imgh_o"][...] = image_halo
+        r["halo_o"][...] = halo
+        r["msg_o"][:, LANES:] = jnp.zeros_like(r["msg_o"][:, LANES:])
+    backward(r["curl"], face_ref, back_ref, r["pat"], r["sigma"], own, r["centre_o"], r.get("rim_o"),
+             r["msg_o"])
 
 
 def last_kernel(rows_ref, even_ref, odd_ref, centre_ref, res_ref, dir_ref, img_ref, sol_ref, scal_ref,
                 inv_ref, blk_ref, weight_ref, coil_ref, sol_out, res_out):
     current, alpha, beta, _ = scalars(rows_ref, inv_ref, scal_ref)
-    left, right = sides(even_ref[...], odd_ref[...])
+    left, right = sides(even_ref[:, 0:LANES], odd_ref[:, 0:LANES])
     image = own_image(left, right, centre_ref[...], weight_ref[...], current,
                       rows_of(coil_ref[...]), blk_ref[...])
     image = image + beta * img_ref[...]
@@ -309,17 +365,24 @@
     res_out[...] = res_ref[...] - alpha * image
 
 
-def call(kernel, args, outs, name, smem=(), scratch=()):
+def call(kernel, args, outs, name, hbm=(), scratch=(), cost=None):
+    args = [
+        pltpu.with_memory_space_constraint(x, pltpu.HBM) if i in hbm else x
+        for i, x in enumerate(args)
+    ]
+    if cost is not None:
+        cost = pl.CostEstimate(flops=cost, transcendentals=0, bytes_accessed=1 << 20)
     return pl.pallas_call(
         kernel,
         name=name,
         in_specs=[
-            pl.BlockSpec(memory_space=pltpu.SMEM if i in smem else VMEM) for i in range(len(args))
+            pl.BlockSpec(memory_space=pltpu.HBM if i in hbm else VMEM) for i in range(len(args))
         ],
         out_specs=[pl.BlockSpec(memory_space=VMEM)] * len(outs),
         out_shape=[jax.ShapeDtypeStruct(s, d) for s, d in outs],
         scratch_shapes=list(scratch),
-        compiler_params=pltpu.CompilerParams(vmem_limit_bytes=24 << 20),
+        cost_estimate=cost,
+        compiler_params=pltpu.CompilerParams(vmem_limit_bytes=8 << 20),
     )(*args)
 
 
@@ -344,25 +407,34 @@
     def gather_rows(rows):
         return lax.all_to_all(rows, "dom", 0, 0, tiled=True)
 
-    (rhs,) = call(
+    def like(x):
+        return (x.shape, x.dtype)
+
+    rhs, weight_v, block_v, coil_v = call(
         rhs_kernel,
         (right_side, cond_weight, block, coil, phase, ohm, switch_state),
-        [tile],
+        [tile, like(cond_weight), like(block), like(coil)],
         "rhs",
-        smem=(6,),
-        scratch=[VMEM((8, LANES), F32)],
+        hbm=range(7),
+        scratch=[VMEM((width, LANES), F32), VMEM(phase.shape, phase.dtype), VMEM(ohm.shape, F32),
+                 pltpu.SMEM(switch_state.shape, switch_state.dtype), VMEM((8, LANES), F32),
+                 pltpu.SemaphoreType.DMA((7,))],
+        cost=COST,
     )
     odd, even = exchange(rhs)
-    pat, blk, coil_hot, inv = call(
+    pat, blk, coil_hot, inv, pattern_v, sigma_v, reluct_v = call(
         table_kernel,
-        (pattern, block, coil, ohm),
+        (pattern, ohm, sigma, reluctivity, block_v, coil_v),
         [((2 * LANES, kinds * LANES), BF16), ((LANES, conductors), BF16),
-         ((LANES, conductors), BF16), ((8, LANES), F32)],
+         ((LANES, conductors), BF16), ((8, LANES), F32), like(pattern), tile, tile],
         "tables",
-    )
-    scratch = [VMEM((kinds, width, LANES), F32), VMEM((width, LANES), F32),
-               VMEM((2 * width, kinds * LANES), BF16)]
-    shared = (sigma, reluctivity, curl_blocks, pattern, cond_weight, block, coil, pat, coil_hot)
+        hbm=range(4),
+        scratch=[VMEM(ohm.shape, F32), pltpu.SemaphoreType.DMA((4,))],
+        cost=COST,
+    )
+    picked, faces = VMEM((kinds, width, LANES), F32), VMEM((width, LANES), F32)
+    back = VMEM((2 * width, kinds * LANES), BF16)
+    shared = (sigma_v, reluct_v, curl_blocks, pattern_v, weight_v, block_v, coil_hot, pat, coil_v)
     line = ((count, LANES), F32)
     wide = ((width + 8, LANES + conductors), F32)
     row, message, centre, rim, halo = call(
@@ -370,34 +442,31 @@
         (rhs, even, odd) + shared,
         [line, wide, tile, tile, tile],
         "apply0",
-        scratch=scratch,
+        scratch=[picked, faces, back],
     )
     odd_c, even_c = odd, even = exchange(message)
     rows = gather_rows(row)
-    state = [line, tile, tile, tile, tile, tile, tile, tile, tile, tile, ((8, LANES), F32)]
-    row, message, centre, rim, res, halo, direction, image, image_halo, sol, scal = call(
-        functools.partial(step_kernel, count, True),
-        (rows, even, odd, centre, rim, rhs, halo, inv, blk) + shared,
-        state,
-        "apply1",
-        scratch=scratch,
-    )
-    for turn in range(2, ITERS):
+    res, direction, image, image_halo, sol, scal = rhs, None, None, None, None, None
+    for turn in range(1, ITERS):
+        first, last = turn == 1, turn == ITERS - 1
+        args = (rows, even, odd) + (() if first else (even_c, odd_c)) + (centre, rim, res, halo)
+        args += () if first else (direction, image, image_halo, sol, scal)
+        state = [line, tile, tile, tile, tile, ((8, LANES), F32)]
+        state += [tile] * 2 if last else [((width, 3 * LANES), F32)] + [tile] * 4
+        row, res, direction, image, sol, scal, message, centre, *rest = call(
+            functools.partial(step_kernel, count, first, last),
+            args + (inv, blk) + shared,
+            state,
+            "apply%d" % turn,
+            scratch=[picked, faces, back],
+        )
+        if not last:
+            rim, halo, image_halo = rest
         odd, even = exchange(message)
         rows = gather_rows(row)
-        row, message, centre, rim, res, halo, direction, image, image_halo, sol, scal = call(
-            functools.partial(step_kernel, count, False),
-            (rows, even, odd, even_c, odd_c, centre, rim, res, halo, direction, image, image_halo,
-             sol, scal, inv, blk) + shared,
-            state,
-            "apply%d" % turn,
-            scratch=scratch,
-        )
-    odd, even = exchange(message)
-    rows = gather_rows(row)
     sol, res = call(
         last_kernel,
-        (rows, even, odd, centre, res, direction, image, sol, scal, inv, blk, cond_weight, coil),
+        (rows, even, odd, centre, res, direction, image, sol, scal, inv, blk, weight_v, coil_v),
         [tile, tile],
         "finish",
     )

time: 97.3 us -> 80.2 us (0.82)
  local copies, waits for them, and re-layouts: 17.9 us -> 0.77 us
  blocking collectives: 23.2 us -> 39.4 us
  starting transfers between devices: 29.1 us -> 19.5 us
  waiting for transfers between devices: 12.6 us -> 6.32 us
    unnamed x42 -> x6, local copies, waits for them, and re-layouts: 17.9 us -> 0.77 us
    all_to_all x1 -> x2, blocking collectives: 23.2 us -> 39.4 us  [gather_rows(): return lax.all_to_all(rows, 'dom', 0, 0, tiled=True)]
    all_to_all x2 -> x1, starting transfers between devices: 13.4 us -> 4.5 us  [gather_rows(): return lax.all_to_all(rows, 'dom', 0, 0, tiled=True)]
    all_to_all x2 -> x1, waiting for transfers between devices: 8.15 us -> 4.03 us  [gather_rows(): return lax.all_to_all(rows, 'dom', 0, 0, tiled=True)]
    ppermute x4, waiting for transfers between devices: 4.44 us -> 2.28 us  [exchange(): lax.ppermute(message, 'dom', outer)]
  transfers between devices with their start and end apart: 10 -> 9, of which waited for: 5 -> 3; matrix products, arithmetic and copies ran while one was open for 0% -> 0% of each run, Pallas kernels for 0% -> 1%
where the time goes in v2:
time: 80.2 us; the launch traced here: 79.9 us
  blocking collectives  39.4 us (49%)
  starting transfers between devices  19.5 us (24%)
  Pallas kernels  13.2 us (16%)
  waiting for transfers between devices  6.32 us (8%)
    all_to_all x2, blocking collectives, gather_rows(): return lax.all_to_all(rows, 'dom', 0, 0, tiled=True)  39.4 us
    ppermute x4, starting transfers between devices, exchange(): lax.ppermute(message, 'dom', outer)  14.7 us
    pallas_call x6, Pallas kernels, call(): pl.pallas_call(kernel, name=name, in_specs=[pl.BlockSpec(memory_space=plt...  13.2 us
    all_to_all x1, starting transfers between devices, gather_rows(): return lax.all_to_all(rows, 'dom', 0, 0, tiled=True)  4.5 us
    all_to_all x1, waiting for transfers between devices, gather_rows(): return lax.all_to_all(rows, 'dom', 0, 0, tiled=True)  4.03 us
    ppermute x4, waiting for transfers between devices, exchange(): lax.ppermute(message, 'dom', outer)  2.28 us
  transfers between devices with their start and end apart: 9, of which 3 were waited for; matrix products, arithmetic and copies ran while one was open for 0% of the time, Pallas kernels for 1%

profile of v2, /device:TPU:1, one launch (start us, length us, event | category | flops | bytes accessed | tf_op | source)
XLA Modules:
  0.0 79.9 jit_solution(15708420768117015410)
XLA Ops:
  0.6 0.0 slice-start
  0.6 0.0 slice-start.1
  0.7 1.4 %rhs.1 = (f32[64,128]{1,0:T(8,128)S(1)}, f32[64,512]{1,0:T(8,128)S(1)}, s32[4,128]{1,0:T(4,128)S(1)}, s32[4,128]{1,0:T(4,128)S(1)}) custom-call(f32[64,128]{1,0:T(8,128)} %side_hbm.1, f32[64,512]{1,0:T(8,128)} %weight_hbm.1, s32[4,128]{1,0:T(4,128)} %bitcast.23, s32[4,128]{1,0:T(4,128)} %bitcast.24, s32[1,84]{1,0:T(1,128)} %bitcast.25, f32[1,84]{1,0:T(1,128)} %bitcast.26, ...), custom_call_target="tpu_custom_call" | custom-call | flops 17179869184 | bytes 1048576 | tf_op jit(solution)/shard_map/rhs/pallas_call | solution.py:375
  2.1 4.8 %collective-permute-start.1 = (f32[64,128]{1,0:T(8,128)S(1)}, f32[64,128]{1,0:T(8,128)S(1)}, u32[]{:S(2)}, u32[]{:S(2)}) collective-permute-start(f32[64,128]{1,0:T(8,128)S(1)} %get-tuple-element.37.rhs_ref.refs_5_), channel_id=1, source_target_pairs={{1,2},{3,4},{5,6},{7,8},{9,10},{11,12},{13,14},{15,16},{17,18},{19... | collective-permute-start | bytes 98312 | tf_op jit(solution)/shard_map/ppermute | solution.py:405
  6.9 0.1 collective-permute-start
  7.0 0.0 slice-start.2
  7.0 1.1 %tables.1 = (bf16[256,768]{1,0:T(8,128)(2,1)S(1)}, bf16[128,512]{1,0:T(8,128)(2,1)S(1)}, bf16[128,512]{1,0:T(8,128)(2,1)S(1)}, f32[8,128]{1,0:T(8,128)S(1)}, s32...) custom-call(s32[6,128]{1,0:T(8,128)} %pattern_hbm.1, f32[1,84]{1,0:T(1,128)} %bitcast.27, ...), custom_call_target="tpu_custom_call" | custom-call | flops 17179869184 | bytes 1048576 | tf_op jit(solution)/shard_map/tables/pallas_call | solution.py:375
  8.1 0.4 collective-permute-done.1.odd_ref
  8.4 0.0 collective-permute-done.even_ref
  8.5 0.0 slice-done
  8.5 0.0 slice-done.1
  8.5 0.8 slice-done.2
  9.2 3.0 %apply0.1 = (f32[128,128]{1,0:T(8,128)S(1)}, f32[72,640]{1,0:T(8,128)S(1)}, f32[64,128]{1,0:T(8,128)S(1)}, f32[64,128]{1,0:T(8,128)S(1)}, f32[64,128]{1,0:T(8,128)S(1)}) custom-call(f32[64,128]{1,0:T(8,128)S(1)} %get-tuple-element.37.rhs_ref.refs_5_, f32[64,128]{1,0:T(8,128)S(1)} %collective-permute-done.even_ref, ...), custom_call_target="tpu_custom_call" | custom-call | tf_op jit(solution)/shard_map/apply0/pallas_call | solution.py:375
  12.3 3.5 %collective-permute-start.3 = (f32[72,640]{1,0:T(8,128)S(1)}, f32[72,640]{1,0:T(8,128)S(1)}, u32[]{:S(2)}, u32[]{:S(2)}) collective-permute-start(f32[72,640]{1,0:T(8,128)S(1)} %get-tuple-element.47), channel_id=1, source_target_pairs={{1,2},{3,4},{5,6},{7,8},{9,10},{11,12},{13,14},{15,16},{17,18},{19... | collective-permute-start | bytes 552968 | tf_op jit(solution)/shard_map/ppermute | solution.py:405
  15.8 0.1 collective-permute-start.2
  15.9 22.6 %all_to_all.33 = f32[128,1,128]{2,1,0:T(1,128)S(1)} all-to-all(f32[128,1,128]{2,1,0:T(1,128)S(1)} %bitcast.22), channel_id=1, replica_groups=mesh['dom'=128] {'dom'}, dimensions={0} | all-to-all | bytes 131072 | tf_op jit(solution)/shard_map/all_to_all | solution.py:408
  38.5 0.0 collective-permute-done.3.refs_2_.refs_4_
  38.5 0.0 collective-permute-done.2.refs_1_.refs_3_
  38.5 3.4 %apply1.1 = (f32[128,128]{1,0:T(8,128)S(1)}, f32[64,128]{1,0:T(8,128)S(1)}, f32[64,128]{1,0:T(8,128)S(1)}, f32[64,128]{1,0:T(8,128)S(1)}, f32[64,128]{1,0:T(8,12...) custom-call(f32[128,128]{1,0:T(8,128)S(1)} %bitcast.19, ...), custom_call_target="tpu_custom_call" | custom-call | tf_op jit(solution)/shard_map/apply1/pallas_call | solution.py:375
  41.9 2.8 %collective-permute-start.5 = (f32[64,384]{1,0:T(8,128)S(1)}, f32[64,384]{1,0:T(8,128)S(1)}, u32[]{:S(2)}, u32[]{:S(2)}) collective-permute-start(f32[64,384]{1,0:T(8,128)S(1)} %get-tuple-element.54), channel_id=1, source_target_pairs={{1,2},{3,4},{5,6},{7,8},{9,10},{11,12},{13,14},{15,16},{17,18},{19... | collective-permute-start | bytes 294920 | tf_op jit(solution)/shard_map/ppermute | solution.py:405
  44.7 0.1 collective-permute-start.4
  44.8 16.7 %all_to_all.34 = f32[128,1,128]{2,1,0:T(1,128)S(1)} all-to-all(f32[128,1,128]{2,1,0:T(1,128)S(1)} %bitcast.21), channel_id=1, replica_groups=mesh['dom'=128] {'dom'}, dimensions={0} | all-to-all | bytes 131072 | tf_op jit(solution)/shard_map/all_to_all | solution.py:408
  61.5 0.0 collective-permute-done.5.refs_2_
  61.6 0.0 collective-permute-done.4.refs_1_
  61.6 3.4 %apply2.1 = (f32[128,128]{1,0:T(8,128)}, f32[64,128]{1,0:T(8,128)S(1)}, f32[64,128]{1,0:T(8,128)S(1)}, f32[64,128]{1,0:T(8,128)S(1)}, f32[64,128]{1,0:T(8,128)S(...) custom-call(f32[128,128]{1,0:T(8,128)S(1)} %bitcast.18, ...), custom_call_target="tpu_custom_call" | custom-call | tf_op jit(solution)/shard_map/apply2/pallas_call | solution.py:375
  65.0 4.5 %all-to-all-start.2 = ((f32[128,1,128]{2,1,0:T(1,128)}), f32[128,1,128]{2,1,0:T(1,128)S(1)}, u32[]{:S(2)}, u32[]{:S(2)}) async-start(f32[128,1,128]{2,1,0:T(1,128)} %bitcast.11), calls=%async_computation.2 | async-start | bytes 131072 | tf_op jit(solution)/shard_map/all_to_all | solution.py:408
  69.5 3.5 %collective-permute-start.7 = (f32[64,128]{1,0:T(8,128)S(1)}, f32[64,128]{1,0:T(8,128)S(1)}, u32[]{:S(2)}, u32[]{:S(2)}) collective-permute-start(f32[64,128]{1,0:T(8,128)S(1)} %get-tuple-element.65), channel_id=1, source_target_pairs={{1,2},{3,4},{5,6},{7,8},{9,10},{11,12},{13,14},{15,16},{17,18},{19... | collective-permute-start | bytes 98312 | tf_op jit(solution)/shard_map/ppermute | solution.py:405
  73.0 0.1 collective-permute-start.6
  73.1 1.9 %collective-permute-done.7.odd_ref = f32[64,128]{1,0:T(8,128)S(1)} collective-permute-done((f32[64,128]{1,0:T(8,128)S(1)}, f32[64,128]{1,0:T(8,128)S(1)}, u32[]{:S(2)}, u32[]{:S(2)}) %collective-permute-start.7) | collective-permute-done | bytes 32800 | tf_op jit(solution)/shard_map/ppermute | solution.py:405
  75.0 0.0 collective-permute-done.6.even_ref
  75.0 4.0 %all-to-all-done.2 = f32[128,1,128]{2,1,0:T(1,128)S(1)} async-done(((f32[128,1,128]{2,1,0:T(1,128)}), f32[128,1,128]{2,1,0:T(1,128)S(1)}, u32[]{:S(2)}, u32[]{:S(2)}) %all-to-all-start.2) | async-done | bytes 65568 | tf_op jit(solution)/shard_map/all_to_all | solution.py:408
  79.0 0.9 %finish.1 = (f32[64,128]{1,0:T(8,128)}, f32[64,128]{1,0:T(8,128)}) custom-call(f32[128,128]{1,0:T(8,128)S(1)} %bitcast.20, f32[64,128]{1,0:T(8,128)S(1)} %collective-permute-done.6.even_ref, f32[64,128]{1,0:T(8,128)S(1)} %collective-permute-done.7.odd_ref, f32[64,128]{1,0:T(8,128)S(1)} %get-tuple-element.66.centre_ref, ...), custom_call_target="tpu_custom_call" | custom-call | tf_op jit(solution)/shard_map/finish/pallas_call | solution.py:375
  (1 shorter events, 0.0 us)
Async XLA Ops:
  0.6 7.8 %slice-start = ((s8[12582912]{0:T(1024)(128)(4,1)}), s8[4194304]{0:T(1024)(128)(4,1)S(1)}, s32[]{:S(2)}) async-start(s8[12582912]{0:T(1024)(128)(4,1)} %bitcast.16), calls=%async_computation.3 | async-start | bytes 8388608
  0.6 7.8 %slice-start.1 = ((s8[12582912]{0:T(1024)(128)(4,1)}), s8[4194304]{0:T(1024)(128)(4,1)S(1)}, s32[]{:S(2)}) async-start(s8[12582912]{0:T(1024)(128)(4,1)} %bitcast.16), calls=%async_computation.4 | async-start | bytes 8388608
  2.1 6.4 %collective-permute-start.1 = (f32[64,128]{1,0:T(8,128)S(1)}, f32[64,128]{1,0:T(8,128)S(1)}, u32[]{:S(2)}, u32[]{:S(2)}) collective-permute-start(f32[64,128]{1,0:T(8,128)S(1)} %get-tuple-element.37.rhs_ref.refs_5_), channel_id=1, source_target_pairs={{1,2},{3,4},{5,6},{7,8},{9,10},{11,12},{13,14},{15,16},{17,18},{19... | collective-permute-start | bytes 98312 | tf_op jit(solution)/shard_map/ppermute | solution.py:405
  6.9 1.6 %collective-permute-start = (f32[64,128]{1,0:T(8,128)S(1)}, f32[64,128]{1,0:T(8,128)S(1)}, u32[]{:S(2)}, u32[]{:S(2)}) collective-permute-start(f32[64,128]{1,0:T(8,128)S(1)} %get-tuple-element.37.rhs_ref.refs_5_), channel_id=1, source_target_pairs={{0,1},{1,0},{2,3},{3,2},{4,5},{5,4},{6,7},{7,6},{8,9},{9,8},{10,11... | collective-permute-start | bytes 98312 | tf_op jit(solution)/shard_map/ppermute | solution.py:405
  7.0 2.3 %slice-start.2 = ((s8[12582912]{0:T(1024)(128)(4,1)}), s8[4194304]{0:T(1024)(128)(4,1)S(1)}, s32[]{:S(2)}) async-start(s8[12582912]{0:T(1024)(128)(4,1)} %bitcast.16), calls=%async_computation.5 | async-start | bytes 8388608
  12.3 26.2 %collective-permute-start.3 = (f32[72,640]{1,0:T(8,128)S(1)}, f32[72,640]{1,0:T(8,128)S(1)}, u32[]{:S(2)}, u32[]{:S(2)}) collective-permute-start(f32[72,640]{1,0:T(8,128)S(1)} %get-tuple-element.47), channel_id=1, source_target_pairs={{1,2},{3,4},{5,6},{7,8},{9,10},{11,12},{13,14},{15,16},{17,18},{19... | collective-permute-start | bytes 552968 | tf_op jit(solution)/shard_map/ppermute | solution.py:405
  15.8 22.7 %collective-permute-start.2 = (f32[72,640]{1,0:T(8,128)S(1)}, f32[72,640]{1,0:T(8,128)S(1)}, u32[]{:S(2)}, u32[]{:S(2)}) collective-permute-start(f32[72,640]{1,0:T(8,128)S(1)} %get-tuple-element.47), channel_id=1, source_target_pairs={{0,1},{1,0},{2,3},{3,2},{4,5},{5,4},{6,7},{7,6},{8,9},{9,8},{10,11... | collective-permute-start | bytes 552968 | tf_op jit(solution)/shard_map/ppermute | solution.py:405
  41.9 19.7 %collective-permute-start.5 = (f32[64,384]{1,0:T(8,128)S(1)}, f32[64,384]{1,0:T(8,128)S(1)}, u32[]{:S(2)}, u32[]{:S(2)}) collective-permute-start(f32[64,384]{1,0:T(8,128)S(1)} %get-tuple-element.54), channel_id=1, source_target_pairs={{1,2},{3,4},{5,6},{7,8},{9,10},{11,12},{13,14},{15,16},{17,18},{19... | collective-permute-start | bytes 294920 | tf_op jit(solution)/shard_map/ppermute | solution.py:405
  44.7 16.8 %collective-permute-start.4 = (f32[64,384]{1,0:T(8,128)S(1)}, f32[64,384]{1,0:T(8,128)S(1)}, u32[]{:S(2)}, u32[]{:S(2)}) collective-permute-start(f32[64,384]{1,0:T(8,128)S(1)} %get-tuple-element.54), channel_id=1, source_target_pairs={{0,1},{1,0},{2,3},{3,2},{4,5},{5,4},{6,7},{7,6},{8,9},{9,8},{10,11... | collective-permute-start | bytes 294920 | tf_op jit(solution)/shard_map/ppermute | solution.py:405
  65.0 14.1 %all-to-all-start.2 = ((f32[128,1,128]{2,1,0:T(1,128)}), f32[128,1,128]{2,1,0:T(1,128)S(1)}, u32[]{:S(2)}, u32[]{:S(2)}) async-start(f32[128,1,128]{2,1,0:T(1,128)} %bitcast.11), calls=%async_computation.2 | async-start | bytes 131072 | tf_op jit(solution)/shard_map/all_to_all | solution.py:408
  69.5 5.5 %collective-permute-start.7 = (f32[64,128]{1,0:T(8,128)S(1)}, f32[64,128]{1,0:T(8,128)S(1)}, u32[]{:S(2)}, u32[]{:S(2)}) collective-permute-start(f32[64,128]{1,0:T(8,128)S(1)} %get-tuple-element.65), channel_id=1, source_target_pairs={{1,2},{3,4},{5,6},{7,8},{9,10},{11,12},{13,14},{15,16},{17,18},{19... | collective-permute-start | bytes 98312 | tf_op jit(solution)/shard_map/ppermute | solution.py:405
  73.0 2.0 %collective-permute-start.6 = (f32[64,128]{1,0:T(8,128)S(1)}, f32[64,128]{1,0:T(8,128)S(1)}, u32[]{:S(2)}, u32[]{:S(2)}) collective-permute-start(f32[64,128]{1,0:T(8,128)S(1)} %get-tuple-element.65), channel_id=1, source_target_pairs={{0,1},{1,0},{2,3},{3,2},{4,5},{5,4},{6,7},{7,6},{8,9},{9,8},{10,11... | collective-permute-start | bytes 98312 | tf_op jit(solution)/shard_map/ppermute | solution.py:405

commit v3 on v2

--- a/solution.py
+++ b/solution.py
@@ -175,8 +175,11 @@
         picked_ref[k] = jnp.where(inside, gather_lanes(own, idx), gather_lanes(halo, idx))
 
 
-def forward(curl_ref, picked_ref, face_ref):
+def forward(curl_ref, picked_ref, face_ref, own_ref, previous_ref, sigma_ref, weight_ref, block_ref,
+            sums_ref):
     kinds, rows, width, _ = curl_ref.shape
+    tiles = block_ref.shape[0]
+    sums_ref[...] = jnp.zeros_like(sums_ref)
 
     @pl.loop(0, rows // 8)
     def _(step):
@@ -187,17 +190,34 @@
                 term = curl_ref[k, pl.ds(first, 8), t : t + 8, :] * picked_ref[k, t : t + 8, :][None]
                 total = term if total is None else total + term
         face_ref[pl.ds(first, 8), :] = jnp.sum(total, axis=1)
+        own = own_ref[pl.ds(first, 8), :]
+        for i in range(tiles):
+            at = slice(i * LANES, (i + 1) * LANES)
+            idx = jnp.broadcast_to(block_ref[i : i + 1, :], (8, LANES))
+            sums_ref[i] += gather_lanes(own, idx) * weight_ref[pl.ds(first, 8), at]
+        square = own * own
+        sums_ref[tiles] += square
+        sums_ref[tiles + 1] += sigma_ref[pl.ds(first, 8), :] * square
+        if previous_ref is not None:
+            sums_ref[tiles + 2] += own * previous_ref[pl.ds(first, 8), :]
 
 
 def backward(curl_ref, bent_ref, back_ref, pat_ref, sigma_ref, own, centre_out, rim_out, msg_out):
     kinds, rows, width, _ = curl_ref.shape
 
-    @pl.loop(0, kinds)
-    def _(k):
-        total = curl_ref[k, 0] * bent_ref[0:1, :]
-        for a in range(1, rows):
-            total = total + curl_ref[k, a] * bent_ref[a : a + 1, :]
-        back_ref[:, pl.ds(pl.multiple_of(k * LANES, LANES), LANES)] = split_rows(total)
+    group = 3
+
+    @pl.loop(0, kinds // group)
+    def _(step):
+        totals = [None] * group
+        for a in range(rows):
+            row = bent_ref[a : a + 1, :]
+            for j in range(group):
+                term = curl_ref[step * group + j, a] * row
+                totals[j] = term if a == 0 else totals[j] + term
+        for j, total in enumerate(totals):
+            at = pl.multiple_of((step * group + j) * LANES, LANES)
+            back_ref[:, pl.ds(at, LANES)] = split_rows(total)
 
     spread = add_halves(nt_dot(back_ref[...], pat_ref[...]))
     rim = spread[:, LANES:]
@@ -212,40 +232,39 @@
     )
 
 
-def summed_row(own, previous, energy, weight_ref, block_ref, coil_hot_ref, row_out):
-    width = own.shape[0]
-    links = []
-    for i in range(block_ref.shape[0]):
-        idx = jnp.broadcast_to(block_ref[i : i + 1, :], (width, LANES))
-        got = gather_lanes(own, idx) * weight_ref[:, i * LANES : (i + 1) * LANES]
-        links.append(jnp.sum(got, axis=0, keepdims=True))
-    link = jnp.concatenate(links, axis=1)
+def total_of(x):
+    return jnp.sum(jnp.sum(x, axis=0, keepdims=True), axis=1, keepdims=True)
+
+
+def summed_row(sums_ref, energy, crossed, coil_hot_ref, row_out):
+    tiles = coil_hot_ref.shape[1] // LANES
+    link = jnp.concatenate(
+        [jnp.sum(sums_ref[i], axis=0, keepdims=True) for i in range(tiles)], axis=1
+    )
     high = link.astype(BF16).astype(F32)
     mid = (link - high).astype(BF16).astype(F32)
     low = link - high - mid
     sub = lax.broadcasted_iota(jnp.int32, (8, link.shape[1]), 0)
     terms = jnp.where(sub == 0, high, jnp.where(sub == 1, mid, jnp.where(sub == 2, low, 0.0)))
-    linkage = jnp.sum(nt_dot(terms.astype(BF16), coil_hot_ref[...]), axis=0, keepdims=True)
-
+    line = jnp.sum(nt_dot(terms.astype(BF16), coil_hot_ref[...]), axis=0, keepdims=True)
     lane = lane_iota()
-    norm = jnp.sum(jnp.sum(own * own, axis=0, keepdims=True), axis=1, keepdims=True)
-    energy = jnp.sum(energy, axis=1, keepdims=True)
-    line = linkage + jnp.where(lane == COILS, norm, 0.0) + jnp.where(lane == COILS + 1, energy, 0.0)
-    if previous is not None:
-        cross = jnp.sum(jnp.sum(own * previous, axis=0, keepdims=True), axis=1, keepdims=True)
-        line = line + jnp.where(lane == COILS + 2, cross, 0.0)
+    line = line + jnp.where(lane == COILS, total_of(sums_ref[tiles]), 0.0)
+    line = line + jnp.where(lane == COILS + 1, total_of(energy + sums_ref[tiles + 1]), 0.0)
+    if crossed:
+        line = line + jnp.where(lane == COILS + 2, total_of(sums_ref[tiles + 2]), 0.0)
     row_out[...] = jnp.broadcast_to(line, row_out.shape)
 
 
-def face_side(refs, own, halo, previous, row_out, picked_ref, face_ref):
+def face_side(refs, own_ref, halo, previous_ref, row_out, picked_ref, face_ref, sums_ref):
     sigma_ref, reluct_ref, curl_ref, pattern_ref, weight_ref, block_ref, coil_hot_ref = refs
-    pick_edges(pattern_ref, own, halo, picked_ref)
-    forward(curl_ref, picked_ref, face_ref)
+    pick_edges(pattern_ref, own_ref[...], halo, picked_ref)
+    forward(curl_ref, picked_ref, face_ref, own_ref, previous_ref, sigma_ref, weight_ref, block_ref,
+            sums_ref)
     face = face_ref[...]
     bent = reluct_ref[...] * face
     face_ref[...] = bent
-    energy = jnp.sum(bent * face + sigma_ref[...] * own * own, axis=0, keepdims=True)
-    summed_row(own, previous, energy, weight_ref, block_ref, coil_hot_ref, row_out)
+    energy = jnp.sum((bent * face).reshape(-1, 8, LANES), axis=0)
+    summed_row(sums_ref, energy, previous_ref is not None, coil_hot_ref, row_out)
 
 
 def pick(line, at):
@@ -255,7 +274,7 @@
 def first_kernel(count, rhs_ref, even_ref, odd_ref, sigma_ref, reluct_ref, curl_ref, pattern_ref,
                  weight_ref, block_ref, coil_hot_ref, pat_ref, coil_ref,
                  row_ref, msg_ref, centre_ref, rim_ref, halo_ref,
-                 picked_ref, face_ref, back_ref):
+                 picked_ref, face_ref, back_ref, sums_ref):
     left, right = sides(even_ref[...], odd_ref[...])
     halo = halo_of(left, right, count)
     halo_ref[...] = halo
@@ -266,7 +285,7 @@
     msg_ref[width + 1 : width + 2, LANES:] = rows_of(coil_ref[...]).astype(F32)
     own = rhs_ref[...]
     refs = (sigma_ref, reluct_ref, curl_ref, pattern_ref, weight_ref, block_ref, coil_hot_ref)
-    face_side(refs, own, halo, None, row_ref, picked_ref, face_ref)
+    face_side(refs, rhs_ref, halo, None, row_ref, picked_ref, face_ref, sums_ref)
     backward(curl_ref, face_ref, back_ref, pat_ref, sigma_ref, own, centre_ref, rim_ref, msg_ref)
 
 
@@ -344,8 +363,8 @@
     halo = r["halo"][...] - alpha * image_halo
     r["res_o"][...] = own
     refs = tuple(r[k] for k in ("sigma", "reluct", "curl", "pattern", "weight", "block", "coilhot"))
-    picked_ref, face_ref, back_ref = scratch
-    face_side(refs, own, halo, image, r["row_o"], picked_ref, face_ref)
+    picked_ref, face_ref, back_ref, sums_ref = scratch
+    face_side(refs, r["res_o"], halo, r["img_o"], r["row_o"], picked_ref, face_ref, sums_ref)
     if not last:
         r["imgh_o"][...] = image_halo
         r["halo_o"][...] = halo
@@ -434,6 +453,7 @@
     )
     picked, faces = VMEM((kinds, width, LANES), F32), VMEM((width, LANES), F32)
     back = VMEM((2 * width, kinds * LANES), BF16)
+    sums = VMEM((conductors // LANES + 3, 8, LANES), F32)
     shared = (sigma_v, reluct_v, curl_blocks, pattern_v, weight_v, block_v, coil_hot, pat, coil_v)
     line = ((count, LANES), F32)
     wide = ((width + 8, LANES + conductors), F32)
@@ -442,7 +462,7 @@
         (rhs, even, odd) + shared,
         [line, wide, tile, tile, tile],
         "apply0",
-        scratch=[picked, faces, back],
+        scratch=[picked, faces, back, sums],
     )
     odd_c, even_c = odd, even = exchange(message)
     rows = gather_rows(row)
@@ -458,7 +478,7 @@
             args + (inv, blk) + shared,
             state,
             "apply%d" % turn,
-            scratch=[picked, faces, back],
+            scratch=[picked, faces, back, sums],
         )
         if not last:
             rim, halo, image_halo = rest

time: 80.2 us -> 79.2 us (0.988)
  Pallas kernels: 13.2 us -> 12.3 us
    pallas_call x6, Pallas kernels: 13.2 us -> 12.3 us  [call(): pl.pallas_call(kernel, name=name, in_specs=[pl.BlockSpec(memory_space=plt...]
where the time goes in v3:
time: 79.2 us; the launch traced here: 79 us
  blocking collectives  39.4 us (50%)
  starting transfers between devices  19.5 us (25%)
  Pallas kernels  12.3 us (16%)
  waiting for transfers between devices  6.32 us (8%)
    all_to_all x2, blocking collectives, gather_rows(): return lax.all_to_all(rows, 'dom', 0, 0, tiled=True)  39.4 us
    ppermute x4, starting transfers between devices, exchange(): lax.ppermute(message, 'dom', outer)  14.6 us
    pallas_call x6, Pallas kernels, call(): pl.pallas_call(kernel, name=name, in_specs=[pl.BlockSpec(memory_space=plt...  12.3 us
    all_to_all x1, starting transfers between devices, gather_rows(): return lax.all_to_all(rows, 'dom', 0, 0, tiled=True)  4.51 us
    all_to_all x1, waiting for transfers between devices, gather_rows(): return lax.all_to_all(rows, 'dom', 0, 0, tiled=True)  4.03 us
    ppermute x4, waiting for transfers between devices, exchange(): lax.ppermute(message, 'dom', outer)  2.28 us
  transfers between devices with their start and end apart: 9, of which 3 were waited for; matrix products, arithmetic and copies ran while one was open for 0% of the time, Pallas kernels for 1%

profile of v3, /device:TPU:1, one launch (start us, length us, event | category | flops | bytes accessed | tf_op | source)
XLA Modules:
  0.0 79.0 jit_solution(4821338310418552651)
XLA Ops:
  0.6 0.0 slice-start
  0.6 0.0 slice-start.1
  0.7 1.4 %rhs.1 = (f32[64,128]{1,0:T(8,128)S(1)}, f32[64,512]{1,0:T(8,128)S(1)}, s32[4,128]{1,0:T(4,128)S(1)}, s32[4,128]{1,0:T(4,128)S(1)}) custom-call(f32[64,128]{1,0:T(8,128)} %side_hbm.1, f32[64,512]{1,0:T(8,128)} %weight_hbm.1, s32[4,128]{1,0:T(4,128)} %bitcast.23, s32[4,128]{1,0:T(4,128)} %bitcast.24, s32[1,84]{1,0:T(1,128)} %bitcast.25, f32[1,84]{1,0:T(1,128)} %bitcast.26, ...), custom_call_target="tpu_custom_call" | custom-call | flops 17179869184 | bytes 1048576 | tf_op jit(solution)/shard_map/rhs/pallas_call | solution.py:394
  2.1 4.8 %collective-permute-start.1 = (f32[64,128]{1,0:T(8,128)S(1)}, f32[64,128]{1,0:T(8,128)S(1)}, u32[]{:S(2)}, u32[]{:S(2)}) collective-permute-start(f32[64,128]{1,0:T(8,128)S(1)} %get-tuple-element.37.rhs_ref.refs_5_), channel_id=1, source_target_pairs={{1,2},{3,4},{5,6},{7,8},{9,10},{11,12},{13,14},{15,16},{17,18},{19... | collective-permute-start | bytes 98312 | tf_op jit(solution)/shard_map/ppermute | solution.py:424
  6.9 0.1 collective-permute-start
  7.0 0.0 slice-start.2
  7.0 1.1 %tables.1 = (bf16[256,768]{1,0:T(8,128)(2,1)S(1)}, bf16[128,512]{1,0:T(8,128)(2,1)S(1)}, bf16[128,512]{1,0:T(8,128)(2,1)S(1)}, f32[8,128]{1,0:T(8,128)S(1)}, s32...) custom-call(s32[6,128]{1,0:T(8,128)} %pattern_hbm.1, f32[1,84]{1,0:T(1,128)} %bitcast.27, ...), custom_call_target="tpu_custom_call" | custom-call | flops 17179869184 | bytes 1048576 | tf_op jit(solution)/shard_map/tables/pallas_call | solution.py:394
  8.1 0.4 collective-permute-done.1.odd_ref
  8.4 0.0 collective-permute-done.even_ref
  8.5 0.0 slice-done
  8.5 0.0 slice-done.1
  8.5 0.8 slice-done.2
  9.2 2.7 %apply0.1 = (f32[128,128]{1,0:T(8,128)S(1)}, f32[72,640]{1,0:T(8,128)S(1)}, f32[64,128]{1,0:T(8,128)S(1)}, f32[64,128]{1,0:T(8,128)S(1)}, f32[64,128]{1,0:T(8,128)S(1)}) custom-call(f32[64,128]{1,0:T(8,128)S(1)} %get-tuple-element.37.rhs_ref.refs_5_, f32[64,128]{1,0:T(8,128)S(1)} %collective-permute-done.even_ref, ...), custom_call_target="tpu_custom_call" | custom-call | tf_op jit(solution)/shard_map/apply0/pallas_call | solution.py:394
  12.0 3.5 %collective-permute-start.3 = (f32[72,640]{1,0:T(8,128)S(1)}, f32[72,640]{1,0:T(8,128)S(1)}, u32[]{:S(2)}, u32[]{:S(2)}) collective-permute-start(f32[72,640]{1,0:T(8,128)S(1)} %get-tuple-element.47), channel_id=1, source_target_pairs={{1,2},{3,4},{5,6},{7,8},{9,10},{11,12},{13,14},{15,16},{17,18},{19... | collective-permute-start | bytes 552968 | tf_op jit(solution)/shard_map/ppermute | solution.py:424
  15.5 0.1 collective-permute-start.2
  15.6 22.6 %all_to_all.33 = f32[128,1,128]{2,1,0:T(1,128)S(1)} all-to-all(f32[128,1,128]{2,1,0:T(1,128)S(1)} %bitcast.22), channel_id=1, replica_groups=mesh['dom'=128] {'dom'}, dimensions={0} | all-to-all | bytes 131072 | tf_op jit(solution)/shard_map/all_to_all | solution.py:427
  38.2 0.0 collective-permute-done.3.refs_2_.refs_4_
  38.2 0.0 collective-permute-done.2.refs_1_.refs_3_
  38.2 3.1 %apply1.1 = (f32[128,128]{1,0:T(8,128)S(1)}, f32[64,128]{1,0:T(8,128)S(1)}, f32[64,128]{1,0:T(8,128)S(1)}, f32[64,128]{1,0:T(8,128)S(1)}, f32[64,128]{1,0:T(8,12...) custom-call(f32[128,128]{1,0:T(8,128)S(1)} %bitcast.19, ...), custom_call_target="tpu_custom_call" | custom-call | tf_op jit(solution)/shard_map/apply1/pallas_call | solution.py:394
  41.3 2.8 %collective-permute-start.5 = (f32[64,384]{1,0:T(8,128)S(1)}, f32[64,384]{1,0:T(8,128)S(1)}, u32[]{:S(2)}, u32[]{:S(2)}) collective-permute-start(f32[64,384]{1,0:T(8,128)S(1)} %get-tuple-element.54), channel_id=1, source_target_pairs={{1,2},{3,4},{5,6},{7,8},{9,10},{11,12},{13,14},{15,16},{17,18},{19... | collective-permute-start | bytes 294920 | tf_op jit(solution)/shard_map/ppermute | solution.py:424
  44.1 0.1 collective-permute-start.4
  44.2 16.7 %all_to_all.34 = f32[128,1,128]{2,1,0:T(1,128)S(1)} all-to-all(f32[128,1,128]{2,1,0:T(1,128)S(1)} %bitcast.21), channel_id=1, replica_groups=mesh['dom'=128] {'dom'}, dimensions={0} | all-to-all | bytes 131072 | tf_op jit(solution)/shard_map/all_to_all | solution.py:427
  60.9 0.0 collective-permute-done.5.refs_2_
  61.0 0.0 collective-permute-done.4.refs_1_
  61.0 3.1 %apply2.1 = (f32[128,128]{1,0:T(8,128)}, f32[64,128]{1,0:T(8,128)S(1)}, f32[64,128]{1,0:T(8,128)S(1)}, f32[64,128]{1,0:T(8,128)S(1)}, f32[64,128]{1,0:T(8,128)S(...) custom-call(f32[128,128]{1,0:T(8,128)S(1)} %bitcast.18, ...), custom_call_target="tpu_custom_call" | custom-call | tf_op jit(solution)/shard_map/apply2/pallas_call | solution.py:394
  64.0 4.5 %all-to-all-start.2 = ((f32[128,1,128]{2,1,0:T(1,128)}), f32[128,1,128]{2,1,0:T(1,128)S(1)}, u32[]{:S(2)}, u32[]{:S(2)}) async-start(f32[128,1,128]{2,1,0:T(1,128)} %bitcast.11), calls=%async_computation.2 | async-start | bytes 131072 | tf_op jit(solution)/shard_map/all_to_all | solution.py:427
  68.5 3.5 %collective-permute-start.7 = (f32[64,128]{1,0:T(8,128)S(1)}, f32[64,128]{1,0:T(8,128)S(1)}, u32[]{:S(2)}, u32[]{:S(2)}) collective-permute-start(f32[64,128]{1,0:T(8,128)S(1)} %get-tuple-element.65), channel_id=1, source_target_pairs={{1,2},{3,4},{5,6},{7,8},{9,10},{11,12},{13,14},{15,16},{17,18},{19... | collective-permute-start | bytes 98312 | tf_op jit(solution)/shard_map/ppermute | solution.py:424
  72.1 0.1 collective-permute-start.6
  72.2 1.9 %collective-permute-done.7.odd_ref = f32[64,128]{1,0:T(8,128)S(1)} collective-permute-done((f32[64,128]{1,0:T(8,128)S(1)}, f32[64,128]{1,0:T(8,128)S(1)}, u32[]{:S(2)}, u32[]{:S(2)}) %collective-permute-start.7) | collective-permute-done | bytes 32800 | tf_op jit(solution)/shard_map/ppermute | solution.py:424
  74.1 0.0 collective-permute-done.6.even_ref
  74.1 4.0 %all-to-all-done.2 = f32[128,1,128]{2,1,0:T(1,128)S(1)} async-done(((f32[128,1,128]{2,1,0:T(1,128)}), f32[128,1,128]{2,1,0:T(1,128)S(1)}, u32[]{:S(2)}, u32[]{:S(2)}) %all-to-all-start.2) | async-done | bytes 65568 | tf_op jit(solution)/shard_map/all_to_all | solution.py:427
  78.1 0.9 %finish.1 = (f32[64,128]{1,0:T(8,128)}, f32[64,128]{1,0:T(8,128)}) custom-call(f32[128,128]{1,0:T(8,128)S(1)} %bitcast.20, f32[64,128]{1,0:T(8,128)S(1)} %collective-permute-done.6.even_ref, f32[64,128]{1,0:T(8,128)S(1)} %collective-permute-done.7.odd_ref, f32[64,128]{1,0:T(8,128)S(1)} %get-tuple-element.66.centre_ref, ...), custom_call_target="tpu_custom_call" | custom-call | tf_op jit(solution)/shard_map/finish/pallas_call | solution.py:394
  (1 shorter events, 0.0 us)
Async XLA Ops:
  0.6 7.8 %slice-start = ((s8[12582912]{0:T(1024)(128)(4,1)}), s8[4194304]{0:T(1024)(128)(4,1)S(1)}, s32[]{:S(2)}) async-start(s8[12582912]{0:T(1024)(128)(4,1)} %bitcast.16), calls=%async_computation.3 | async-start | bytes 8388608
  0.6 7.8 %slice-start.1 = ((s8[12582912]{0:T(1024)(128)(4,1)}), s8[4194304]{0:T(1024)(128)(4,1)S(1)}, s32[]{:S(2)}) async-start(s8[12582912]{0:T(1024)(128)(4,1)} %bitcast.16), calls=%async_computation.4 | async-start | bytes 8388608
  2.1 6.4 %collective-permute-start.1 = (f32[64,128]{1,0:T(8,128)S(1)}, f32[64,128]{1,0:T(8,128)S(1)}, u32[]{:S(2)}, u32[]{:S(2)}) collective-permute-start(f32[64,128]{1,0:T(8,128)S(1)} %get-tuple-element.37.rhs_ref.refs_5_), channel_id=1, source_target_pairs={{1,2},{3,4},{5,6},{7,8},{9,10},{11,12},{13,14},{15,16},{17,18},{19... | collective-permute-start | bytes 98312 | tf_op jit(solution)/shard_map/ppermute | solution.py:424
  6.9 1.6 %collective-permute-start = (f32[64,128]{1,0:T(8,128)S(1)}, f32[64,128]{1,0:T(8,128)S(1)}, u32[]{:S(2)}, u32[]{:S(2)}) collective-permute-start(f32[64,128]{1,0:T(8,128)S(1)} %get-tuple-element.37.rhs_ref.refs_5_), channel_id=1, source_target_pairs={{0,1},{1,0},{2,3},{3,2},{4,5},{5,4},{6,7},{7,6},{8,9},{9,8},{10,11... | collective-permute-start | bytes 98312 | tf_op jit(solution)/shard_map/ppermute | solution.py:424
  7.0 2.3 %slice-start.2 = ((s8[12582912]{0:T(1024)(128)(4,1)}), s8[4194304]{0:T(1024)(128)(4,1)S(1)}, s32[]{:S(2)}) async-start(s8[12582912]{0:T(1024)(128)(4,1)} %bitcast.16), calls=%async_computation.5 | async-start | bytes 8388608
  12.0 26.2 %collective-permute-start.3 = (f32[72,640]{1,0:T(8,128)S(1)}, f32[72,640]{1,0:T(8,128)S(1)}, u32[]{:S(2)}, u32[]{:S(2)}) collective-permute-start(f32[72,640]{1,0:T(8,128)S(1)} %get-tuple-element.47), channel_id=1, source_target_pairs={{1,2},{3,4},{5,6},{7,8},{9,10},{11,12},{13,14},{15,16},{17,18},{19... | collective-permute-start | bytes 552968 | tf_op jit(solution)/shard_map/ppermute | solution.py:424
  15.5 22.7 %collective-permute-start.2 = (f32[72,640]{1,0:T(8,128)S(1)}, f32[72,640]{1,0:T(8,128)S(1)}, u32[]{:S(2)}, u32[]{:S(2)}) collective-permute-start(f32[72,640]{1,0:T(8,128)S(1)} %get-tuple-element.47), channel_id=1, source_target_pairs={{0,1},{1,0},{2,3},{3,2},{4,5},{5,4},{6,7},{7,6},{8,9},{9,8},{10,11... | collective-permute-start | bytes 552968 | tf_op jit(solution)/shard_map/ppermute | solution.py:424
  41.3 19.7 %collective-permute-start.5 = (f32[64,384]{1,0:T(8,128)S(1)}, f32[64,384]{1,0:T(8,128)S(1)}, u32[]{:S(2)}, u32[]{:S(2)}) collective-permute-start(f32[64,384]{1,0:T(8,128)S(1)} %get-tuple-element.54), channel_id=1, source_target_pairs={{1,2},{3,4},{5,6},{7,8},{9,10},{11,12},{13,14},{15,16},{17,18},{19... | collective-permute-start | bytes 294920 | tf_op jit(solution)/shard_map/ppermute | solution.py:424
  44.1 16.8 %collective-permute-start.4 = (f32[64,384]{1,0:T(8,128)S(1)}, f32[64,384]{1,0:T(8,128)S(1)}, u32[]{:S(2)}, u32[]{:S(2)}) collective-permute-start(f32[64,384]{1,0:T(8,128)S(1)} %get-tuple-element.54), channel_id=1, source_target_pairs={{0,1},{1,0},{2,3},{3,2},{4,5},{5,4},{6,7},{7,6},{8,9},{9,8},{10,11... | collective-permute-start | bytes 294920 | tf_op jit(solution)/shard_map/ppermute | solution.py:424
  64.0 14.1 %all-to-all-start.2 = ((f32[128,1,128]{2,1,0:T(1,128)}), f32[128,1,128]{2,1,0:T(1,128)S(1)}, u32[]{:S(2)}, u32[]{:S(2)}) async-start(f32[128,1,128]{2,1,0:T(1,128)} %bitcast.11), calls=%async_computation.2 | async-start | bytes 131072 | tf_op jit(solution)/shard_map/all_to_all | solution.py:427
  68.5 5.5 %collective-permute-start.7 = (f32[64,128]{1,0:T(8,128)S(1)}, f32[64,128]{1,0:T(8,128)S(1)}, u32[]{:S(2)}, u32[]{:S(2)}) collective-permute-start(f32[64,128]{1,0:T(8,128)S(1)} %get-tuple-element.65), channel_id=1, source_target_pairs={{1,2},{3,4},{5,6},{7,8},{9,10},{11,12},{13,14},{15,16},{17,18},{19... | collective-permute-start | bytes 98312 | tf_op jit(solution)/shard_map/ppermute | solution.py:424
  72.1 2.0 %collective-permute-start.6 = (f32[64,128]{1,0:T(8,128)S(1)}, f32[64,128]{1,0:T(8,128)S(1)}, u32[]{:S(2)}, u32[]{:S(2)}) collective-permute-start(f32[64,128]{1,0:T(8,128)S(1)} %get-tuple-element.65), channel_id=1, source_target_pairs={{0,1},{1,0},{2,3},{3,2},{4,5},{5,4},{6,7},{7,6},{8,9},{9,8},{10,11... | collective-permute-start | bytes 98312 | tf_op jit(solution)/shard_map/ppermute | solution.py:424

commit v4 on v3

--- a/solution.py
+++ b/solution.py
@@ -271,7 +271,7 @@
     return jnp.sum(jnp.where(lane_iota() == at, line, 0.0), axis=1, keepdims=True)
 
 
-def first_kernel(count, rhs_ref, even_ref, odd_ref, sigma_ref, reluct_ref, curl_ref, pattern_ref,
+def first_kernel(count, rhs_ref, odd_ref, even_ref, sigma_ref, reluct_ref, curl_ref, pattern_ref,
                  weight_ref, block_ref, coil_hot_ref, pat_ref, coil_ref,
                  row_ref, msg_ref, centre_ref, rim_ref, halo_ref,
                  picked_ref, face_ref, back_ref, sums_ref):
@@ -314,7 +314,7 @@
 
 
 def step_kernel(count, first, last, *refs):
-    names = ["rows", "even", "odd"] + ([] if first else ["evenc", "oddc"])
+    names = ["rows", "odd", "even"] + ([] if first else ["oddc", "evenc"])
     names += ["centre", "rim", "res", "halo"] + ([] if first else ["dir", "img", "imgh", "sol", "scal"])
     names += ["inv", "blk", "sigma", "reluct", "curl", "pattern", "weight", "block", "coilhot", "pat",
               "coil"]
@@ -373,7 +373,7 @@
              r["msg_o"])
 
 
-def last_kernel(rows_ref, even_ref, odd_ref, centre_ref, res_ref, dir_ref, img_ref, sol_ref, scal_ref,
+def last_kernel(rows_ref, odd_ref, even_ref, centre_ref, res_ref, dir_ref, img_ref, sol_ref, scal_ref,
                 inv_ref, blk_ref, weight_ref, coil_ref, sol_out, res_out):
     current, alpha, beta, _ = scalars(rows_ref, inv_ref, scal_ref)
     left, right = sides(even_ref[:, 0:LANES], odd_ref[:, 0:LANES])
@@ -421,7 +421,8 @@
     outer = outer + [(b, a) for a, b in outer]
 
     def exchange(message):
-        return lax.ppermute(message, "dom", outer), lax.ppermute(message, "dom", inner)
+        near = lax.ppermute(message, "dom", inner)
+        return lax.ppermute(message, "dom", outer), near
 
     def gather_rows(rows):
         return lax.all_to_all(rows, "dom", 0, 0, tiled=True)
@@ -459,7 +460,7 @@
     wide = ((width + 8, LANES + conductors), F32)
     row, message, centre, rim, halo = call(
         functools.partial(first_kernel, count),
-        (rhs, even, odd) + shared,
+        (rhs, odd, even) + shared,
         [line, wide, tile, tile, tile],
         "apply0",
         scratch=[picked, faces, back, sums],
@@ -469,7 +470,7 @@
     res, direction, image, image_halo, sol, scal = rhs, None, None, None, None, None
     for turn in range(1, ITERS):
         first, last = turn == 1, turn == ITERS - 1
-        args = (rows, even, odd) + (() if first else (even_c, odd_c)) + (centre, rim, res, halo)
+        args = (rows, odd, even) + (() if first else (odd_c, even_c)) + (centre, rim, res, halo)
         args += () if first else (direction, image, image_halo, sol, scal)
         state = [line, tile, tile, tile, tile, ((8, LANES), F32)]
         state += [tile] * 2 if last else [((width, 3 * LANES), F32)] + [tile] * 4
@@ -486,7 +487,7 @@
         rows = gather_rows(row)
     sol, res = call(
         last_kernel,
-        (rows, even, odd, centre, res, direction, image, sol, scal, inv, blk, weight_v, coil_v),
+        (rows, odd, even, centre, res, direction, image, sol, scal, inv, blk, weight_v, coil_v),
         [tile, tile],
         "finish",
     )

time: 79.2 us -> 79.2 us (level)
    ppermute x8, waiting for transfers between devices: 2.29 us -> 3.64 us  [the longest x4 3.63 us: exchange(): return (lax.ppermute(message, 'dom', outer), near)]
    all_to_all x1, waiting for transfers between devices: 4.03 us -> 2.9 us  [gather_rows(): return lax.all_to_all(rows, 'dom', 0, 0, tiled=True)]
where the time goes in v4:
time: 79.2 us; the launch traced here: 78.9 us
  blocking collectives  39.3 us (50%)
  starting transfers between devices  19.6 us (25%)
  Pallas kernels  12.3 us (16%)
  waiting for transfers between devices  6.54 us (8%)
    all_to_all x2, blocking collectives, gather_rows(): return lax.all_to_all(rows, 'dom', 0, 0, tiled=True)  39.3 us
    pallas_call x6, Pallas kernels, call(): pl.pallas_call(kernel, name=name, in_specs=[pl.BlockSpec(memory_space=plt...  12.3 us
    ppermute x4, starting transfers between devices, exchange(): return (lax.ppermute(message, 'dom', outer), near)  11.6 us
    all_to_all x1, starting transfers between devices, gather_rows(): return lax.all_to_all(rows, 'dom', 0, 0, tiled=True)  4.5 us
    ppermute x4, waiting for transfers between devices, exchange(): return (lax.ppermute(message, 'dom', outer), near)  3.63 us
    ppermute x4, starting transfers between devices, exchange(): near = lax.ppermute(message, 'dom', inner)  3.57 us
    all_to_all x1, waiting for transfers between devices, gather_rows(): return lax.all_to_all(rows, 'dom', 0, 0, tiled=True)  2.9 us
  transfers between devices with their start and end apart: 9, of which 3 were waited for; matrix products, arithmetic and copies ran while one was open for 0% of the time, Pallas kernels for 1%

profile of v4, /device:TPU:1, one launch (start us, length us, event | category | flops | bytes accessed | tf_op | source)
XLA Modules:
  0.0 78.9 jit_solution(12246243144232928368)
XLA Ops:
  0.6 0.0 slice-start
  0.6 0.0 slice-start.1
  0.7 1.4 %rhs.1 = (f32[64,128]{1,0:T(8,128)S(1)}, f32[64,512]{1,0:T(8,128)S(1)}, s32[4,128]{1,0:T(4,128)S(1)}, s32[4,128]{1,0:T(4,128)S(1)}) custom-call(f32[64,128]{1,0:T(8,128)} %side_hbm.1, f32[64,512]{1,0:T(8,128)} %weight_hbm.1, s32[4,128]{1,0:T(4,128)} %bitcast.23, s32[4,128]{1,0:T(4,128)} %bitcast.24, s32[1,84]{1,0:T(1,128)} %bitcast.25, f32[1,84]{1,0:T(1,128)} %bitcast.26, ...), custom_call_target="tpu_custom_call" | custom-call | flops 17179869184 | bytes 1048576 | tf_op jit(solution)/shard_map/rhs/pallas_call | solution.py:394
  2.1 1.5 %collective-permute-start.1 = (f32[64,128]{1,0:T(8,128)S(1)}, f32[64,128]{1,0:T(8,128)S(1)}, u32[]{:S(2)}, u32[]{:S(2)}) collective-permute-start(f32[64,128]{1,0:T(8,128)S(1)} %get-tuple-element.37.rhs_ref.refs_5_), channel_id=1, source_target_pairs={{0,1},{1,0},{2,3},{3,2},{4,5},{5,4},{6,7},{7,6},{8,9},{9,8},{10,11... | collective-permute-start | bytes 98312 | tf_op jit(solution)/shard_map/ppermute | solution.py:424
  3.6 3.4 %collective-permute-start = (f32[64,128]{1,0:T(8,128)S(1)}, f32[64,128]{1,0:T(8,128)S(1)}, u32[]{:S(2)}, u32[]{:S(2)}) collective-permute-start(f32[64,128]{1,0:T(8,128)S(1)} %get-tuple-element.37.rhs_ref.refs_5_), channel_id=1, source_target_pairs={{1,2},{3,4},{5,6},{7,8},{9,10},{11,12},{13,14},{15,16},{17,18},{19... | collective-permute-start | bytes 98312 | tf_op jit(solution)/shard_map/ppermute | solution.py:425
  7.0 0.0 slice-start.2
  7.0 1.1 %tables.1 = (bf16[256,768]{1,0:T(8,128)(2,1)S(1)}, bf16[128,512]{1,0:T(8,128)(2,1)S(1)}, bf16[128,512]{1,0:T(8,128)(2,1)S(1)}, f32[8,128]{1,0:T(8,128)S(1)}, s32...) custom-call(s32[6,128]{1,0:T(8,128)} %pattern_hbm.1, f32[1,84]{1,0:T(1,128)} %bitcast.27, ...), custom_call_target="tpu_custom_call" | custom-call | flops 17179869184 | bytes 1048576 | tf_op jit(solution)/shard_map/tables/pallas_call | solution.py:394
  8.1 0.0 collective-permute-done.1.even_ref
  8.1 0.7 collective-permute-done.odd_ref
  8.8 0.0 slice-done
  8.8 0.0 slice-done.1
  8.8 0.4 slice-done.2
  9.2 2.7 %apply0.1 = (f32[128,128]{1,0:T(8,128)S(1)}, f32[72,640]{1,0:T(8,128)S(1)}, f32[64,128]{1,0:T(8,128)S(1)}, f32[64,128]{1,0:T(8,128)S(1)}, f32[64,128]{1,0:T(8,128)S(1)}) custom-call(f32[64,128]{1,0:T(8,128)S(1)} %get-tuple-element.37.rhs_ref.refs_5_, f32[64,128]{1,0:T(8,128)S(1)} %collective-permute-done.odd_ref, ...), custom_call_target="tpu_custom_call" | custom-call | tf_op jit(solution)/shard_map/apply0/pallas_call | solution.py:394
  12.0 0.1 collective-permute-start.3
  12.0 3.5 %collective-permute-start.2 = (f32[72,640]{1,0:T(8,128)S(1)}, f32[72,640]{1,0:T(8,128)S(1)}, u32[]{:S(2)}, u32[]{:S(2)}) collective-permute-start(f32[72,640]{1,0:T(8,128)S(1)} %get-tuple-element.47), channel_id=1, source_target_pairs={{1,2},{3,4},{5,6},{7,8},{9,10},{11,12},{13,14},{15,16},{17,18},{19... | collective-permute-start | bytes 552968 | tf_op jit(solution)/shard_map/ppermute | solution.py:425
  15.5 22.9 %all_to_all.33 = f32[128,1,128]{2,1,0:T(1,128)S(1)} all-to-all(f32[128,1,128]{2,1,0:T(1,128)S(1)} %bitcast.22), channel_id=1, replica_groups=mesh['dom'=128] {'dom'}, dimensions={0} | all-to-all | bytes 131072 | tf_op jit(solution)/shard_map/all_to_all | solution.py:428
  38.5 0.0 collective-permute-done.3.refs_2_.refs_4_
  38.5 0.0 collective-permute-done.2.refs_1_.refs_3_
  38.5 3.1 %apply1.1 = (f32[128,128]{1,0:T(8,128)S(1)}, f32[64,128]{1,0:T(8,128)S(1)}, f32[64,128]{1,0:T(8,128)S(1)}, f32[64,128]{1,0:T(8,128)S(1)}, f32[64,128]{1,0:T(8,12...) custom-call(f32[128,128]{1,0:T(8,128)S(1)} %bitcast.19, ...), custom_call_target="tpu_custom_call" | custom-call | tf_op jit(solution)/shard_map/apply1/pallas_call | solution.py:394
  41.6 0.8 %collective-permute-start.5 = (f32[64,384]{1,0:T(8,128)S(1)}, f32[64,384]{1,0:T(8,128)S(1)}, u32[]{:S(2)}, u32[]{:S(2)}) collective-permute-start(f32[64,384]{1,0:T(8,128)S(1)} %get-tuple-element.54), channel_id=1, source_target_pairs={{0,1},{1,0},{2,3},{3,2},{4,5},{5,4},{6,7},{7,6},{8,9},{9,8},{10,11... | collective-permute-start | bytes 294920 | tf_op jit(solution)/shard_map/ppermute | solution.py:424
  42.4 2.1 %collective-permute-start.4 = (f32[64,384]{1,0:T(8,128)S(1)}, f32[64,384]{1,0:T(8,128)S(1)}, u32[]{:S(2)}, u32[]{:S(2)}) collective-permute-start(f32[64,384]{1,0:T(8,128)S(1)} %get-tuple-element.54), channel_id=1, source_target_pairs={{1,2},{3,4},{5,6},{7,8},{9,10},{11,12},{13,14},{15,16},{17,18},{19... | collective-permute-start | bytes 294920 | tf_op jit(solution)/shard_map/ppermute | solution.py:425
  44.5 16.4 %all_to_all.34 = f32[128,1,128]{2,1,0:T(1,128)S(1)} all-to-all(f32[128,1,128]{2,1,0:T(1,128)S(1)} %bitcast.21), channel_id=1, replica_groups=mesh['dom'=128] {'dom'}, dimensions={0} | all-to-all | bytes 131072 | tf_op jit(solution)/shard_map/all_to_all | solution.py:428
  60.9 0.0 collective-permute-done.5.refs_2_
  60.9 0.0 collective-permute-done.4.refs_1_
  60.9 3.1 %apply2.1 = (f32[128,128]{1,0:T(8,128)}, f32[64,128]{1,0:T(8,128)S(1)}, f32[64,128]{1,0:T(8,128)S(1)}, f32[64,128]{1,0:T(8,128)S(1)}, f32[64,128]{1,0:T(8,128)S(...) custom-call(f32[128,128]{1,0:T(8,128)S(1)} %bitcast.18, ...), custom_call_target="tpu_custom_call" | custom-call | tf_op jit(solution)/shard_map/apply2/pallas_call | solution.py:394
  64.0 4.5 %all-to-all-start.2 = ((f32[128,1,128]{2,1,0:T(1,128)}), f32[128,1,128]{2,1,0:T(1,128)S(1)}, u32[]{:S(2)}, u32[]{:S(2)}) async-start(f32[128,1,128]{2,1,0:T(1,128)} %bitcast.11), calls=%async_computation.2 | async-start | bytes 131072 | tf_op jit(solution)/shard_map/all_to_all | solution.py:428
  68.5 1.1 %collective-permute-start.7 = (f32[64,128]{1,0:T(8,128)S(1)}, f32[64,128]{1,0:T(8,128)S(1)}, u32[]{:S(2)}, u32[]{:S(2)}) collective-permute-start(f32[64,128]{1,0:T(8,128)S(1)} %get-tuple-element.65), channel_id=1, source_target_pairs={{0,1},{1,0},{2,3},{3,2},{4,5},{5,4},{6,7},{7,6},{8,9},{9,8},{10,11... | collective-permute-start | bytes 98312 | tf_op jit(solution)/shard_map/ppermute | solution.py:424
  69.6 2.6 %collective-permute-start.6 = (f32[64,128]{1,0:T(8,128)S(1)}, f32[64,128]{1,0:T(8,128)S(1)}, u32[]{:S(2)}, u32[]{:S(2)}) collective-permute-start(f32[64,128]{1,0:T(8,128)S(1)} %get-tuple-element.65), channel_id=1, source_target_pairs={{1,2},{3,4},{5,6},{7,8},{9,10},{11,12},{13,14},{15,16},{17,18},{19... | collective-permute-start | bytes 98312 | tf_op jit(solution)/shard_map/ppermute | solution.py:425
  72.2 0.0 collective-permute-done.7.even_ref
  72.2 2.9 %collective-permute-done.6.odd_ref = f32[64,128]{1,0:T(8,128)S(1)} collective-permute-done((f32[64,128]{1,0:T(8,128)S(1)}, f32[64,128]{1,0:T(8,128)S(1)}, u32[]{:S(2)}, u32[]{:S(2)}) %collective-permute-start.6) | collective-permute-done | bytes 32800 | tf_op jit(solution)/shard_map/ppermute | solution.py:425
  75.1 2.9 %all-to-all-done.2 = f32[128,1,128]{2,1,0:T(1,128)S(1)} async-done(((f32[128,1,128]{2,1,0:T(1,128)}), f32[128,1,128]{2,1,0:T(1,128)S(1)}, u32[]{:S(2)}, u32[]{:S(2)}) %all-to-all-start.2) | async-done | bytes 65568 | tf_op jit(solution)/shard_map/all_to_all | solution.py:428
  78.0 0.9 %finish.1 = (f32[64,128]{1,0:T(8,128)}, f32[64,128]{1,0:T(8,128)}) custom-call(f32[128,128]{1,0:T(8,128)S(1)} %bitcast.20, f32[64,128]{1,0:T(8,128)S(1)} %collective-permute-done.6.odd_ref, f32[64,128]{1,0:T(8,128)S(1)} %collective-permute-done.7.even_ref, f32[64,128]{1,0:T(8,128)S(1)} %get-tuple-element.66.centre_ref, ...), custom_call_target="tpu_custom_call" | custom-call | tf_op jit(solution)/shard_map/finish/pallas_call | solution.py:394
  (1 shorter events, 0.0 us)
Async XLA Ops:
  0.6 8.2 %slice-start = ((s8[12582912]{0:T(1024)(128)(4,1)}), s8[4194304]{0:T(1024)(128)(4,1)S(1)}, s32[]{:S(2)}) async-start(s8[12582912]{0:T(1024)(128)(4,1)} %bitcast.16), calls=%async_computation.3 | async-start | bytes 8388608
  0.6 8.2 %slice-start.1 = ((s8[12582912]{0:T(1024)(128)(4,1)}), s8[4194304]{0:T(1024)(128)(4,1)S(1)}, s32[]{:S(2)}) async-start(s8[12582912]{0:T(1024)(128)(4,1)} %bitcast.16), calls=%async_computation.4 | async-start | bytes 8388608
  2.1 6.0 %collective-permute-start.1 = (f32[64,128]{1,0:T(8,128)S(1)}, f32[64,128]{1,0:T(8,128)S(1)}, u32[]{:S(2)}, u32[]{:S(2)}) collective-permute-start(f32[64,128]{1,0:T(8,128)S(1)} %get-tuple-element.37.rhs_ref.refs_5_), channel_id=1, source_target_pairs={{0,1},{1,0},{2,3},{3,2},{4,5},{5,4},{6,7},{7,6},{8,9},{9,8},{10,11... | collective-permute-start | bytes 98312 | tf_op jit(solution)/shard_map/ppermute | solution.py:424
  3.6 5.2 %collective-permute-start = (f32[64,128]{1,0:T(8,128)S(1)}, f32[64,128]{1,0:T(8,128)S(1)}, u32[]{:S(2)}, u32[]{:S(2)}) collective-permute-start(f32[64,128]{1,0:T(8,128)S(1)} %get-tuple-element.37.rhs_ref.refs_5_), channel_id=1, source_target_pairs={{1,2},{3,4},{5,6},{7,8},{9,10},{11,12},{13,14},{15,16},{17,18},{19... | collective-permute-start | bytes 98312 | tf_op jit(solution)/shard_map/ppermute | solution.py:425
  7.0 2.3 %slice-start.2 = ((s8[12582912]{0:T(1024)(128)(4,1)}), s8[4194304]{0:T(1024)(128)(4,1)S(1)}, s32[]{:S(2)}) async-start(s8[12582912]{0:T(1024)(128)(4,1)} %bitcast.16), calls=%async_computation.5 | async-start | bytes 8388608
  12.0 26.5 %collective-permute-start.3 = (f32[72,640]{1,0:T(8,128)S(1)}, f32[72,640]{1,0:T(8,128)S(1)}, u32[]{:S(2)}, u32[]{:S(2)}) collective-permute-start(f32[72,640]{1,0:T(8,128)S(1)} %get-tuple-element.47), channel_id=1, source_target_pairs={{0,1},{1,0},{2,3},{3,2},{4,5},{5,4},{6,7},{7,6},{8,9},{9,8},{10,11... | collective-permute-start | bytes 552968 | tf_op jit(solution)/shard_map/ppermute | solution.py:424
  12.0 26.4 %collective-permute-start.2 = (f32[72,640]{1,0:T(8,128)S(1)}, f32[72,640]{1,0:T(8,128)S(1)}, u32[]{:S(2)}, u32[]{:S(2)}) collective-permute-start(f32[72,640]{1,0:T(8,128)S(1)} %get-tuple-element.47), channel_id=1, source_target_pairs={{1,2},{3,4},{5,6},{7,8},{9,10},{11,12},{13,14},{15,16},{17,18},{19... | collective-permute-start | bytes 552968 | tf_op jit(solution)/shard_map/ppermute | solution.py:425
  41.6 19.3 %collective-permute-start.5 = (f32[64,384]{1,0:T(8,128)S(1)}, f32[64,384]{1,0:T(8,128)S(1)}, u32[]{:S(2)}, u32[]{:S(2)}) collective-permute-start(f32[64,384]{1,0:T(8,128)S(1)} %get-tuple-element.54), channel_id=1, source_target_pairs={{0,1},{1,0},{2,3},{3,2},{4,5},{5,4},{6,7},{7,6},{8,9},{9,8},{10,11... | collective-permute-start | bytes 294920 | tf_op jit(solution)/shard_map/ppermute | solution.py:424
  42.4 18.5 %collective-permute-start.4 = (f32[64,384]{1,0:T(8,128)S(1)}, f32[64,384]{1,0:T(8,128)S(1)}, u32[]{:S(2)}, u32[]{:S(2)}) collective-permute-start(f32[64,384]{1,0:T(8,128)S(1)} %get-tuple-element.54), channel_id=1, source_target_pairs={{1,2},{3,4},{5,6},{7,8},{9,10},{11,12},{13,14},{15,16},{17,18},{19... | collective-permute-start | bytes 294920 | tf_op jit(solution)/shard_map/ppermute | solution.py:425
  64.0 14.1 %all-to-all-start.2 = ((f32[128,1,128]{2,1,0:T(1,128)}), f32[128,1,128]{2,1,0:T(1,128)S(1)}, u32[]{:S(2)}, u32[]{:S(2)}) async-start(f32[128,1,128]{2,1,0:T(1,128)} %bitcast.11), calls=%async_computation.2 | async-start | bytes 131072 | tf_op jit(solution)/shard_map/all_to_all | solution.py:428
  68.5 3.8 %collective-permute-start.7 = (f32[64,128]{1,0:T(8,128)S(1)}, f32[64,128]{1,0:T(8,128)S(1)}, u32[]{:S(2)}, u32[]{:S(2)}) collective-permute-start(f32[64,128]{1,0:T(8,128)S(1)} %get-tuple-element.65), channel_id=1, source_target_pairs={{0,1},{1,0},{2,3},{3,2},{4,5},{5,4},{6,7},{7,6},{8,9},{9,8},{10,11... | collective-permute-start | bytes 98312 | tf_op jit(solution)/shard_map/ppermute | solution.py:424
  69.6 5.5 %collective-permute-start.6 = (f32[64,128]{1,0:T(8,128)S(1)}, f32[64,128]{1,0:T(8,128)S(1)}, u32[]{:S(2)}, u32[]{:S(2)}) collective-permute-start(f32[64,128]{1,0:T(8,128)S(1)} %get-tuple-element.65), channel_id=1, source_target_pairs={{1,2},{3,4},{5,6},{7,8},{9,10},{11,12},{13,14},{15,16},{17,18},{19... | collective-permute-start | bytes 98312 | tf_op jit(solution)/shard_map/ppermute | solution.py:425

commit v5 on v4

--- a/solution.py
+++ b/solution.py
@@ -202,24 +202,22 @@
             sums_ref[tiles + 2] += own * previous_ref[pl.ds(first, 8), :]
 
 
-def backward(curl_ref, bent_ref, back_ref, pat_ref, sigma_ref, own, centre_out, rim_out, msg_out):
+def backward(curl_ref, bent_ref, pat_ref, sigma_ref, own, centre_out, rim_out, msg_out):
     kinds, rows, width, _ = curl_ref.shape
 
     group = 3
-
-    @pl.loop(0, kinds // group)
-    def _(step):
+    spread = None
+    for base in range(0, kinds, group):
         totals = [None] * group
         for a in range(rows):
             row = bent_ref[a : a + 1, :]
             for j in range(group):
-                term = curl_ref[step * group + j, a] * row
+                term = curl_ref[base + j, a] * row
                 totals[j] = term if a == 0 else totals[j] + term
-        for j, total in enumerate(totals):
-            at = pl.multiple_of((step * group + j) * LANES, LANES)
-            back_ref[:, pl.ds(at, LANES)] = split_rows(total)
-
-    spread = add_halves(nt_dot(back_ref[...], pat_ref[...]))
+        terms = jnp.concatenate([split_rows(total) for total in totals], axis=1)
+        part = nt_dot(terms, pat_ref[:, base * LANES : (base + group) * LANES])
+        spread = part if spread is None else spread + part
+    spread = add_halves(spread)
     rim = spread[:, LANES:]
     centre = sigma_ref[...] * own + spread[:, :LANES]
     centre_out[...] = centre
@@ -274,7 +272,7 @@
 def first_kernel(count, rhs_ref, odd_ref, even_ref, sigma_ref, reluct_ref, curl_ref, pattern_ref,
                  weight_ref, block_ref, coil_hot_ref, pat_ref, coil_ref,
                  row_ref, msg_ref, centre_ref, rim_ref, halo_ref,
-                 picked_ref, face_ref, back_ref, sums_ref):
+                 picked_ref, face_ref, sums_ref):
     left, right = sides(even_ref[...], odd_ref[...])
     halo = halo_of(left, right, count)
     halo_ref[...] = halo
@@ -286,7 +284,7 @@
     own = rhs_ref[...]
     refs = (sigma_ref, reluct_ref, curl_ref, pattern_ref, weight_ref, block_ref, coil_hot_ref)
     face_side(refs, rhs_ref, halo, None, row_ref, picked_ref, face_ref, sums_ref)
-    backward(curl_ref, face_ref, back_ref, pat_ref, sigma_ref, own, centre_ref, rim_ref, msg_ref)
+    backward(curl_ref, face_ref, pat_ref, sigma_ref, own, centre_ref, rim_ref, msg_ref)
 
 
 def scalars(rows_ref, inv_ref, scal_ref):
@@ -363,13 +361,13 @@
     halo = r["halo"][...] - alpha * image_halo
     r["res_o"][...] = own
     refs = tuple(r[k] for k in ("sigma", "reluct", "curl", "pattern", "weight", "block", "coilhot"))
-    picked_ref, face_ref, back_ref, sums_ref = scratch
+    picked_ref, face_ref, sums_ref = scratch
     face_side(refs, r["res_o"], halo, r["img_o"], r["row_o"], picked_ref, face_ref, sums_ref)
     if not last:
         r["imgh_o"][...] = image_halo
         r["halo_o"][...] = halo
         r["msg_o"][:, LANES:] = jnp.zeros_like(r["msg_o"][:, LANES:])
-    backward(r["curl"], face_ref, back_ref, r["pat"], r["sigma"], own, r["centre_o"], r.get("rim_o"),
+    backward(r["curl"], face_ref, r["pat"], r["sigma"], own, r["centre_o"], r.get("rim_o"),
              r["msg_o"])
 
 
@@ -453,7 +451,6 @@
         cost=COST,
     )
     picked, faces = VMEM((kinds, width, LANES), F32), VMEM((width, LANES), F32)
-    back = VMEM((2 * width, kinds * LANES), BF16)
     sums = VMEM((conductors // LANES + 3, 8, LANES), F32)
     shared = (sigma_v, reluct_v, curl_blocks, pattern_v, weight_v, block_v, coil_hot, pat, coil_v)
     line = ((count, LANES), F32)
@@ -463,7 +460,7 @@
         (rhs, odd, even) + shared,
         [line, wide, tile, tile, tile],
         "apply0",
-        scratch=[picked, faces, back, sums],
+        scratch=[picked, faces, sums],
     )
     odd_c, even_c = odd, even = exchange(message)
     rows = gather_rows(row)
@@ -479,7 +476,7 @@
             args + (inv, blk) + shared,
             state,
             "apply%d" % turn,
-            scratch=[picked, faces, back, sums],
+            scratch=[picked, faces, sums],
         )
         if not last:
             rim, halo, image_halo = rest

time: 79.2 us -> 78.5 us (level)
  no operation moved by 1% of the time
where the time goes in v5:
time: 78.5 us; the launch traced here: 78.2 us
  blocking collectives  39.3 us (50%)
  starting transfers between devices  19.6 us (25%)
  Pallas kernels  11.6 us (15%)
  waiting for transfers between devices  6.54 us (8%)
    all_to_all x2, blocking collectives, gather_rows(): return lax.all_to_all(rows, 'dom', 0, 0, tiled=True)  39.3 us
    pallas_call x6, Pallas kernels, call(): pl.pallas_call(kernel, name=name, in_specs=[pl.BlockSpec(memory_space=plt...  11.6 us
    ppermute x4, starting transfers between devices, exchange(): return (lax.ppermute(message, 'dom', outer), near)  11.6 us
    all_to_all x1, starting transfers between devices, gather_rows(): return lax.all_to_all(rows, 'dom', 0, 0, tiled=True)  4.5 us
    ppermute x4, waiting for transfers between devices, exchange(): return (lax.ppermute(message, 'dom', outer), near)  3.63 us
    ppermute x4, starting transfers between devices, exchange(): near = lax.ppermute(message, 'dom', inner)  3.57 us
    all_to_all x1, waiting for transfers between devices, gather_rows(): return lax.all_to_all(rows, 'dom', 0, 0, tiled=True)  2.9 us
  transfers between devices with their start and end apart: 9, of which 3 were waited for; matrix products, arithmetic and copies ran while one was open for 0% of the time, Pallas kernels for 1%

profile of v5, /device:TPU:1, one launch (start us, length us, event | category | flops | bytes accessed | tf_op | source)
XLA Modules:
  0.0 78.2 jit_solution(10178413999855807404)
XLA Ops:
  0.6 0.0 slice-start
  0.6 0.0 slice-start.1
  0.7 1.4 %rhs.1 = (f32[64,128]{1,0:T(8,128)S(1)}, f32[64,512]{1,0:T(8,128)S(1)}, s32[4,128]{1,0:T(4,128)S(1)}, s32[4,128]{1,0:T(4,128)S(1)}) custom-call(f32[64,128]{1,0:T(8,128)} %side_hbm.1, f32[64,512]{1,0:T(8,128)} %weight_hbm.1, s32[4,128]{1,0:T(4,128)} %bitcast.23, s32[4,128]{1,0:T(4,128)} %bitcast.24, s32[1,84]{1,0:T(1,128)} %bitcast.25, f32[1,84]{1,0:T(1,128)} %bitcast.26, ...), custom_call_target="tpu_custom_call" | custom-call | flops 17179869184 | bytes 1048576 | tf_op jit(solution)/shard_map/rhs/pallas_call | solution.py:392
  2.1 1.5 %collective-permute-start.1 = (f32[64,128]{1,0:T(8,128)S(1)}, f32[64,128]{1,0:T(8,128)S(1)}, u32[]{:S(2)}, u32[]{:S(2)}) collective-permute-start(f32[64,128]{1,0:T(8,128)S(1)} %get-tuple-element.37.rhs_ref.refs_5_), channel_id=1, source_target_pairs={{0,1},{1,0},{2,3},{3,2},{4,5},{5,4},{6,7},{7,6},{8,9},{9,8},{10,11... | collective-permute-start | bytes 98312 | tf_op jit(solution)/shard_map/ppermute | solution.py:422
  3.6 3.4 %collective-permute-start = (f32[64,128]{1,0:T(8,128)S(1)}, f32[64,128]{1,0:T(8,128)S(1)}, u32[]{:S(2)}, u32[]{:S(2)}) collective-permute-start(f32[64,128]{1,0:T(8,128)S(1)} %get-tuple-element.37.rhs_ref.refs_5_), channel_id=1, source_target_pairs={{1,2},{3,4},{5,6},{7,8},{9,10},{11,12},{13,14},{15,16},{17,18},{19... | collective-permute-start | bytes 98312 | tf_op jit(solution)/shard_map/ppermute | solution.py:423
  7.0 0.0 slice-start.2
  7.0 1.1 %tables.1 = (bf16[256,768]{1,0:T(8,128)(2,1)S(1)}, bf16[128,512]{1,0:T(8,128)(2,1)S(1)}, bf16[128,512]{1,0:T(8,128)(2,1)S(1)}, f32[8,128]{1,0:T(8,128)S(1)}, s32...) custom-call(s32[6,128]{1,0:T(8,128)} %pattern_hbm.1, f32[1,84]{1,0:T(1,128)} %bitcast.27, ...), custom_call_target="tpu_custom_call" | custom-call | flops 17179869184 | bytes 1048576 | tf_op jit(solution)/shard_map/tables/pallas_call | solution.py:392
  8.1 0.0 collective-permute-done.1.even_ref
  8.1 0.7 collective-permute-done.odd_ref
  8.8 0.0 slice-done
  8.8 0.0 slice-done.1
  8.8 0.4 slice-done.2
  9.2 2.4 %apply0.1 = (f32[128,128]{1,0:T(8,128)S(1)}, f32[72,640]{1,0:T(8,128)S(1)}, f32[64,128]{1,0:T(8,128)S(1)}, f32[64,128]{1,0:T(8,128)S(1)}, f32[64,128]{1,0:T(8,128)S(1)}) custom-call(f32[64,128]{1,0:T(8,128)S(1)} %get-tuple-element.37.rhs_ref.refs_5_, f32[64,128]{1,0:T(8,128)S(1)} %collective-permute-done.odd_ref, ...), custom_call_target="tpu_custom_call" | custom-call | tf_op jit(solution)/shard_map/apply0/pallas_call | solution.py:392
  11.6 0.1 collective-permute-start.3
  11.7 3.5 %collective-permute-start.2 = (f32[72,640]{1,0:T(8,128)S(1)}, f32[72,640]{1,0:T(8,128)S(1)}, u32[]{:S(2)}, u32[]{:S(2)}) collective-permute-start(f32[72,640]{1,0:T(8,128)S(1)} %get-tuple-element.47), channel_id=1, source_target_pairs={{1,2},{3,4},{5,6},{7,8},{9,10},{11,12},{13,14},{15,16},{17,18},{19... | collective-permute-start | bytes 552968 | tf_op jit(solution)/shard_map/ppermute | solution.py:423
  15.2 22.9 %all_to_all.33 = f32[128,1,128]{2,1,0:T(1,128)S(1)} all-to-all(f32[128,1,128]{2,1,0:T(1,128)S(1)} %bitcast.22), channel_id=1, replica_groups=mesh['dom'=128] {'dom'}, dimensions={0} | all-to-all | bytes 131072 | tf_op jit(solution)/shard_map/all_to_all | solution.py:426
  38.1 0.0 collective-permute-done.3.refs_2_.refs_4_
  38.1 0.0 collective-permute-done.2.refs_1_.refs_3_
  38.1 2.7 %apply1.1 = (f32[128,128]{1,0:T(8,128)S(1)}, f32[64,128]{1,0:T(8,128)S(1)}, f32[64,128]{1,0:T(8,128)S(1)}, f32[64,128]{1,0:T(8,128)S(1)}, f32[64,128]{1,0:T(8,12...) custom-call(f32[128,128]{1,0:T(8,128)S(1)} %bitcast.19, ...), custom_call_target="tpu_custom_call" | custom-call | tf_op jit(solution)/shard_map/apply1/pallas_call | solution.py:392
  40.9 0.8 %collective-permute-start.5 = (f32[64,384]{1,0:T(8,128)S(1)}, f32[64,384]{1,0:T(8,128)S(1)}, u32[]{:S(2)}, u32[]{:S(2)}) collective-permute-start(f32[64,384]{1,0:T(8,128)S(1)} %get-tuple-element.54), channel_id=1, source_target_pairs={{0,1},{1,0},{2,3},{3,2},{4,5},{5,4},{6,7},{7,6},{8,9},{9,8},{10,11... | collective-permute-start | bytes 294920 | tf_op jit(solution)/shard_map/ppermute | solution.py:422
  41.7 2.1 %collective-permute-start.4 = (f32[64,384]{1,0:T(8,128)S(1)}, f32[64,384]{1,0:T(8,128)S(1)}, u32[]{:S(2)}, u32[]{:S(2)}) collective-permute-start(f32[64,384]{1,0:T(8,128)S(1)} %get-tuple-element.54), channel_id=1, source_target_pairs={{1,2},{3,4},{5,6},{7,8},{9,10},{11,12},{13,14},{15,16},{17,18},{19... | collective-permute-start | bytes 294920 | tf_op jit(solution)/shard_map/ppermute | solution.py:423
  43.8 16.4 %all_to_all.34 = f32[128,1,128]{2,1,0:T(1,128)S(1)} all-to-all(f32[128,1,128]{2,1,0:T(1,128)S(1)} %bitcast.21), channel_id=1, replica_groups=mesh['dom'=128] {'dom'}, dimensions={0} | all-to-all | bytes 131072 | tf_op jit(solution)/shard_map/all_to_all | solution.py:426
  60.2 0.0 collective-permute-done.5.refs_2_
  60.2 0.0 collective-permute-done.4.refs_1_
  60.2 3.1 %apply2.1 = (f32[128,128]{1,0:T(8,128)}, f32[64,128]{1,0:T(8,128)S(1)}, f32[64,128]{1,0:T(8,128)S(1)}, f32[64,128]{1,0:T(8,128)S(1)}, f32[64,128]{1,0:T(8,128)S(...) custom-call(f32[128,128]{1,0:T(8,128)S(1)} %bitcast.18, ...), custom_call_target="tpu_custom_call" | custom-call | tf_op jit(solution)/shard_map/apply2/pallas_call | solution.py:392
  63.3 4.5 %all-to-all-start.2 = ((f32[128,1,128]{2,1,0:T(1,128)}), f32[128,1,128]{2,1,0:T(1,128)S(1)}, u32[]{:S(2)}, u32[]{:S(2)}) async-start(f32[128,1,128]{2,1,0:T(1,128)} %bitcast.11), calls=%async_computation.2 | async-start | bytes 131072 | tf_op jit(solution)/shard_map/all_to_all | solution.py:426
  67.8 1.1 %collective-permute-start.7 = (f32[64,128]{1,0:T(8,128)S(1)}, f32[64,128]{1,0:T(8,128)S(1)}, u32[]{:S(2)}, u32[]{:S(2)}) collective-permute-start(f32[64,128]{1,0:T(8,128)S(1)} %get-tuple-element.65), channel_id=1, source_target_pairs={{0,1},{1,0},{2,3},{3,2},{4,5},{5,4},{6,7},{7,6},{8,9},{9,8},{10,11... | collective-permute-start | bytes 98312 | tf_op jit(solution)/shard_map/ppermute | solution.py:422
  68.9 2.6 %collective-permute-start.6 = (f32[64,128]{1,0:T(8,128)S(1)}, f32[64,128]{1,0:T(8,128)S(1)}, u32[]{:S(2)}, u32[]{:S(2)}) collective-permute-start(f32[64,128]{1,0:T(8,128)S(1)} %get-tuple-element.65), channel_id=1, source_target_pairs={{1,2},{3,4},{5,6},{7,8},{9,10},{11,12},{13,14},{15,16},{17,18},{19... | collective-permute-start | bytes 98312 | tf_op jit(solution)/shard_map/ppermute | solution.py:423
  71.5 0.0 collective-permute-done.7.even_ref
  71.5 2.9 %collective-permute-done.6.odd_ref = f32[64,128]{1,0:T(8,128)S(1)} collective-permute-done((f32[64,128]{1,0:T(8,128)S(1)}, f32[64,128]{1,0:T(8,128)S(1)}, u32[]{:S(2)}, u32[]{:S(2)}) %collective-permute-start.6) | collective-permute-done | bytes 32800 | tf_op jit(solution)/shard_map/ppermute | solution.py:423
  74.4 2.9 %all-to-all-done.2 = f32[128,1,128]{2,1,0:T(1,128)S(1)} async-done(((f32[128,1,128]{2,1,0:T(1,128)}), f32[128,1,128]{2,1,0:T(1,128)S(1)}, u32[]{:S(2)}, u32[]{:S(2)}) %all-to-all-start.2) | async-done | bytes 65568 | tf_op jit(solution)/shard_map/all_to_all | solution.py:426
  77.3 0.9 %finish.1 = (f32[64,128]{1,0:T(8,128)}, f32[64,128]{1,0:T(8,128)}) custom-call(f32[128,128]{1,0:T(8,128)S(1)} %bitcast.20, f32[64,128]{1,0:T(8,128)S(1)} %collective-permute-done.6.odd_ref, f32[64,128]{1,0:T(8,128)S(1)} %collective-permute-done.7.even_ref, f32[64,128]{1,0:T(8,128)S(1)} %get-tuple-element.66.centre_ref, ...), custom_call_target="tpu_custom_call" | custom-call | tf_op jit(solution)/shard_map/finish/pallas_call | solution.py:392
  (1 shorter events, 0.0 us)
Async XLA Ops:
  0.6 8.2 %slice-start = ((s8[12582912]{0:T(1024)(128)(4,1)}), s8[4194304]{0:T(1024)(128)(4,1)S(1)}, s32[]{:S(2)}) async-start(s8[12582912]{0:T(1024)(128)(4,1)} %bitcast.16), calls=%async_computation.3 | async-start | bytes 8388608
  0.6 8.2 %slice-start.1 = ((s8[12582912]{0:T(1024)(128)(4,1)}), s8[4194304]{0:T(1024)(128)(4,1)S(1)}, s32[]{:S(2)}) async-start(s8[12582912]{0:T(1024)(128)(4,1)} %bitcast.16), calls=%async_computation.4 | async-start | bytes 8388608
  2.1 6.0 %collective-permute-start.1 = (f32[64,128]{1,0:T(8,128)S(1)}, f32[64,128]{1,0:T(8,128)S(1)}, u32[]{:S(2)}, u32[]{:S(2)}) collective-permute-start(f32[64,128]{1,0:T(8,128)S(1)} %get-tuple-element.37.rhs_ref.refs_5_), channel_id=1, source_target_pairs={{0,1},{1,0},{2,3},{3,2},{4,5},{5,4},{6,7},{7,6},{8,9},{9,8},{10,11... | collective-permute-start | bytes 98312 | tf_op jit(solution)/shard_map/ppermute | solution.py:422
  3.6 5.2 %collective-permute-start = (f32[64,128]{1,0:T(8,128)S(1)}, f32[64,128]{1,0:T(8,128)S(1)}, u32[]{:S(2)}, u32[]{:S(2)}) collective-permute-start(f32[64,128]{1,0:T(8,128)S(1)} %get-tuple-element.37.rhs_ref.refs_5_), channel_id=1, source_target_pairs={{1,2},{3,4},{5,6},{7,8},{9,10},{11,12},{13,14},{15,16},{17,18},{19... | collective-permute-start | bytes 98312 | tf_op jit(solution)/shard_map/ppermute | solution.py:423
  7.0 2.3 %slice-start.2 = ((s8[12582912]{0:T(1024)(128)(4,1)}), s8[4194304]{0:T(1024)(128)(4,1)S(1)}, s32[]{:S(2)}) async-start(s8[12582912]{0:T(1024)(128)(4,1)} %bitcast.16), calls=%async_computation.5 | async-start | bytes 8388608
  11.6 26.5 %collective-permute-start.3 = (f32[72,640]{1,0:T(8,128)S(1)}, f32[72,640]{1,0:T(8,128)S(1)}, u32[]{:S(2)}, u32[]{:S(2)}) collective-permute-start(f32[72,640]{1,0:T(8,128)S(1)} %get-tuple-element.47), channel_id=1, source_target_pairs={{0,1},{1,0},{2,3},{3,2},{4,5},{5,4},{6,7},{7,6},{8,9},{9,8},{10,11... | collective-permute-start | bytes 552968 | tf_op jit(solution)/shard_map/ppermute | solution.py:422
  11.7 26.4 %collective-permute-start.2 = (f32[72,640]{1,0:T(8,128)S(1)}, f32[72,640]{1,0:T(8,128)S(1)}, u32[]{:S(2)}, u32[]{:S(2)}) collective-permute-start(f32[72,640]{1,0:T(8,128)S(1)} %get-tuple-element.47), channel_id=1, source_target_pairs={{1,2},{3,4},{5,6},{7,8},{9,10},{11,12},{13,14},{15,16},{17,18},{19... | collective-permute-start | bytes 552968 | tf_op jit(solution)/shard_map/ppermute | solution.py:423
  40.9 19.3 %collective-permute-start.5 = (f32[64,384]{1,0:T(8,128)S(1)}, f32[64,384]{1,0:T(8,128)S(1)}, u32[]{:S(2)}, u32[]{:S(2)}) collective-permute-start(f32[64,384]{1,0:T(8,128)S(1)} %get-tuple-element.54), channel_id=1, source_target_pairs={{0,1},{1,0},{2,3},{3,2},{4,5},{5,4},{6,7},{7,6},{8,9},{9,8},{10,11... | collective-permute-start | bytes 294920 | tf_op jit(solution)/shard_map/ppermute | solution.py:422
  41.7 18.5 %collective-permute-start.4 = (f32[64,384]{1,0:T(8,128)S(1)}, f32[64,384]{1,0:T(8,128)S(1)}, u32[]{:S(2)}, u32[]{:S(2)}) collective-permute-start(f32[64,384]{1,0:T(8,128)S(1)} %get-tuple-element.54), channel_id=1, source_target_pairs={{1,2},{3,4},{5,6},{7,8},{9,10},{11,12},{13,14},{15,16},{17,18},{19... | collective-permute-start | bytes 294920 | tf_op jit(solution)/shard_map/ppermute | solution.py:423
  63.3 14.1 %all-to-all-start.2 = ((f32[128,1,128]{2,1,0:T(1,128)}), f32[128,1,128]{2,1,0:T(1,128)S(1)}, u32[]{:S(2)}, u32[]{:S(2)}) async-start(f32[128,1,128]{2,1,0:T(1,128)} %bitcast.11), calls=%async_computation.2 | async-start | bytes 131072 | tf_op jit(solution)/shard_map/all_to_all | solution.py:426
  67.8 3.8 %collective-permute-start.7 = (f32[64,128]{1,0:T(8,128)S(1)}, f32[64,128]{1,0:T(8,128)S(1)}, u32[]{:S(2)}, u32[]{:S(2)}) collective-permute-start(f32[64,128]{1,0:T(8,128)S(1)} %get-tuple-element.65), channel_id=1, source_target_pairs={{0,1},{1,0},{2,3},{3,2},{4,5},{5,4},{6,7},{7,6},{8,9},{9,8},{10,11... | collective-permute-start | bytes 98312 | tf_op jit(solution)/shard_map/ppermute | solution.py:422
  68.9 5.5 %collective-permute-start.6 = (f32[64,128]{1,0:T(8,128)S(1)}, f32[64,128]{1,0:T(8,128)S(1)}, u32[]{:S(2)}, u32[]{:S(2)}) collective-permute-start(f32[64,128]{1,0:T(8,128)S(1)} %get-tuple-element.65), channel_id=1, source_target_pairs={{1,2},{3,4},{5,6},{7,8},{9,10},{11,12},{13,14},{15,16},{17,18},{19... | collective-permute-start | bytes 98312 | tf_op jit(solution)/shard_map/ppermute | solution.py:423

commit v6 on v5

--- a/solution.py
+++ b/solution.py
@@ -93,17 +93,17 @@
 ):
     copies = move(
         [
+            (weight_hbm, weight_ref),
             (coil_hbm, coil_ref),
             (phase_hbm, phase_ref),
             (ohm_hbm, ohm_ref),
             (state_hbm, state_ref),
-            (weight_hbm, weight_ref),
             (block_hbm, block_ref),
             (side_hbm, side_ref),
         ],
         sems,
     )
-    for copy in copies:
+    for copy in copies[1:6]:
         copy.wait()
     s0, s1, s2 = (state_ref[i].astype(F32) for i in range(3))
     mean = (s0 + s1 + s2) / 3.0
@@ -114,9 +114,18 @@
         jnp.where(phase == 1, s1 - mean, jnp.where(phase == 2, s2 - mean, 0.0)),
     )
     source = pad_lanes(LINK_SCALE * volts / ohm_ref[...], pad_ref)
-    coils, blocks = rows_of(coil_ref[...]), rows_of(block_ref[...])
-    spread = split_rows(weighted(weight_ref[...], source, coils))
-    rhs_ref[...] = side_ref[...] + add_halves(nt_dot(spread, onehot(blocks, LANES)))
+    wide = jnp.broadcast_to(source, (8, LANES))
+    coils = coil_ref[...]
+    rows = [
+        gather_lanes(wide, jnp.broadcast_to(coils[i : i + 1], (8, LANES)))[0:1]
+        for i in range(coils.shape[0])
+    ]
+    amount = jnp.concatenate(rows, axis=1)
+    hot = onehot(rows_of(block_ref[...]), LANES)
+    copies[0].wait()
+    copies[6].wait()
+    spread = split_rows(weight_ref[...] * amount)
+    rhs_ref[...] = side_ref[...] + add_halves(nt_dot(spread, hot))
 
 
 def table_kernel(

time: 78.5 us -> 78.4 us (level)
  no operation moved by 1% of the time
where the time goes in v6:
time: 78.4 us; the launch traced here: 78.1 us
  blocking collectives  39.3 us (50%)
  starting transfers between devices  19.6 us (25%)
  Pallas kernels  11.5 us (15%)
  waiting for transfers between devices  6.54 us (8%)
    all_to_all x2, blocking collectives, gather_rows(): return lax.all_to_all(rows, 'dom', 0, 0, tiled=True)  39.3 us
    ppermute x4, starting transfers between devices, exchange(): return (lax.ppermute(message, 'dom', outer), near)  11.6 us
    pallas_call x6, Pallas kernels, call(): pl.pallas_call(kernel, name=name, in_specs=[pl.BlockSpec(memory_space=plt...  11.5 us
    all_to_all x1, starting transfers between devices, gather_rows(): return lax.all_to_all(rows, 'dom', 0, 0, tiled=True)  4.5 us
    ppermute x4, waiting for transfers between devices, exchange(): return (lax.ppermute(message, 'dom', outer), near)  3.63 us
    ppermute x4, starting transfers between devices, exchange(): near = lax.ppermute(message, 'dom', inner)  3.57 us
    all_to_all x1, waiting for transfers between devices, gather_rows(): return lax.all_to_all(rows, 'dom', 0, 0, tiled=True)  2.9 us
  transfers between devices with their start and end apart: 9, of which 3 were waited for; matrix products, arithmetic and copies ran while one was open for 0% of the time, Pallas kernels for 1%

profile of v6, /device:TPU:1, one launch (start us, length us, event | category | flops | bytes accessed | tf_op | source)
XLA Modules:
  0.0 78.1 jit_solution(10678938112925401953)
XLA Ops:
  0.6 0.0 slice-start
  0.6 0.0 slice-start.1
  0.7 1.3 %rhs.1 = (f32[64,128]{1,0:T(8,128)S(1)}, f32[64,512]{1,0:T(8,128)S(1)}, s32[4,128]{1,0:T(4,128)S(1)}, s32[4,128]{1,0:T(4,128)S(1)}) custom-call(f32[64,128]{1,0:T(8,128)} %side_hbm.1, f32[64,512]{1,0:T(8,128)} %weight_hbm.1, s32[4,128]{1,0:T(4,128)} %bitcast.23, s32[4,128]{1,0:T(4,128)} %bitcast.24, s32[1,84]{1,0:T(1,128)} %bitcast.25, f32[1,84]{1,0:T(1,128)} %bitcast.26, ...), custom_call_target="tpu_custom_call" | custom-call | flops 17179869184 | bytes 1048576 | tf_op jit(solution)/shard_map/rhs/pallas_call | solution.py:401
  2.0 1.5 %collective-permute-start.1 = (f32[64,128]{1,0:T(8,128)S(1)}, f32[64,128]{1,0:T(8,128)S(1)}, u32[]{:S(2)}, u32[]{:S(2)}) collective-permute-start(f32[64,128]{1,0:T(8,128)S(1)} %get-tuple-element.37.rhs_ref.refs_5_), channel_id=1, source_target_pairs={{0,1},{1,0},{2,3},{3,2},{4,5},{5,4},{6,7},{7,6},{8,9},{9,8},{10,11... | collective-permute-start | bytes 98312 | tf_op jit(solution)/shard_map/ppermute | solution.py:431
  3.5 3.4 %collective-permute-start = (f32[64,128]{1,0:T(8,128)S(1)}, f32[64,128]{1,0:T(8,128)S(1)}, u32[]{:S(2)}, u32[]{:S(2)}) collective-permute-start(f32[64,128]{1,0:T(8,128)S(1)} %get-tuple-element.37.rhs_ref.refs_5_), channel_id=1, source_target_pairs={{1,2},{3,4},{5,6},{7,8},{9,10},{11,12},{13,14},{15,16},{17,18},{19... | collective-permute-start | bytes 98312 | tf_op jit(solution)/shard_map/ppermute | solution.py:432
  6.8 0.0 slice-start.2
  6.9 1.1 %tables.1 = (bf16[256,768]{1,0:T(8,128)(2,1)S(1)}, bf16[128,512]{1,0:T(8,128)(2,1)S(1)}, bf16[128,512]{1,0:T(8,128)(2,1)S(1)}, f32[8,128]{1,0:T(8,128)S(1)}, s32...) custom-call(s32[6,128]{1,0:T(8,128)} %pattern_hbm.1, f32[1,84]{1,0:T(1,128)} %bitcast.27, ...), custom_call_target="tpu_custom_call" | custom-call | flops 17179869184 | bytes 1048576 | tf_op jit(solution)/shard_map/tables/pallas_call | solution.py:401
  8.0 0.0 collective-permute-done.1.even_ref
  8.0 0.7 collective-permute-done.odd_ref
  8.7 0.0 slice-done
  8.7 0.0 slice-done.1
  8.7 0.4 slice-done.2
  9.1 2.4 %apply0.1 = (f32[128,128]{1,0:T(8,128)S(1)}, f32[72,640]{1,0:T(8,128)S(1)}, f32[64,128]{1,0:T(8,128)S(1)}, f32[64,128]{1,0:T(8,128)S(1)}, f32[64,128]{1,0:T(8,128)S(1)}) custom-call(f32[64,128]{1,0:T(8,128)S(1)} %get-tuple-element.37.rhs_ref.refs_5_, f32[64,128]{1,0:T(8,128)S(1)} %collective-permute-done.odd_ref, ...), custom_call_target="tpu_custom_call" | custom-call | tf_op jit(solution)/shard_map/apply0/pallas_call | solution.py:401
  11.5 0.1 collective-permute-start.3
  11.6 3.5 %collective-permute-start.2 = (f32[72,640]{1,0:T(8,128)S(1)}, f32[72,640]{1,0:T(8,128)S(1)}, u32[]{:S(2)}, u32[]{:S(2)}) collective-permute-start(f32[72,640]{1,0:T(8,128)S(1)} %get-tuple-element.47), channel_id=1, source_target_pairs={{1,2},{3,4},{5,6},{7,8},{9,10},{11,12},{13,14},{15,16},{17,18},{19... | collective-permute-start | bytes 552968 | tf_op jit(solution)/shard_map/ppermute | solution.py:432
  15.1 22.9 %all_to_all.33 = f32[128,1,128]{2,1,0:T(1,128)S(1)} all-to-all(f32[128,1,128]{2,1,0:T(1,128)S(1)} %bitcast.22), channel_id=1, replica_groups=mesh['dom'=128] {'dom'}, dimensions={0} | all-to-all | bytes 131072 | tf_op jit(solution)/shard_map/all_to_all | solution.py:435
  38.0 0.0 collective-permute-done.3.refs_2_.refs_4_
  38.0 0.0 collective-permute-done.2.refs_1_.refs_3_
  38.0 2.7 %apply1.1 = (f32[128,128]{1,0:T(8,128)S(1)}, f32[64,128]{1,0:T(8,128)S(1)}, f32[64,128]{1,0:T(8,128)S(1)}, f32[64,128]{1,0:T(8,128)S(1)}, f32[64,128]{1,0:T(8,12...) custom-call(f32[128,128]{1,0:T(8,128)S(1)} %bitcast.19, ...), custom_call_target="tpu_custom_call" | custom-call | tf_op jit(solution)/shard_map/apply1/pallas_call | solution.py:401
  40.7 0.8 %collective-permute-start.5 = (f32[64,384]{1,0:T(8,128)S(1)}, f32[64,384]{1,0:T(8,128)S(1)}, u32[]{:S(2)}, u32[]{:S(2)}) collective-permute-start(f32[64,384]{1,0:T(8,128)S(1)} %get-tuple-element.54), channel_id=1, source_target_pairs={{0,1},{1,0},{2,3},{3,2},{4,5},{5,4},{6,7},{7,6},{8,9},{9,8},{10,11... | collective-permute-start | bytes 294920 | tf_op jit(solution)/shard_map/ppermute | solution.py:431
  41.6 2.1 %collective-permute-start.4 = (f32[64,384]{1,0:T(8,128)S(1)}, f32[64,384]{1,0:T(8,128)S(1)}, u32[]{:S(2)}, u32[]{:S(2)}) collective-permute-start(f32[64,384]{1,0:T(8,128)S(1)} %get-tuple-element.54), channel_id=1, source_target_pairs={{1,2},{3,4},{5,6},{7,8},{9,10},{11,12},{13,14},{15,16},{17,18},{19... | collective-permute-start | bytes 294920 | tf_op jit(solution)/shard_map/ppermute | solution.py:432
  43.7 16.4 %all_to_all.34 = f32[128,1,128]{2,1,0:T(1,128)S(1)} all-to-all(f32[128,1,128]{2,1,0:T(1,128)S(1)} %bitcast.21), channel_id=1, replica_groups=mesh['dom'=128] {'dom'}, dimensions={0} | all-to-all | bytes 131072 | tf_op jit(solution)/shard_map/all_to_all | solution.py:435
  60.1 0.0 collective-permute-done.5.refs_2_
  60.1 0.0 collective-permute-done.4.refs_1_
  60.1 3.1 %apply2.1 = (f32[128,128]{1,0:T(8,128)}, f32[64,128]{1,0:T(8,128)S(1)}, f32[64,128]{1,0:T(8,128)S(1)}, f32[64,128]{1,0:T(8,128)S(1)}, f32[64,128]{1,0:T(8,128)S(...) custom-call(f32[128,128]{1,0:T(8,128)S(1)} %bitcast.18, ...), custom_call_target="tpu_custom_call" | custom-call | tf_op jit(solution)/shard_map/apply2/pallas_call | solution.py:401
  63.2 4.5 %all-to-all-start.2 = ((f32[128,1,128]{2,1,0:T(1,128)}), f32[128,1,128]{2,1,0:T(1,128)S(1)}, u32[]{:S(2)}, u32[]{:S(2)}) async-start(f32[128,1,128]{2,1,0:T(1,128)} %bitcast.11), calls=%async_computation.2 | async-start | bytes 131072 | tf_op jit(solution)/shard_map/all_to_all | solution.py:435
  67.7 1.1 %collective-permute-start.7 = (f32[64,128]{1,0:T(8,128)S(1)}, f32[64,128]{1,0:T(8,128)S(1)}, u32[]{:S(2)}, u32[]{:S(2)}) collective-permute-start(f32[64,128]{1,0:T(8,128)S(1)} %get-tuple-element.65), channel_id=1, source_target_pairs={{0,1},{1,0},{2,3},{3,2},{4,5},{5,4},{6,7},{7,6},{8,9},{9,8},{10,11... | collective-permute-start | bytes 98312 | tf_op jit(solution)/shard_map/ppermute | solution.py:431
  68.8 2.6 %collective-permute-start.6 = (f32[64,128]{1,0:T(8,128)S(1)}, f32[64,128]{1,0:T(8,128)S(1)}, u32[]{:S(2)}, u32[]{:S(2)}) collective-permute-start(f32[64,128]{1,0:T(8,128)S(1)} %get-tuple-element.65), channel_id=1, source_target_pairs={{1,2},{3,4},{5,6},{7,8},{9,10},{11,12},{13,14},{15,16},{17,18},{19... | collective-permute-start | bytes 98312 | tf_op jit(solution)/shard_map/ppermute | solution.py:432
  71.4 0.0 collective-permute-done.7.even_ref
  71.4 2.9 %collective-permute-done.6.odd_ref = f32[64,128]{1,0:T(8,128)S(1)} collective-permute-done((f32[64,128]{1,0:T(8,128)S(1)}, f32[64,128]{1,0:T(8,128)S(1)}, u32[]{:S(2)}, u32[]{:S(2)}) %collective-permute-start.6) | collective-permute-done | bytes 32800 | tf_op jit(solution)/shard_map/ppermute | solution.py:432
  74.3 2.9 %all-to-all-done.2 = f32[128,1,128]{2,1,0:T(1,128)S(1)} async-done(((f32[128,1,128]{2,1,0:T(1,128)}), f32[128,1,128]{2,1,0:T(1,128)S(1)}, u32[]{:S(2)}, u32[]{:S(2)}) %all-to-all-start.2) | async-done | bytes 65568 | tf_op jit(solution)/shard_map/all_to_all | solution.py:435
  77.2 0.9 %finish.1 = (f32[64,128]{1,0:T(8,128)}, f32[64,128]{1,0:T(8,128)}) custom-call(f32[128,128]{1,0:T(8,128)S(1)} %bitcast.20, f32[64,128]{1,0:T(8,128)S(1)} %collective-permute-done.6.odd_ref, f32[64,128]{1,0:T(8,128)S(1)} %collective-permute-done.7.even_ref, f32[64,128]{1,0:T(8,128)S(1)} %get-tuple-element.66.centre_ref, ...), custom_call_target="tpu_custom_call" | custom-call | tf_op jit(solution)/shard_map/finish/pallas_call | solution.py:401
  (1 shorter events, 0.0 us)
Async XLA Ops:
  0.6 8.1 %slice-start = ((s8[12582912]{0:T(1024)(128)(4,1)}), s8[4194304]{0:T(1024)(128)(4,1)S(1)}, s32[]{:S(2)}) async-start(s8[12582912]{0:T(1024)(128)(4,1)} %bitcast.16), calls=%async_computation.3 | async-start | bytes 8388608
  0.6 8.1 %slice-start.1 = ((s8[12582912]{0:T(1024)(128)(4,1)}), s8[4194304]{0:T(1024)(128)(4,1)S(1)}, s32[]{:S(2)}) async-start(s8[12582912]{0:T(1024)(128)(4,1)} %bitcast.16), calls=%async_computation.4 | async-start | bytes 8388608
  2.0 6.0 %collective-permute-start.1 = (f32[64,128]{1,0:T(8,128)S(1)}, f32[64,128]{1,0:T(8,128)S(1)}, u32[]{:S(2)}, u32[]{:S(2)}) collective-permute-start(f32[64,128]{1,0:T(8,128)S(1)} %get-tuple-element.37.rhs_ref.refs_5_), channel_id=1, source_target_pairs={{0,1},{1,0},{2,3},{3,2},{4,5},{5,4},{6,7},{7,6},{8,9},{9,8},{10,11... | collective-permute-start | bytes 98312 | tf_op jit(solution)/shard_map/ppermute | solution.py:431
  3.5 5.2 %collective-permute-start = (f32[64,128]{1,0:T(8,128)S(1)}, f32[64,128]{1,0:T(8,128)S(1)}, u32[]{:S(2)}, u32[]{:S(2)}) collective-permute-start(f32[64,128]{1,0:T(8,128)S(1)} %get-tuple-element.37.rhs_ref.refs_5_), channel_id=1, source_target_pairs={{1,2},{3,4},{5,6},{7,8},{9,10},{11,12},{13,14},{15,16},{17,18},{19... | collective-permute-start | bytes 98312 | tf_op jit(solution)/shard_map/ppermute | solution.py:432
  6.8 2.3 %slice-start.2 = ((s8[12582912]{0:T(1024)(128)(4,1)}), s8[4194304]{0:T(1024)(128)(4,1)S(1)}, s32[]{:S(2)}) async-start(s8[12582912]{0:T(1024)(128)(4,1)} %bitcast.16), calls=%async_computation.5 | async-start | bytes 8388608
  11.5 26.5 %collective-permute-start.3 = (f32[72,640]{1,0:T(8,128)S(1)}, f32[72,640]{1,0:T(8,128)S(1)}, u32[]{:S(2)}, u32[]{:S(2)}) collective-permute-start(f32[72,640]{1,0:T(8,128)S(1)} %get-tuple-element.47), channel_id=1, source_target_pairs={{0,1},{1,0},{2,3},{3,2},{4,5},{5,4},{6,7},{7,6},{8,9},{9,8},{10,11... | collective-permute-start | bytes 552968 | tf_op jit(solution)/shard_map/ppermute | solution.py:431
  11.6 26.4 %collective-permute-start.2 = (f32[72,640]{1,0:T(8,128)S(1)}, f32[72,640]{1,0:T(8,128)S(1)}, u32[]{:S(2)}, u32[]{:S(2)}) collective-permute-start(f32[72,640]{1,0:T(8,128)S(1)} %get-tuple-element.47), channel_id=1, source_target_pairs={{1,2},{3,4},{5,6},{7,8},{9,10},{11,12},{13,14},{15,16},{17,18},{19... | collective-permute-start | bytes 552968 | tf_op jit(solution)/shard_map/ppermute | solution.py:432
  40.7 19.3 %collective-permute-start.5 = (f32[64,384]{1,0:T(8,128)S(1)}, f32[64,384]{1,0:T(8,128)S(1)}, u32[]{:S(2)}, u32[]{:S(2)}) collective-permute-start(f32[64,384]{1,0:T(8,128)S(1)} %get-tuple-element.54), channel_id=1, source_target_pairs={{0,1},{1,0},{2,3},{3,2},{4,5},{5,4},{6,7},{7,6},{8,9},{9,8},{10,11... | collective-permute-start | bytes 294920 | tf_op jit(solution)/shard_map/ppermute | solution.py:431
  41.6 18.5 %collective-permute-start.4 = (f32[64,384]{1,0:T(8,128)S(1)}, f32[64,384]{1,0:T(8,128)S(1)}, u32[]{:S(2)}, u32[]{:S(2)}) collective-permute-start(f32[64,384]{1,0:T(8,128)S(1)} %get-tuple-element.54), channel_id=1, source_target_pairs={{1,2},{3,4},{5,6},{7,8},{9,10},{11,12},{13,14},{15,16},{17,18},{19... | collective-permute-start | bytes 294920 | tf_op jit(solution)/shard_map/ppermute | solution.py:432
  63.2 14.1 %all-to-all-start.2 = ((f32[128,1,128]{2,1,0:T(1,128)}), f32[128,1,128]{2,1,0:T(1,128)S(1)}, u32[]{:S(2)}, u32[]{:S(2)}) async-start(f32[128,1,128]{2,1,0:T(1,128)} %bitcast.11), calls=%async_computation.2 | async-start | bytes 131072 | tf_op jit(solution)/shard_map/all_to_all | solution.py:435
  67.7 3.8 %collective-permute-start.7 = (f32[64,128]{1,0:T(8,128)S(1)}, f32[64,128]{1,0:T(8,128)S(1)}, u32[]{:S(2)}, u32[]{:S(2)}) collective-permute-start(f32[64,128]{1,0:T(8,128)S(1)} %get-tuple-element.65), channel_id=1, source_target_pairs={{0,1},{1,0},{2,3},{3,2},{4,5},{5,4},{6,7},{7,6},{8,9},{9,8},{10,11... | collective-permute-start | bytes 98312 | tf_op jit(solution)/shard_map/ppermute | solution.py:431
  68.8 5.5 %collective-permute-start.6 = (f32[64,128]{1,0:T(8,128)S(1)}, f32[64,128]{1,0:T(8,128)S(1)}, u32[]{:S(2)}, u32[]{:S(2)}) collective-permute-start(f32[64,128]{1,0:T(8,128)S(1)} %get-tuple-element.65), channel_id=1, source_target_pairs={{1,2},{3,4},{5,6},{7,8},{9,10},{11,12},{13,14},{15,16},{17,18},{19... | collective-permute-start | bytes 98312 | tf_op jit(solution)/shard_map/ppermute | solution.py:432
